TPU v7x, 32 devices: a whole 2x2x4 slice. The times are simulated.
32 devices in a mesh: row: 8 (over y, x, core), col: 4 (over z).
Axes of the slice: x: 2, y: 2, z: 4, core: 2. Of those that a mesh axis runs over, the one named last changes fastest.
Arguments:
- tiles: bfloat16 [8, 64, 128, 128], P('row', 'col'), may hold values from -2 to 2
- tile_index: int32 [8, 64], P('row', 'col'), may hold values from 0 to 16384, as said below
- u_basis: float32 [64, 131072], P(None, ('row', 'col')), may hold values from -10 to 10
- v_basis: float32 [64, 4, 16384], P(None, 'col', 'row'), may hold values from -10 to 10
- v_start: float32 [65536], P('col'), may hold values from -0.5 to 1.5
Outputs:
- left_vectors: float32 [2, 131072], P(None, ('row', 'col'))
- right_vectors: float32 [2, 4, 16384], P(None, 'col', 'row')
- bidiagonal: float32 [2, 2], replicated
Inputs may be any that keep to these rules, and one draw needn't show every extreme that they name: `tile_index`: each block's 16 slots name distinct tiles of its 128 x 128 block as r * 128 + c; the value 128 * 128 marks an empty slot, and empty slots come after all live ones. Blocks have different numbers of live slots, at least 4; some block has all 16 slots live.
All inputs are finite; a program needn't handle non-finite values.
Results may differ from a plain program's by a relative error of at most 0.0003.
Values sent between devices are 32-bit elements; how exact they have to be, the bound alone decides.
No kernel may reach another device: no remote copies, remote signals or barrier semaphores. Data moves between devices by JAX's collectives and lax.ppermute only.
A program may use at most 64 MiB of HBM per device.

v0:
```python
import jax
import jax.numpy as jnp
from jax import lax
from jax.sharding import PartitionSpec as P

ITERS = 2


HIGHEST = lax.Precision.HIGHEST
EPSILON = 1e-06


def project_gram(share, basis, gram, total):
    coeffs, squares = lax.psum(
        (jnp.dot(basis, share, precision=HIGHEST), jnp.sum(share * share)), ("row", "col")
    )
    coeffs = coeffs / total
    squares = squares / total
    second = coeffs - jnp.dot(gram, coeffs, precision=HIGHEST)
    combined = coeffs + second
    gram_comb = jnp.dot(gram, combined, precision=HIGHEST)
    remaining = coeffs - gram_comb
    squared = (
        squares
        - 2.0 * jnp.dot(combined, coeffs, precision=HIGHEST)
        + jnp.dot(combined, gram_comb, precision=HIGHEST)
    )
    scale = jnp.sqrt(squared + EPSILON)
    unit = (share - jnp.dot(combined, basis, precision=HIGHEST)) / scale
    column = remaining / scale
    corner = squared / (scale * scale)
    upper = jnp.concatenate([gram, column[:, None]], 1)
    lower = jnp.concatenate([column, corner[None]])[None, :]
    return (unit, scale, jnp.concatenate([upper, lower], 0), combined)


def shards(tiles, tile_index, u_basis, v_basis, v_start):
    blocks = tiles[0].astype(jnp.float32)
    slots = tile_index[0]
    width = blocks.shape[1]
    cols_len = v_start.shape[0]
    col_blocks = cols_len // width
    row_count = lax.axis_size("row")
    col_count = lax.axis_size("col")
    left_piece = u_basis.shape[1]
    right_piece = v_basis.shape[2]
    rows_len = left_piece * col_count
    row_blocks = rows_len // width
    total_left = rows_len * row_count
    total_right = cols_len * col_count
    rows_hot = (slots[:, None] // col_blocks == jnp.arange(row_blocks)[None, :]).astype(jnp.float32)
    cols_hot = (slots[:, None] % col_blocks == jnp.arange(col_blocks)[None, :]).astype(jnp.float32)
    left_start = lax.axis_index("col") * left_piece
    right_start = lax.axis_index("row") * right_piece

    def forward_many(vectors):
        count = vectors.shape[0]
        picked = jnp.einsum(
            "tc,mck->mtk", cols_hot, vectors.reshape(count, col_blocks, width), precision=HIGHEST
        )
        product = jnp.einsum("tab,mtb->mta", blocks, picked, precision=HIGHEST)
        return jnp.einsum("tr,mta->mra", rows_hot, product, precision=HIGHEST).reshape(
            count, rows_len
        )

    def forward(vector):
        return forward_many(vector[None, :])[0]

    left_basis = u_basis
    start_share = lax.dynamic_slice_in_dim(v_start, right_start, right_piece)
    right_basis = jnp.concatenate([v_basis[:, 0, :], start_share[None, :]], 0)
    left_gram, right_gram = lax.psum(
        (
            jnp.dot(left_basis, left_basis.T, precision=HIGHEST),
            jnp.dot(right_basis, right_basis.T, precision=HIGHEST),
        ),
        ("row", "col"),
    )
    left_gram = left_gram / total_left
    right_gram = right_gram / total_right
    forward_now = forward(v_start)
    lefts, rights, alphas, betas = ([], [], [], [])
    for iteration in range(ITERS):
        left_whole = lax.psum(forward_now, "col")
        left_result = lax.dynamic_slice_in_dim(left_whole, left_start, left_piece)
        share = left_result
        left_unit, alpha, left_gram, combined = project_gram(
            share, left_basis, left_gram, total_left
        )
        left_basis = jnp.concatenate([left_basis, left_unit[None, :]], 0)
        join_joined = lax.all_gather(left_unit, "col", axis=0, tiled=True)
        backward_vectors = join_joined[None, :]
        backward_count = backward_vectors.shape[0]
        backward_picked = jnp.einsum(
            "tr,mrk->mtk",
            rows_hot,
            backward_vectors.reshape(backward_count, row_blocks, width),
            precision=HIGHEST,
        )
        backward_product = jnp.einsum("tab,mta->mtb", blocks, backward_picked, precision=HIGHEST)
        backward_now = jnp.einsum(
            "tc,mtb->mcb", cols_hot, backward_product, precision=HIGHEST
        ).reshape(backward_count, cols_len)[0]
        whole = lax.psum(backward_now, "row")
        result = lax.dynamic_slice_in_dim(whole, right_start, right_piece)
        share = result
        right_unit, beta, right_gram, combined = project_gram(
            share, right_basis, right_gram, total_right
        )
        right_basis = jnp.concatenate([right_basis, right_unit[None, :]], 0)
        if iteration + 1 < ITERS:
            joined = lax.all_gather(right_unit, "row", axis=0, tiled=True)
            forward_now = forward(joined)
        lefts.append(left_unit)
        rights.append(right_unit)
        alphas.append(alpha)
        betas.append(beta)
    left_vectors = jnp.stack(lefts)
    right_vectors = jnp.stack(rights)[:, None, :]
    bidiagonal = jnp.stack([jnp.stack(alphas), jnp.stack(betas)])
    return (left_vectors, right_vectors, bidiagonal)


def solution(mesh):
    placed = (
        P("row", "col", None, None),
        P("row", "col"),
        P(None, ("row", "col")),
        P(None, "col", "row"),
        P("col"),
    )
    return jax.shard_map(
        shards,
        mesh=mesh,
        in_specs=placed,
        out_specs=(P(None, ("row", "col")), P(None, "col", "row"), P()),
        check_vma=False,
    )
```

profile of v0, /device:TPU:0, one launch (start us, length us, event | category | flops | bytes accessed | tf_op | source)
XLA Modules:
  0.0 422.3 jit_solution(5851223043497568862)
XLA Ops:
  7.9 1.0 fusion.30
  9.0 0.9 fusion.19
  10.2 0.7 copy.16
  11.0 2.8 fusion.72
  13.8 0.8 dynamic_slice.17
  15.4 32.7 %all-reduce.9.cloned.1.call-done = f32[16384]{0:T(1024)} async-done(((f32[16384]{0:T(1024)}), f32[16384]{0:T(1024)}) %all-reduce.9.cloned.1.call-update) | async-done | bytes 65552 | tf_op jit(solution)/shard_map/psum | solution.py:84
  48.1 1.3 multiply_reduce_fusion.1
  49.4 0.9 convolution_bitcast_fusion.5
  50.3 40.5 %all-reduce.3 = (f32[64]{0:T(128)S(1)}, f32[64,64]{1,0:T(8,128)S(1)}, f32[]{:T(128)}) all-reduce(f32[64]{0:T(128)S(1)} %convolution_bitcast_fusion.5, f32[64,64]{1,0:T(8,128)S(1)} %fusion.72, f32[]{:T(128)} %get-tuple-element.23), channel_id=1, replica_groups=mesh['row'=8,'col'=4] {'row','col'}, use_global_device_ids=true, to_apply=%region_1.2 | all-reduce | flops 4161 | bytes 33288 | tf_op jit(solution)/shard_map/psum | solution.py:14
  91.6 0.8 multiply_reduce_fusion.8
  94.4 13.3 %all_gather.9 = f32[16384]{0:T(1024)S(1)} all-gather(f32[4096]{0:T(1024)S(1)} %subtract_divide_fusion.1), channel_id=1, replica_groups=mesh['row'=8,'col'=4] {'col'}, dimensions={0}, use_global_device_ids=true | all-gather | bytes 81920 | tf_op jit(solution)/shard_map/all_gather | solution.py:91
  108.7 0.7 copy.17
  109.7 52.5 %all-reduce.11.cloned.1.call-done = f32[16384]{0:T(1024)} async-done(((f32[16384]{0:T(1024)}), f32[16384]{0:T(1024)}) %all-reduce.11.cloned.1.call-update) | async-done | bytes 65552 | tf_op jit(solution)/shard_map/psum | solution.py:104
  162.2 1.3 multiply_reduce_fusion.3
  164.1 39.8 %all-reduce.2 = (f32[65]{0:T(128)S(1)}, f32[65,65]{1,0:T(8,128)S(1)}, f32[]{:T(128)}) all-reduce(f32[65]{0:T(128)S(1)} %convolution_bitcast_fusion.15, f32[65,65]{1,0:T(8,128)S(1)} %fusion.23, f32[]{:T(128)} %get-tuple-element.21), channel_id=1, replica_groups=mesh['row'=8,'col'=4] {'row','col'}, use_global_device_ids=true, to_apply=%region_6.7 | all-reduce | flops 4291 | bytes 34328 | tf_op jit(solution)/shard_map/psum | solution.py:14
  204.5 0.9 multiply_reduce_fusion.6
  207.4 10.0 %all_gather.10 = f32[16384]{0:T(1024)S(1)} all-gather(f32[2048]{0:T(1024)S(1)} %subtract_divide_fusion.3), channel_id=1, replica_groups=mesh['row'=8,'col'=4] {'row'}, dimensions={0}, use_global_device_ids=true | all-gather | bytes 73728 | tf_op jit(solution)/shard_map/all_gather | solution.py:112
  217.6 0.9 fusion.15
  218.8 0.7 copy.18
  219.8 33.1 %all-reduce.13.cloned.1.call-done = f32[16384]{0:T(1024)} async-done(((f32[16384]{0:T(1024)}), f32[16384]{0:T(1024)}) %all-reduce.13.cloned.1.call-update) | async-done | bytes 65552 | tf_op jit(solution)/shard_map/psum | solution.py:84
  252.9 1.3 multiply_reduce_fusion
  254.3 1.0 convolution_bitcast_fusion.4
  255.3 40.3 %all-reduce.1 = (f32[65]{0:T(128)S(1)}, f32[]{:T(128)}) all-reduce(f32[65]{0:T(128)S(1)} %convolution_bitcast_fusion.4, f32[]{:T(128)} %get-tuple-element.19), channel_id=1, replica_groups=mesh['row'=8,'col'=4] {'row','col'}, use_global_device_ids=true, to_apply=%region_11.12 | all-reduce | flops 66 | bytes 528 | tf_op jit(solution)/shard_map/psum | solution.py:14
  295.5 0.9 multiply_reduce_fusion.5
  297.1 0.9 fusion.11
  300.1 13.3 %all_gather.11 = f32[16384]{0:T(1024)S(1)} all-gather(f32[4096]{0:T(1024)S(1)} %subtract_divide_fusion), channel_id=1, replica_groups=mesh['row'=8,'col'=4] {'col'}, dimensions={0}, use_global_device_ids=true | all-gather | bytes 81920 | tf_op jit(solution)/shard_map/all_gather | solution.py:91
  315.0 0.7 copy.20
  315.8 53.1 %all-reduce.15.cloned.1.call-done = f32[16384]{0:T(1024)} async-done(((f32[16384]{0:T(1024)}), f32[16384]{0:T(1024)}) %all-reduce.15.cloned.1.call-update) | async-done | bytes 65552 | tf_op jit(solution)/shard_map/psum | solution.py:104
  368.9 1.3 multiply_reduce_fusion.2
  370.8 39.5 %all-reduce = (f32[66]{0:T(128)S(1)}, f32[]{:T(128)}) all-reduce(f32[66]{0:T(128)S(1)} %convolution_bitcast_fusion.14, f32[]{:T(128)} %get-tuple-element.17), channel_id=1, replica_groups=mesh['row'=8,'col'=4] {'row','col'}, use_global_device_ids=true, to_apply=%region_15.16 | all-reduce | flops 67 | bytes 536 | tf_op jit(solution)/shard_map/psum | solution.py:14
  410.3 0.9 multiply_reduce_fusion.4
  411.5 0.9 fusion.12
  (52 shorter events, 10.4 us)
Async XLA Ops:
  7.2 1.8 copy-start
  7.2 40.9 %all-reduce.9.cloned.1.call-start = ((), (), s32[]{:S(2)}) async-start(), calls=%async_computation | async-start | bytes 131072 | tf_op jit(solution)/shard_map/psum | solution.py:84
  10.9 151.3 %all-reduce.11.cloned.1.call-start = ((), (), s32[]{:S(2)}) async-start(), calls=%async_computation.1 | async-start | bytes 131072 | tf_op jit(solution)/shard_map/psum | solution.py:104
  11.0 3.6 copy-start.2
  13.8 35.6 %copy-start.1 = (f32[64,4096]{1,0:T(8,128)S(1)}, f32[64,4096]{1,0:T(8,128)}, u32[]{:S(2)}) copy-start(f32[64,4096]{1,0:T(8,128)} %param.7) | copy-start | bytes 3145732
  109.4 143.5 %all-reduce.13.cloned.1.call-start = ((), (), s32[]{:S(2)}) async-start(), calls=%async_computation.2 | async-start | bytes 131072 | tf_op jit(solution)/shard_map/psum | solution.py:84
  219.5 149.4 %all-reduce.15.cloned.1.call-start = ((), (), s32[]{:S(2)}) async-start(), calls=%async_computation.3 | async-start | bytes 131072 | tf_op jit(solution)/shard_map/psum | solution.py:104
Sparse Core Ops, SparseCore 0:
  11.0 37.0 all-reduce.8
  109.5 52.6 all-reduce.10
  219.6 33.2 all-reduce.12
  315.9 52.9 all-reduce.14
where the time goes:
time: 424 us; the launch traced here: 422 us
  blocking collectives  197 us (46%)
  waiting for transfers between devices  171 us (40%)
  between operations  22.1 us (5%)
  matrix products  19.7 us (5%)
  other arithmetic  7.56 us (2%)
  local copies, waits for them, and re-layouts  4.67 us (1%)
    psum x4, blocking collectives, project_gram(): lax.psum((jnp.dot(basis, share, precision=HIGHEST), jnp.sum(share * share...  160 us
    psum x2, waiting for transfers between devices, shards(): whole = lax.psum(backward_now, 'row')  106 us
    psum x2, waiting for transfers between devices, shards(): left_whole = lax.psum(forward_now, 'col')  65.8 us
    all_gather x2, blocking collectives, shards(): join_joined = lax.all_gather(left_unit, 'col', axis=0, tiled=True)  26.6 us
    all_gather x1, blocking collectives, shards(): joined = lax.all_gather(right_unit, 'row', axis=0, tiled=True)  9.99 us
  transfers between devices with their start and end apart: 4, of which 4 were waited for; matrix products, arithmetic and copies ran while one was open for 1% of the time, Pallas kernels for 0%

commit v1 on v0

v1 whole, which is shorter than its diff:
```python
import jax
import jax.numpy as jnp
from jax import lax
from jax.sharding import PartitionSpec as P

ITERS = 2


HIGHEST = lax.Precision.HIGHEST
EPSILON = 1e-06
BOTH = ("row", "col")


def swap(chunks, axis):
    return lax.all_to_all(chunks, axis, 0, 0, tiled=True)


def reduce_scatter(chunks, axis):
    return jnp.sum(swap(chunks, axis), 0)


def gather(piece, axis):
    count = lax.axis_size(axis)
    return swap(jnp.broadcast_to(piece[None], (count,) + piece.shape), axis)


def project_gram(share, basis, gram, coeffs, squares, total):
    coeffs = coeffs / total
    squares = squares / total
    second = coeffs - jnp.dot(gram, coeffs, precision=HIGHEST)
    combined = coeffs + second
    gram_comb = jnp.dot(gram, combined, precision=HIGHEST)
    remaining = coeffs - gram_comb
    squared = (
        squares
        - 2.0 * jnp.dot(combined, coeffs, precision=HIGHEST)
        + jnp.dot(combined, gram_comb, precision=HIGHEST)
    )
    scale = jnp.sqrt(squared + EPSILON)
    unit = (share - jnp.dot(combined, basis, precision=HIGHEST)) / scale
    column = remaining / scale
    corner = squared / (scale * scale)
    upper = jnp.concatenate([gram, column[:, None]], 1)
    lower = jnp.concatenate([column, corner[None]])[None, :]
    return (unit, scale, jnp.concatenate([upper, lower], 0))


def shards(tiles, tile_index, u_basis, v_basis, v_start):
    blocks = tiles[0].astype(jnp.float32)
    slots = tile_index[0]
    width = blocks.shape[1]
    cols_len = v_start.shape[0]
    col_blocks = cols_len // width
    row_count = lax.axis_size("row")
    col_count = lax.axis_size("col")
    devices = row_count * col_count
    left_piece = u_basis.shape[1]
    right_piece = v_basis.shape[2]
    rows_len = left_piece * col_count
    row_blocks = rows_len // width
    total_left = rows_len * row_count
    total_right = cols_len * col_count
    rows_hot = (slots[:, None] // col_blocks == jnp.arange(row_blocks)[None, :]).astype(jnp.float32)
    cols_hot = (slots[:, None] % col_blocks == jnp.arange(col_blocks)[None, :]).astype(jnp.float32)
    right_start = lax.axis_index("row") * right_piece

    def forward(vector):
        picked = jnp.dot(cols_hot, vector.reshape(col_blocks, width), precision=HIGHEST)
        product = jnp.einsum("tab,tb->ta", blocks, picked, precision=HIGHEST)
        dense = jnp.einsum("tr,ta->ra", rows_hot, product, precision=HIGHEST)
        return reduce_scatter(dense.reshape(col_count, left_piece), "col")

    def backward(vector):
        picked = jnp.dot(rows_hot, vector.reshape(row_blocks, width), precision=HIGHEST)
        product = jnp.einsum("tab,ta->tb", blocks, picked, precision=HIGHEST)
        dense = jnp.einsum("tc,tb->cb", cols_hot, product, precision=HIGHEST)
        return reduce_scatter(dense.reshape(row_count, right_piece), "row")

    left_basis = u_basis
    start_share = lax.dynamic_slice_in_dim(v_start, right_start, right_piece)
    right_basis = jnp.concatenate([v_basis[:, 0, :], start_share[None, :]], 0)
    kept = left_basis.shape[0]
    kept_right = right_basis.shape[0]
    grams = jnp.concatenate(
        [
            jnp.dot(left_basis, left_basis.T, precision=HIGHEST).reshape(-1),
            jnp.dot(right_basis, right_basis.T, precision=HIGHEST).reshape(-1),
        ]
    )
    gram_len = grams.shape[0]
    chunk = -(-gram_len // devices)
    grams = jnp.pad(grams, (0, chunk * devices - gram_len)).reshape(devices, chunk)
    gram_chunk = reduce_scatter(grams, BOTH)
    vector = v_start
    lefts, rights, alphas, betas = ([], [], [], [])
    for iteration in range(ITERS):
        share = forward(vector)
        sent = [jnp.dot(left_basis, share, precision=HIGHEST), jnp.sum(share * share)[None]]
        size = left_basis.shape[0]
        if iteration == 0:
            sent.append(gram_chunk)
        received = gather(jnp.concatenate(sent), BOTH)
        summed = jnp.sum(received[:, : size + 1], 0)
        if iteration == 0:
            whole = received[:, size + 1 :].reshape(-1)
            left_gram = whole[: kept * kept].reshape(kept, kept) / total_left
            right_gram = whole[kept * kept : gram_len].reshape(kept_right, kept_right) / total_right
        left_unit, alpha, left_gram = project_gram(
            share, left_basis, left_gram, summed[:size], summed[size], total_left
        )
        left_basis = jnp.concatenate([left_basis, left_unit[None, :]], 0)
        share = backward(gather(left_unit, "col").reshape(-1))
        size = right_basis.shape[0]
        sent = [jnp.dot(right_basis, share, precision=HIGHEST), jnp.sum(share * share)[None]]
        summed = jnp.sum(gather(jnp.concatenate(sent), BOTH), 0)
        right_unit, beta, right_gram = project_gram(
            share, right_basis, right_gram, summed[:size], summed[size], total_right
        )
        right_basis = jnp.concatenate([right_basis, right_unit[None, :]], 0)
        if iteration + 1 < ITERS:
            vector = gather(right_unit, "row").reshape(-1)
        lefts.append(left_unit)
        rights.append(right_unit)
        alphas.append(alpha)
        betas.append(beta)
    left_vectors = jnp.stack(lefts)
    right_vectors = jnp.stack(rights)[:, None, :]
    bidiagonal = jnp.stack([jnp.stack(alphas), jnp.stack(betas)])
    return (left_vectors, right_vectors, bidiagonal)


def solution(mesh):
    placed = (
        P("row", "col", None, None),
        P("row", "col"),
        P(None, ("row", "col")),
        P(None, "col", "row"),
        P("col"),
    )
    return jax.shard_map(
        shards,
        mesh=mesh,
        in_specs=placed,
        out_specs=(P(None, ("row", "col")), P(None, "col", "row"), P()),
        check_vma=False,
    )
```

time: 424 us -> 154 us (0.36)
  blocking collectives: 197 us -> 24.6 us
  waiting for transfers between devices: 171 us -> 52.3 us
  starting transfers between devices: 0.16 us -> 31.5 us
  between operations: 22.1 us -> 9.05 us
  local copies, waits for them, and re-layouts: 4.67 us -> 9.14 us
    psum x4 -> x0, waiting for transfers between devices: 171 us -> none  [the longest x2 106 us: shards(): whole = lax.psum(backward_now, 'row')]
    psum x4 -> x0, blocking collectives: 160 us -> none  [project_gram(): lax.psum((jnp.dot(basis, share, precision=HIGHEST), jnp.sum(share * share...]
    all_to_all x0 -> x9, waiting for transfers between devices: none -> 52.3 us  [swap(): return lax.all_to_all(chunks, axis, 0, 0, tiled=True)]
    all_gather x3 -> x0, blocking collectives: 36.6 us -> none  [the longest x2 26.6 us: shards(): join_joined = lax.all_gather(left_unit, 'col', axis=0, tiled=True)]
    all_to_all x0 -> x9, starting transfers between devices: none -> 31.5 us  [swap(): return lax.all_to_all(chunks, axis, 0, 0, tiled=True)]
    all_to_all x0 -> x3, blocking collectives: none -> 24.6 us  [swap(): return lax.all_to_all(chunks, axis, 0, 0, tiled=True)]
  transfers between devices with their start and end apart: 4 -> 9, of which waited for: 4 -> 9; matrix products, arithmetic and copies ran while one was open for 1% -> 2% of each run, Pallas kernels for 0% -> 0%
where the time goes in v1:
time: 154 us; the launch traced here: 153 us
  waiting for transfers between devices  52.3 us (34%)
  starting transfers between devices  31.5 us (20%)
  blocking collectives  24.6 us (16%)
  matrix products  19.1 us (12%)
  local copies, waits for them, and re-layouts  9.14 us (6%)
  between operations  9.05 us (6%)
  other arithmetic  7.35 us (5%)
    all_to_all x9, waiting for transfers between devices, swap(): return lax.all_to_all(chunks, axis, 0, 0, tiled=True)  52.3 us
    all_to_all x9, starting transfers between devices, swap(): return lax.all_to_all(chunks, axis, 0, 0, tiled=True)  31.5 us
    all_to_all x3, blocking collectives, swap(): return lax.all_to_all(chunks, axis, 0, 0, tiled=True)  24.6 us
    dot_general x4, matrix products, project_gram(): gram_comb = jnp.dot(gram, combined, precision=HIGHEST)  3.44 us
    broadcast_in_dim x7, local copies, waits for them, and re-layouts, gather(): return swap(jnp.broadcast_to(piece[None], (count,) + piece.shape), axis)  3.23 us
  transfers between devices with their start and end apart: 9, of which 9 were waited for; matrix products, arithmetic and copies ran while one was open for 2% of the time, Pallas kernels for 0%

profile of v1, /device:TPU:0, one launch (start us, length us, event | category | flops | bytes accessed | tf_op | source)
XLA Modules:
  0.0 153.0 jit_solution(1084927664362510394)
XLA Ops:
  0.7 1.3 copy.61
  2.8 1.0 fusion.67
  4.6 7.3 %all-to-all-start.1 = ((f32[32,1,261]{2,1,0:T(1,128)}), f32[32,1,261]{2,1,0:T(1,128)S(1)}, u32[]{:S(2)}, u32[]{:S(2)}) async-start(f32[32,1,261]{2,1,0:T(1,128)} %all_to_all.62), calls=%async_computation.1 | async-start | bytes 98304 | tf_op jit(solution)/shard_map/all_to_all | solution.py:15
  12.2 0.9 fusion.19
  13.1 1.0 fusion.32
  14.1 5.3 %all-to-all-done.1 = f32[32,1,261]{2,1,0:T(1,128)S(1)} async-done(((f32[32,1,261]{2,1,0:T(1,128)}), f32[32,1,261]{2,1,0:T(1,128)S(1)}, u32[]{:S(2)}, u32[]{:S(2)}) %all-to-all-start.1) | async-done | bytes 33440 | tf_op jit(solution)/shard_map/all_to_all | solution.py:15
  19.4 3.3 %all-to-all-start = ((f32[4,1,4096]{2,1,0:T(1,128)}), f32[4,1,4096]{2,1,0:T(1,128)S(1)}, u32[]{:S(2)}, u32[]{:S(2)}) async-start(f32[4,1,4096]{2,1,0:T(1,128)} %bitcast.7), calls=%async_computation | async-start | bytes 131072 | tf_op jit(solution)/shard_map/all_to_all | solution.py:15
  22.7 5.6 %all-to-all-done = f32[4,1,4096]{2,1,0:T(1,128)S(1)} async-done(((f32[4,1,4096]{2,1,0:T(1,128)}), f32[4,1,4096]{2,1,0:T(1,128)S(1)}, u32[]{:S(2)}, u32[]{:S(2)}) %all-to-all-start) | async-done | bytes 65568 | tf_op jit(solution)/shard_map/all_to_all | solution.py:15
  29.0 0.9 convolution_bitcast_fusion.1
  30.7 9.1 %all_to_all.90 = f32[32,1,326]{2,1,0:T(1,128)S(1)} all-to-all(f32[32,1,326]{2,1,0:T(1,128)S(1)} %broadcast_in_dim.42), channel_id=1, replica_groups=mesh['row'=8,'col'=4] {'row','col'}, dimensions={0} | all-to-all | bytes 83456 | tf_op jit(solution)/shard_map/all_to_all | solution.py:15
  44.3 8.1 %all_to_all.91 = f32[4,1,4096]{2,1,0:T(1,128)S(1)} all-to-all(f32[4,1,4096]{2,1,0:T(1,128)S(1)} %broadcast_in_dim.43), channel_id=1, replica_groups=mesh['row'=8,'col'=4] {'col'}, dimensions={0} | all-to-all | bytes 131072 | tf_op jit(solution)/shard_map/all_to_all | solution.py:15
  53.5 7.4 %all_to_all.92 = f32[8,1,2048]{2,1,0:T(1,128)S(1)} all-to-all(f32[8,1,2048]{2,1,0:T(1,128)S(1)} %bitcast.230), channel_id=1, replica_groups=mesh['row'=8,'col'=4] {'row'}, dimensions={0} | all-to-all | bytes 131072 | tf_op jit(solution)/shard_map/all_to_all | solution.py:15
  63.5 2.5 %all-to-all-start.5 = ((f32[32,1,66]{2,1,0:T(1,128)}), f32[32,1,66]{2,1,0:T(1,128)S(1)}, u32[]{:S(2)}, u32[]{:S(2)}) async-start(f32[32,1,66]{2,1,0:T(1,128)} %broadcast_in_dim.89), calls=%async_computation.5 | async-start | bytes 32768 | tf_op jit(solution)/shard_map/all_to_all | solution.py:15
  66.2 7.0 %all-to-all-done.5 = f32[32,1,66]{2,1,0:T(1,128)S(1)} async-done(((f32[32,1,66]{2,1,0:T(1,128)}), f32[32,1,66]{2,1,0:T(1,128)S(1)}, u32[]{:S(2)}, u32[]{:S(2)}) %all-to-all-start.5) | async-done | bytes 8480 | tf_op jit(solution)/shard_map/all_to_all | solution.py:15
  74.3 0.9 multiply_reduce_fusion.6
  77.9 3.3 %all-to-all-start.6 = ((f32[8,1,2048]{2,1,0:T(1,128)}), f32[8,1,2048]{2,1,0:T(1,128)S(1)}, u32[]{:S(2)}, u32[]{:S(2)}) async-start(f32[8,1,2048]{2,1,0:T(1,128)} %broadcast_in_dim.90), calls=%async_computation.6 | async-start | bytes 131072 | tf_op jit(solution)/shard_map/all_to_all | solution.py:15
  81.4 4.8 %all-to-all-done.6 = f32[8,1,2048]{2,1,0:T(1,128)S(1)} async-done(((f32[8,1,2048]{2,1,0:T(1,128)}), f32[8,1,2048]{2,1,0:T(1,128)S(1)}, u32[]{:S(2)}, u32[]{:S(2)}) %all-to-all-start.6) | async-done | bytes 65568 | tf_op jit(solution)/shard_map/all_to_all | solution.py:15
  86.4 0.9 fusion.15
  87.3 1.0 fusion.30
  88.3 3.3 %all-to-all-start.7 = ((f32[4,1,4096]{2,1,0:T(1,128)}), f32[4,1,4096]{2,1,0:T(1,128)S(1)}, u32[]{:S(2)}, u32[]{:S(2)}) async-start(f32[4,1,4096]{2,1,0:T(1,128)} %bitcast.42), calls=%async_computation.7 | async-start | bytes 131072 | tf_op jit(solution)/shard_map/all_to_all | solution.py:15
  91.7 5.6 %all-to-all-done.7 = f32[4,1,4096]{2,1,0:T(1,128)S(1)} async-done(((f32[4,1,4096]{2,1,0:T(1,128)}), f32[4,1,4096]{2,1,0:T(1,128)S(1)}, u32[]{:S(2)}, u32[]{:S(2)}) %all-to-all-start.7) | async-done | bytes 65568 | tf_op jit(solution)/shard_map/all_to_all | solution.py:15
  98.0 1.0 convolution_bitcast_fusion
  100.3 2.5 %all-to-all-start.8 = ((f32[32,1,66]{2,1,0:T(1,128)}), f32[32,1,66]{2,1,0:T(1,128)S(1)}, u32[]{:S(2)}, u32[]{:S(2)}) async-start(f32[32,1,66]{2,1,0:T(1,128)} %broadcast_in_dim.92), calls=%async_computation.8 | async-start | bytes 32768 | tf_op jit(solution)/shard_map/all_to_all | solution.py:15
  103.1 7.0 %all-to-all-done.8 = f32[32,1,66]{2,1,0:T(1,128)S(1)} async-done(((f32[32,1,66]{2,1,0:T(1,128)}), f32[32,1,66]{2,1,0:T(1,128)S(1)}, u32[]{:S(2)}, u32[]{:S(2)}) %all-to-all-start.8) | async-done | bytes 8480 | tf_op jit(solution)/shard_map/all_to_all | solution.py:15
  115.6 3.3 %all-to-all-start.9 = ((f32[4,1,4096]{2,1,0:T(1,128)}), f32[4,1,4096]{2,1,0:T(1,128)S(1)}, u32[]{:S(2)}, u32[]{:S(2)}) async-start(f32[4,1,4096]{2,1,0:T(1,128)} %broadcast_in_dim.97), calls=%async_computation.9 | async-start | bytes 131072 | tf_op jit(solution)/shard_map/all_to_all | solution.py:15
  119.0 5.6 %all-to-all-done.9 = f32[4,1,4096]{2,1,0:T(1,128)S(1)} async-done(((f32[4,1,4096]{2,1,0:T(1,128)}), f32[4,1,4096]{2,1,0:T(1,128)S(1)}, u32[]{:S(2)}, u32[]{:S(2)}) %all-to-all-start.9) | async-done | bytes 65568 | tf_op jit(solution)/shard_map/all_to_all | solution.py:15
  125.4 0.9 fusion.26
  126.3 3.3 %all-to-all-start.10 = ((f32[8,1,2048]{2,1,0:T(1,128)}), f32[8,1,2048]{2,1,0:T(1,128)S(1)}, u32[]{:S(2)}, u32[]{:S(2)}) async-start(f32[8,1,2048]{2,1,0:T(1,128)} %bitcast.64), calls=%async_computation.10 | async-start | bytes 131072 | tf_op jit(solution)/shard_map/all_to_all | solution.py:15
  130.3 4.3 %all-to-all-done.10 = f32[8,1,2048]{2,1,0:T(1,128)S(1)} async-done(((f32[8,1,2048]{2,1,0:T(1,128)}), f32[8,1,2048]{2,1,0:T(1,128)S(1)}, u32[]{:S(2)}, u32[]{:S(2)}) %all-to-all-start.10) | async-done | bytes 65568 | tf_op jit(solution)/shard_map/all_to_all | solution.py:15
  137.2 2.5 %all-to-all-start.11 = ((f32[32,1,67]{2,1,0:T(1,128)}), f32[32,1,67]{2,1,0:T(1,128)S(1)}, u32[]{:S(2)}, u32[]{:S(2)}) async-start(f32[32,1,67]{2,1,0:T(1,128)} %broadcast_in_dim.99), calls=%async_computation.11 | async-start | bytes 32768 | tf_op jit(solution)/shard_map/all_to_all | solution.py:15
  139.8 7.0 %all-to-all-done.11 = f32[32,1,67]{2,1,0:T(1,128)S(1)} async-done(((f32[32,1,67]{2,1,0:T(1,128)}), f32[32,1,67]{2,1,0:T(1,128)S(1)}, u32[]{:S(2)}, u32[]{:S(2)}) %all-to-all-start.11) | async-done | bytes 8608 | tf_op jit(solution)/shard_map/all_to_all | solution.py:15
  148.7 0.9 fusion.12
  (85 shorter events, 24.8 us)
Async XLA Ops:
  0.6 11.5 %copy-start = (bf16[1,16,128,128]{3,2,1,0:T(8,128)(2,1)S(1)}, bf16[1,16,128,128]{3,2,1,0:T(8,128)(2,1)}, u32[]{:S(2)}) copy-start(bf16[1,16,128,128]{3,2,1,0:T(8,128)(2,1)} %param.5) | copy-start | bytes 1572868
  0.6 1.4 copy-start.2
  0.7 2.1 %copy-start.1 = (f32[64,4096]{1,0:T(8,128)S(1)}, f32[64,4096]{1,0:T(8,128)}, u32[]{:S(2)}) copy-start(f32[64,4096]{1,0:T(8,128)} %param.7) | copy-start | bytes 3145732
  2.8 9.2 %copy-start.3 = (s32[1,16]{1,0:T(1,128)S(1)}, s32[1,16]{1,0:T(1,128)}, u32[]{:S(2)}) copy-start(s32[1,16]{1,0:T(1,128)} %param.6) | copy-start | bytes 196
  4.6 14.7 %all-to-all-start.1 = ((f32[32,1,261]{2,1,0:T(1,128)}), f32[32,1,261]{2,1,0:T(1,128)S(1)}, u32[]{:S(2)}, u32[]{:S(2)}) async-start(f32[32,1,261]{2,1,0:T(1,128)} %all_to_all.62), calls=%async_computation.1 | async-start | bytes 98304 | tf_op jit(solution)/shard_map/all_to_all | solution.py:15
  19.4 9.0 %all-to-all-start = ((f32[4,1,4096]{2,1,0:T(1,128)}), f32[4,1,4096]{2,1,0:T(1,128)S(1)}, u32[]{:S(2)}, u32[]{:S(2)}) async-start(f32[4,1,4096]{2,1,0:T(1,128)} %bitcast.7), calls=%async_computation | async-start | bytes 131072 | tf_op jit(solution)/shard_map/all_to_all | solution.py:15
  63.5 9.7 %all-to-all-start.5 = ((f32[32,1,66]{2,1,0:T(1,128)}), f32[32,1,66]{2,1,0:T(1,128)S(1)}, u32[]{:S(2)}, u32[]{:S(2)}) async-start(f32[32,1,66]{2,1,0:T(1,128)} %broadcast_in_dim.89), calls=%async_computation.5 | async-start | bytes 32768 | tf_op jit(solution)/shard_map/all_to_all | solution.py:15
  77.9 8.3 %all-to-all-start.6 = ((f32[8,1,2048]{2,1,0:T(1,128)}), f32[8,1,2048]{2,1,0:T(1,128)S(1)}, u32[]{:S(2)}, u32[]{:S(2)}) async-start(f32[8,1,2048]{2,1,0:T(1,128)} %broadcast_in_dim.90), calls=%async_computation.6 | async-start | bytes 131072 | tf_op jit(solution)/shard_map/all_to_all | solution.py:15
  88.3 9.0 %all-to-all-start.7 = ((f32[4,1,4096]{2,1,0:T(1,128)}), f32[4,1,4096]{2,1,0:T(1,128)S(1)}, u32[]{:S(2)}, u32[]{:S(2)}) async-start(f32[4,1,4096]{2,1,0:T(1,128)} %bitcast.42), calls=%async_computation.7 | async-start | bytes 131072 | tf_op jit(solution)/shard_map/all_to_all | solution.py:15
  100.3 9.7 %all-to-all-start.8 = ((f32[32,1,66]{2,1,0:T(1,128)}), f32[32,1,66]{2,1,0:T(1,128)S(1)}, u32[]{:S(2)}, u32[]{:S(2)}) async-start(f32[32,1,66]{2,1,0:T(1,128)} %broadcast_in_dim.92), calls=%async_computation.8 | async-start | bytes 32768 | tf_op jit(solution)/shard_map/all_to_all | solution.py:15
  115.6 9.0 %all-to-all-start.9 = ((f32[4,1,4096]{2,1,0:T(1,128)}), f32[4,1,4096]{2,1,0:T(1,128)S(1)}, u32[]{:S(2)}, u32[]{:S(2)}) async-start(f32[4,1,4096]{2,1,0:T(1,128)} %broadcast_in_dim.97), calls=%async_computation.9 | async-start | bytes 131072 | tf_op jit(solution)/shard_map/all_to_all | solution.py:15
  126.3 8.3 %all-to-all-start.10 = ((f32[8,1,2048]{2,1,0:T(1,128)}), f32[8,1,2048]{2,1,0:T(1,128)S(1)}, u32[]{:S(2)}, u32[]{:S(2)}) async-start(f32[8,1,2048]{2,1,0:T(1,128)} %bitcast.64), calls=%async_computation.10 | async-start | bytes 131072 | tf_op jit(solution)/shard_map/all_to_all | solution.py:15
  137.2 9.7 %all-to-all-start.11 = ((f32[32,1,67]{2,1,0:T(1,128)}), f32[32,1,67]{2,1,0:T(1,128)S(1)}, u32[]{:S(2)}, u32[]{:S(2)}) async-start(f32[32,1,67]{2,1,0:T(1,128)} %broadcast_in_dim.99), calls=%async_computation.11 | async-start | bytes 32768 | tf_op jit(solution)/shard_map/all_to_all | solution.py:15

commit v2 on v1

v2 whole, which is shorter than its diff:
```python
import jax
import jax.numpy as jnp
from jax import lax
from jax.experimental import pallas as pl
from jax.experimental.pallas import tpu as pltpu
from jax.sharding import PartitionSpec as P

ITERS = 2


HIGHEST = lax.Precision.HIGHEST
EPSILON = 1e-06
BOTH = ("row", "col")
LANES = 128
GROUP = 8
PARAMS = pltpu.CompilerParams(vmem_limit_bytes=8 * 2**20)
VMEM = pl.BlockSpec(memory_space=pltpu.VMEM)
SMEM = pl.BlockSpec(memory_space=pltpu.SMEM)


def swap(chunks, axis):
    return lax.all_to_all(chunks, axis, 0, 0, tiled=True)


def call(kernel, outs, args, specs=None):
    shapes = tuple(jax.ShapeDtypeStruct(shape, jnp.float32) for shape in outs)
    return pl.pallas_call(
        kernel,
        out_shape=shapes,
        in_specs=specs or [VMEM] * len(args),
        out_specs=tuple([VMEM] * len(outs)),
        compiler_params=PARAMS,
    )(*args)


def three_parts(x):
    high = x.astype(jnp.bfloat16)
    rest = x - high.astype(jnp.float32)
    middle = rest.astype(jnp.bfloat16)
    low = (rest - middle.astype(jnp.float32)).astype(jnp.bfloat16)
    return jnp.concatenate([high, middle, low], 0)


def multiply_tiles(tiles, slots, vector, in_blocks, out_blocks, is_forward):
    count, width = tiles.shape[0], tiles.shape[1]
    divisor = in_blocks if is_forward else out_blocks
    limit = in_blocks * out_blocks

    def kernel(slots_ref, tiles_ref, vector_ref, dense_ref, picked_ref):
        dense_ref[...] = jnp.zeros_like(dense_ref)
        for t in range(count):
            slot = jnp.minimum(slots_ref[t], limit - 1)
            row = slot // divisor
            source = slot - row * divisor if is_forward else row
            picked_ref[pl.ds(t, 1), :] = vector_ref[pl.ds(source, 1), :]
        parts = three_parts(picked_ref[...])
        contract = (((1,), (1,)), ((), ())) if is_forward else (((1,), (0,)), ((), ()))
        for t in range(count):
            result = lax.dot_general(parts, tiles_ref[t], contract, preferred_element_type=jnp.float32)
            slot = slots_ref[t]
            live = slot < limit
            slot = jnp.minimum(slot, limit - 1)
            row = slot // divisor
            target = row if is_forward else slot - row * divisor
            value = (
                result[t : t + 1]
                + result[count + t : count + t + 1]
                + result[2 * count + t : 2 * count + t + 1]
            )
            value = jnp.where(live, value, 0.0)
            dense_ref[pl.ds(target, 1), :] = dense_ref[pl.ds(target, 1), :] + value

    return pl.pallas_call(
        kernel,
        out_shape=jax.ShapeDtypeStruct((out_blocks, width), jnp.float32),
        in_specs=[SMEM, VMEM, VMEM],
        out_specs=VMEM,
        scratch_shapes=[pltpu.VMEM((count, width), jnp.float32)],
        compiler_params=PARAMS,
    )(slots, tiles, vector)


def diagonal(rows):
    shape = (rows, LANES)
    return lax.broadcasted_iota(jnp.int32, shape, 0) == lax.broadcasted_iota(jnp.int32, shape, 1)


def as_row(column):
    return jnp.sum(jnp.where(diagonal(column.shape[0]), column, 0.0), 0, keepdims=True)


def total_sum(x):
    return jnp.sum(jnp.sum(x, 0, keepdims=True), 1, keepdims=True)


def inner_products(received, basis, extras, copies):
    kept = basis.shape[0]
    rows = received.shape[1]

    def kernel(received_ref, basis_ref, *refs):
        extra_refs, piece_ref, row_ref = refs[: len(extras)], refs[-2], refs[-1]
        piece = jnp.sum(received_ref[...], 0)
        piece_ref[...] = piece
        total = jnp.zeros((kept, LANES), jnp.float32)
        for k in range(rows):
            total = total + basis_ref[:, k * LANES : (k + 1) * LANES] * piece[k : k + 1, :]
        row = as_row(jnp.sum(total, 1, keepdims=True))
        lane = lax.broadcasted_iota(jnp.int32, (1, LANES), 1)
        for e, extra_ref in enumerate(extra_refs):
            row = row + jnp.where(lane == kept + e, total_sum(extra_ref[...] * piece), 0.0)
        row = row + jnp.where(lane == LANES - 1, total_sum(piece * piece), 0.0)
        row_ref[...] = jnp.broadcast_to(row, row_ref.shape)

    return call(kernel, [(rows, LANES), (copies, LANES)], [received, basis, *extras])


def new_vector(rows_received, gram, piece, basis, extras, total, copies):
    kept = basis.shape[0]
    rows = piece.shape[0]
    size = kept + len(extras)
    padded = gram.shape[0]

    def kernel(received_ref, gram_ref, piece_ref, basis_ref, *refs):
        extra_refs = refs[: len(extras)]
        copies_ref, gram_out_ref, scale_ref = refs[len(extras) :]
        sums = jnp.sum(received_ref[...], 0, keepdims=True) * (1.0 / total)
        lane = lax.broadcasted_iota(jnp.int32, (1, LANES), 1)
        coeffs = jnp.where(lane < size, sums, 0.0)
        squares = jnp.sum(jnp.where(lane == LANES - 1, sums, 0.0), 1, keepdims=True)
        products = gram_ref[...]
        eye = diagonal(padded)
        coeffs_col = jnp.sum(jnp.where(eye, coeffs, 0.0), 1, keepdims=True)
        combined = 2.0 * coeffs_col - jnp.sum(products * coeffs, 1, keepdims=True)
        gram_comb = jnp.sum(products * as_row(combined), 1, keepdims=True)
        remaining = coeffs_col - gram_comb
        squared = squares + jnp.sum(combined * (gram_comb - 2.0 * coeffs_col), 0, keepdims=True)
        squared = jnp.maximum(squared, 0.0)
        scale = jnp.sqrt(squared + EPSILON)
        inverse = 1.0 / scale
        spread = jnp.broadcast_to(combined[:kept], (kept, LANES))
        own = piece_ref[...]
        for e, extra_ref in enumerate(extra_refs):
            own = own - combined[kept + e : kept + e + 1] * extra_ref[...]
        for k in range(rows):
            part = jnp.sum(spread * basis_ref[:, k * LANES : (k + 1) * LANES], 0, keepdims=True)
            line = (own[k : k + 1, :] - part) * inverse
            for copy in range(copies):
                copies_ref[copy, pl.ds(k, 1), :] = line
        remaining = remaining * inverse
        sub_at = lax.broadcasted_iota(jnp.int32, (padded, LANES), 0)
        lane_at = lax.broadcasted_iota(jnp.int32, (padded, LANES), 1)
        wider = jnp.where((lane_at == size) & (sub_at < size), remaining, products)
        wider = jnp.where((sub_at == size) & (lane_at < size), as_row(remaining), wider)
        wider = jnp.where((sub_at == size) & (lane_at == size), squared * inverse * inverse, wider)
        gram_out_ref[...] = wider
        scale_ref[...] = jnp.broadcast_to(scale, scale_ref.shape)

    return call(
        kernel,
        [(copies, rows, LANES), (padded, LANES), (1, LANES)],
        [rows_received, gram, piece, basis, *extras],
    )


def shards(tiles, tile_index, u_basis, v_basis, v_start):
    blocks = tiles[0]
    slots = tile_index[0]
    width = blocks.shape[1]
    cols_len = v_start.shape[0]
    col_blocks = cols_len // width
    row_count = lax.axis_size("row")
    col_count = lax.axis_size("col")
    devices = row_count * col_count
    kept = u_basis.shape[0]
    left_piece = u_basis.shape[1]
    right_piece = v_basis.shape[2]
    rows_len = left_piece * col_count
    row_blocks = rows_len // width
    left_rows = left_piece // width
    right_rows = right_piece // width
    total_left = rows_len * row_count
    total_right = cols_len * col_count
    padded = kept + GROUP

    whole_start = v_start.reshape(col_blocks, width)
    dense = multiply_tiles(blocks, slots, whole_start, col_blocks, row_blocks, True)
    chunks = dense.reshape(col_count, left_rows, width)
    me = lax.axis_index("col")
    arrived = [lax.dynamic_index_in_dim(chunks, me, 0, True)]
    for shift in range(1, col_count):
        pairs = [(i, (i + shift) % col_count) for i in range(col_count)]
        chunk = lax.dynamic_index_in_dim(chunks, (me + shift) % col_count, 0, True)
        arrived.append(lax.ppermute(chunk, "col", pairs))
    received = jnp.concatenate(arrived, 0)

    right_basis = v_basis[:, 0, :]
    start_share = lax.dynamic_slice_in_dim(
        whole_start, lax.axis_index("row") * right_rows, right_rows, 0
    )
    grams = jnp.concatenate(
        [
            jnp.dot(u_basis, u_basis.T, precision=HIGHEST) / total_left,
            jnp.dot(right_basis, right_basis.T, precision=HIGHEST) / total_right,
        ],
        1,
    )
    chunk = grams.size // devices
    gram_chunk = jnp.sum(swap(grams.reshape(devices, chunk), BOTH), 0)
    chunk_rows = -(-chunk // LANES)
    gram_chunk = jnp.pad(gram_chunk, (0, chunk_rows * LANES - chunk)).reshape(1, chunk_rows, LANES)
    _, start_row = inner_products(start_share[None], right_basis, [start_share], 1)

    lefts, rights, alphas, betas = ([], [], [], [])
    left_extras, right_extras = ([], [start_share])
    for iteration in range(ITERS):
        piece, row = inner_products(received, u_basis, left_extras, devices)
        row = row.reshape(devices, 1, LANES)
        if iteration == 0:
            start_rows = jnp.broadcast_to(start_row[None], (devices, 1, LANES))
            chunk_sent = jnp.broadcast_to(gram_chunk, (devices, chunk_rows, LANES))
            everything = swap(jnp.concatenate([row, start_rows, chunk_sent], 1), BOTH)
            summed_rows = everything[:, 0, :]
            start_products = jnp.sum(everything[:, 1, :], 0) / total_right
            whole = everything[:, 2:, :].reshape(devices, chunk_rows * LANES)[:, :chunk]
            whole = whole.reshape(kept, 2 * kept)
            left_gram = jnp.pad(whole[:, :kept], ((0, GROUP), (0, LANES - kept)))
            lane = jnp.arange(LANES)
            start_products = jnp.where(lane <= kept, start_products, 0.0)
            right_gram = jnp.pad(whole[:, kept:], ((0, GROUP), (0, LANES - kept)))
            right_gram = right_gram.at[kept, :].set(start_products)
            right_gram = right_gram.at[:, kept].set(start_products[:padded])
        else:
            summed_rows = swap(row, BOTH).reshape(devices, LANES)
        copies, left_gram, alpha = new_vector(
            summed_rows, left_gram, piece, u_basis, left_extras, total_left, col_count
        )
        left_unit = copies[0]
        left_extras = left_extras + [left_unit]
        joined = swap(copies, "col").reshape(row_blocks, width)
        dense = multiply_tiles(blocks, slots, joined, row_blocks, col_blocks, False)
        received = swap(dense.reshape(row_count, right_rows, width), "row")
        piece, row = inner_products(received, right_basis, right_extras, devices)
        summed_rows = swap(row.reshape(devices, 1, LANES), BOTH).reshape(devices, LANES)
        copies, right_gram, beta = new_vector(
            summed_rows, right_gram, piece, right_basis, right_extras, total_right, row_count
        )
        right_unit = copies[0]
        right_extras = right_extras + [right_unit]
        if iteration + 1 < ITERS:
            joined = swap(copies, "row").reshape(col_blocks, width)
            dense = multiply_tiles(blocks, slots, joined, col_blocks, row_blocks, True)
            received = swap(dense.reshape(col_count, left_rows, width), "col")
        lefts.append(left_unit.reshape(-1))
        rights.append(right_unit.reshape(-1))
        alphas.append(alpha[0, 0])
        betas.append(beta[0, 0])
    left_vectors = jnp.stack(lefts)
    right_vectors = jnp.stack(rights)[:, None, :]
    bidiagonal = jnp.stack([jnp.stack(alphas), jnp.stack(betas)])
    return (left_vectors, right_vectors, bidiagonal)


def solution(mesh):
    placed = (
        P("row", "col", None, None),
        P("row", "col"),
        P(None, ("row", "col")),
        P(None, "col", "row"),
        P("col"),
    )
    return jax.shard_map(
        shards,
        mesh=mesh,
        in_specs=placed,
        out_specs=(P(None, ("row", "col")), P(None, "col", "row"), P()),
        check_vma=False,
    )
```

time: 154 us -> 126 us (0.82)
  matrix products: 19.1 us -> 4.71 us
  Pallas kernels: 0 us -> 11.1 us
  waiting for transfers between devices: 52.3 us -> 43.6 us
  between operations: 9.05 us -> 0.93 us
  local copies, waits for them, and re-layouts: 9.14 us -> 2.81 us
  other arithmetic: 7.35 us -> 4.2 us
  starting transfers between devices: 31.5 us -> 33.8 us
    dot_general x30 -> x2, matrix products: 19.1 us -> 4.71 us  [the longest x1 2.6 us: shards(): jnp.dot(u_basis, u_basis.T, precision=HIGHEST) / total_left]
    all_to_all x9 -> x8, waiting for transfers between devices: 52.3 us -> 39.9 us  [swap(): return lax.all_to_all(chunks, axis, 0, 0, tiled=True)]
    pallas_call x0 -> x13, Pallas kernels: none -> 11.1 us  [the longest x4 5.74 us: multiply_tiles(): pl.pallas_call(kernel, out_shape=jax.ShapeDtypeStruct((out_blocks, width)...]
    ppermute x0 -> x3, starting transfers between devices: none -> 4.75 us  [shards(): arrived.append(lax.ppermute(chunk, 'col', pairs))]
    ppermute x0 -> x3, waiting for transfers between devices: none -> 3.64 us  [shards(): arrived.append(lax.ppermute(chunk, 'col', pairs))]
    broadcast_in_dim x9 -> x3, local copies, waits for them, and re-layouts: 3.43 us -> 0.03 us  [the longest x1 0.01 us: shards(): chunk_sent = jnp.broadcast_to(gram_chunk, (devices, chunk_rows, LANES))]
    reduce_sum x13 -> x2, other arithmetic: 2.8 us -> 0.11 us  [the longest x1 0.05 us: shards(): gram_chunk = jnp.sum(swap(grams.reshape(devices, chunk), BOTH), 0)]
    all_to_all x9 -> x8, starting transfers between devices: 31.5 us -> 29 us  [swap(): return lax.all_to_all(chunks, axis, 0, 0, tiled=True)]
  transfers between devices with their start and end apart: 9 -> 11, of which waited for: 9 -> 9; matrix products, arithmetic and copies ran while one was open for 2% -> 3% of each run, Pallas kernels for 0% -> 1%
where the time goes in v2:
time: 126 us; the launch traced here: 125 us
  waiting for transfers between devices  43.6 us (35%)
  starting transfers between devices  33.8 us (27%)
  blocking collectives  24.4 us (19%)
  Pallas kernels  11.1 us (9%)
  matrix products  4.71 us (4%)
  other arithmetic  4.2 us (3%)
  local copies, waits for them, and re-layouts  2.81 us (2%)
    all_to_all x8, waiting for transfers between devices, swap(): return lax.all_to_all(chunks, axis, 0, 0, tiled=True)  39.9 us
    all_to_all x8, starting transfers between devices, swap(): return lax.all_to_all(chunks, axis, 0, 0, tiled=True)  29 us
    all_to_all x3, blocking collectives, swap(): return lax.all_to_all(chunks, axis, 0, 0, tiled=True)  24.4 us
    pallas_call x4, Pallas kernels, multiply_tiles(): pl.pallas_call(kernel, out_shape=jax.ShapeDtypeStruct((out_blocks, width)...  5.74 us
    pallas_call x9, Pallas kernels, call(): pl.pallas_call(kernel, out_shape=shapes, in_specs=specs or [VMEM] * len(a...  5.38 us
    ppermute x3, starting transfers between devices, shards(): arrived.append(lax.ppermute(chunk, 'col', pairs))  4.75 us
    ppermute x3, waiting for transfers between devices, shards(): arrived.append(lax.ppermute(chunk, 'col', pairs))  3.64 us
    dot_general x1, matrix products, shards(): jnp.dot(u_basis, u_basis.T, precision=HIGHEST) / total_left  2.6 us
  transfers between devices with their start and end apart: 11, of which 9 were waited for; matrix products, arithmetic and copies ran while one was open for 3% of the time, Pallas kernels for 1%

profile of v2, /device:TPU:0, one launch (start us, length us, event | category | flops | bytes accessed | tf_op | source)
XLA Modules:
  0.0 125.5 jit_solution(15188006397636478942)
XLA Ops:
  0.6 2.1 %convolution_multiply_fusion = f32[64,64]{1,0:T(8,128)S(1)} fusion(f32[64,1,2048]{2,1,0:T(1,128)} %param.12), kind=kOutput, calls=%fused_computation | convolution fusion | flops 100667392 | bytes 540672 | tf_op jit(solution)/shard_map/dot_general | solution.py:203
  2.8 2.6 %convolution_multiply_fusion.1 = f32[64,64]{1,0:T(8,128)S(1)} fusion(f32[64,4096]{1,0:T(8,128)} %basis_ref.7), kind=kOutput, calls=%fused_computation.1 | convolution fusion | flops 201330688 | bytes 1064960 | tf_op jit(solution)/shard_map/dot_general | solution.py:202
  6.1 7.3 %all-to-all-start = ((f32[32,1,256]{2,1,0:T(1,128)}), f32[32,1,256]{2,1,0:T(1,128)S(1)}, u32[]{:S(2)}, u32[]{:S(2)}) async-start(f32[32,1,256]{2,1,0:T(1,128)} %bitcast.8), calls=%async_computation | async-start | bytes 65536 | tf_op jit(solution)/shard_map/all_to_all | solution.py:22
  13.5 0.8 copy-done.2
  14.2 1.0 shard_map.76
  15.3 3.7 %collective-permute-start.2 = (f32[1,32,128]{2,1,0:T(8,128)S(1)}, f32[1,32,128]{2,1,0:T(8,128)S(1)}, u32[]{:S(2)}, u32[]{:S(2)}) collective-permute-start(f32[1,32,128]{2,1,0:T(8,128)S(1)} %get-tuple-element.72), channel_id=1, source_target_pairs={{0,3},{1,0},{2,1},{3,2},{4,7},{5,4},{6,5},{7,6},{8,11},{9,8},{10,9... | collective-permute-start | bytes 49160 | tf_op jit(solution)/shard_map/ppermute | solution.py:193
  19.0 1.1 collective-permute-start
  20.9 2.7 %collective-permute-done.1 = f32[1,32,128]{2,1,0:T(8,128)S(1)} collective-permute-done((f32[1,32,128]{2,1,0:T(8,128)S(1)}, f32[1,32,128]{2,1,0:T(8,128)S(1)}, u32[]{:S(2)}, u32[]{:S(2)}) %collective-permute-start.1) | collective-permute-done | bytes 16416 | tf_op jit(solution)/shard_map/ppermute | solution.py:193
  23.6 0.9 collective-permute-done
  25.5 3.3 %all-to-all-start.1 = ((f32[32,4,128]{2,1,0:T(4,128)}), f32[32,4,128]{2,1,0:T(4,128)S(1)}, u32[]{:S(2)}, u32[]{:S(2)}) async-start(f32[32,4,128]{2,1,0:T(4,128)} %pad_maximum_fusion.1), calls=%async_computation.1 | async-start | bytes 131072 | tf_op jit(solution)/shard_map/all_to_all | solution.py:22
  29.5 6.9 %all-to-all-done.1 = f32[32,4,128]{2,1,0:T(4,128)S(1)} async-done(((f32[32,4,128]{2,1,0:T(4,128)}), f32[32,4,128]{2,1,0:T(4,128)S(1)}, u32[]{:S(2)}, u32[]{:S(2)}) %all-to-all-start.1) | async-done | bytes 65568 | tf_op jit(solution)/shard_map/all_to_all | solution.py:22
  36.5 0.9 shard_map.79
  37.4 3.3 %all-to-all-start.2 = ((f32[4,32,128]{2,1,0:T(8,128)}), f32[4,32,128]{2,1,0:T(8,128)S(1)}, u32[]{:S(2)}, u32[]{:S(2)}) async-start(f32[4,32,128]{2,1,0:T(8,128)} %get-tuple-element.49), calls=%async_computation.2 | async-start | bytes 131072 | tf_op jit(solution)/shard_map/all_to_all | solution.py:22
  40.7 5.7 %all-to-all-done.2 = f32[4,32,128]{2,1,0:T(8,128)S(1)} async-done(((f32[4,32,128]{2,1,0:T(8,128)}), f32[4,32,128]{2,1,0:T(8,128)S(1)}, u32[]{:S(2)}, u32[]{:S(2)}) %all-to-all-start.2) | async-done | bytes 65568 | tf_op jit(solution)/shard_map/all_to_all | solution.py:22
  46.4 1.5 %shard_map.80 = f32[128,128]{1,0:T(8,128)} custom-call(s32[16]{0:T(128)S(1)} %bitcast.87, bf16[16,128,128]{2,1,0:T(8,128)(2,1)S(1)} %bitcast.70, f32[128,128]{1,0:T(8,128)S(1)} %bitcast.73), custom_call_target="tpu_custom_call" | custom-call | tf_op jit(solution)/shard_map/pallas_call | solution.py:73
  47.9 3.3 %all-to-all-start.3 = ((f32[8,16,128]{2,1,0:T(8,128)}), f32[8,16,128]{2,1,0:T(8,128)S(1)}, u32[]{:S(2)}, u32[]{:S(2)}) async-start(f32[8,16,128]{2,1,0:T(8,128)} %bitcast.14), calls=%async_computation.3 | async-start | bytes 131072 | tf_op jit(solution)/shard_map/all_to_all | solution.py:22
  51.4 4.8 %all-to-all-done.3.received_ref = f32[8,16,128]{2,1,0:T(8,128)S(1)} async-done(((f32[8,16,128]{2,1,0:T(8,128)}), f32[8,16,128]{2,1,0:T(8,128)S(1)}, u32[]{:S(2)}, u32[]{:S(2)}) %all-to-all-start.3) | async-done | bytes 65568 | tf_op jit(solution)/shard_map/all_to_all | solution.py:22
  57.0 2.5 %all-to-all-start.4 = ((f32[32,1,128]{2,1,0:T(1,128)}), f32[32,1,128]{2,1,0:T(1,128)S(1)}, u32[]{:S(2)}, u32[]{:S(2)}) async-start(f32[32,1,128]{2,1,0:T(1,128)} %bitcast.16), calls=%async_computation.4 | async-start | bytes 32768 | tf_op jit(solution)/shard_map/all_to_all | solution.py:22
  60.5 6.2 %all-to-all-done.4 = f32[32,1,128]{2,1,0:T(1,128)S(1)} async-done(((f32[32,1,128]{2,1,0:T(1,128)}), f32[32,1,128]{2,1,0:T(1,128)S(1)}, u32[]{:S(2)}, u32[]{:S(2)}) %all-to-all-start.4) | async-done | bytes 16416 | tf_op jit(solution)/shard_map/all_to_all | solution.py:22
  66.9 7.4 %all_to_all.59 = f32[8,16,128]{2,1,0:T(8,128)S(1)} all-to-all(f32[8,16,128]{2,1,0:T(8,128)S(1)} %get-tuple-element.52), channel_id=1, replica_groups=mesh['row'=8,'col'=4] {'row'}, dimensions={0} | all-to-all | bytes 131072 | tf_op jit(solution)/shard_map/all_to_all | solution.py:22
  74.3 1.7 %shard_map.83 = f32[128,128]{1,0:T(8,128)} custom-call(s32[16]{0:T(128)S(1)} %bitcast.88, bf16[16,128,128]{2,1,0:T(8,128)(2,1)S(1)} %bitcast.71, f32[128,128]{1,0:T(8,128)S(1)} %bitcast.75), custom_call_target="tpu_custom_call" | custom-call | tf_op jit(solution)/shard_map/pallas_call | solution.py:73
  76.0 3.3 %all-to-all-start.6 = ((f32[4,32,128]{2,1,0:T(8,128)}), f32[4,32,128]{2,1,0:T(8,128)S(1)}, u32[]{:S(2)}, u32[]{:S(2)}) async-start(f32[4,32,128]{2,1,0:T(8,128)} %bitcast.21), calls=%async_computation.6 | async-start | bytes 131072 | tf_op jit(solution)/shard_map/all_to_all | solution.py:22
  80.0 5.0 %all-to-all-done.6.received_ref = f32[4,32,128]{2,1,0:T(8,128)S(1)} async-done(((f32[4,32,128]{2,1,0:T(8,128)}), f32[4,32,128]{2,1,0:T(8,128)S(1)}, u32[]{:S(2)}, u32[]{:S(2)}) %all-to-all-start.6) | async-done | bytes 65568 | tf_op jit(solution)/shard_map/all_to_all | solution.py:22
  85.1 8.9 %all_to_all.60 = f32[32,1,128]{2,1,0:T(1,128)S(1)} all-to-all(f32[32,1,128]{2,1,0:T(1,128)S(1)} %bitcast.84), channel_id=1, replica_groups=mesh['row'=8,'col'=4] {'row','col'}, dimensions={0} | all-to-all | bytes 32768 | tf_op jit(solution)/shard_map/all_to_all | solution.py:22
  94.0 0.9 shard_map.85
  94.9 8.1 %all_to_all.61 = f32[4,32,128]{2,1,0:T(8,128)S(1)} all-to-all(f32[4,32,128]{2,1,0:T(8,128)S(1)} %get-tuple-element.56), channel_id=1, replica_groups=mesh['row'=8,'col'=4] {'col'}, dimensions={0} | all-to-all | bytes 131072 | tf_op jit(solution)/shard_map/all_to_all | solution.py:22
  103.0 1.5 %shard_map.86 = f32[128,128]{1,0:T(8,128)} custom-call(s32[16]{0:T(128)S(1)} %bitcast.89, bf16[16,128,128]{2,1,0:T(8,128)(2,1)S(1)} %bitcast.72, f32[128,128]{1,0:T(8,128)S(1)} %bitcast.76), custom_call_target="tpu_custom_call" | custom-call | tf_op jit(solution)/shard_map/pallas_call | solution.py:73
  104.6 3.3 %all-to-all-start.9 = ((f32[8,16,128]{2,1,0:T(8,128)}), f32[8,16,128]{2,1,0:T(8,128)S(1)}, u32[]{:S(2)}, u32[]{:S(2)}) async-start(f32[8,16,128]{2,1,0:T(8,128)} %bitcast.29), calls=%async_computation.9 | async-start | bytes 131072 | tf_op jit(solution)/shard_map/all_to_all | solution.py:22
  107.9 4.9 %all-to-all-done.9.received_ref = f32[8,16,128]{2,1,0:T(8,128)S(1)} async-done(((f32[8,16,128]{2,1,0:T(8,128)}), f32[8,16,128]{2,1,0:T(8,128)S(1)}, u32[]{:S(2)}, u32[]{:S(2)}) %all-to-all-start.9) | async-done | bytes 65568 | tf_op jit(solution)/shard_map/all_to_all | solution.py:22
  113.6 2.5 %all-to-all-start.10 = ((f32[32,1,128]{2,1,0:T(1,128)}), f32[32,1,128]{2,1,0:T(1,128)S(1)}, u32[]{:S(2)}, u32[]{:S(2)}) async-start(f32[32,1,128]{2,1,0:T(1,128)} %bitcast.32), calls=%async_computation.10 | async-start | bytes 32768 | tf_op jit(solution)/shard_map/all_to_all | solution.py:22
  116.8 6.5 %all-to-all-done.10 = f32[32,1,128]{2,1,0:T(1,128)S(1)} async-done(((f32[32,1,128]{2,1,0:T(1,128)}), f32[32,1,128]{2,1,0:T(1,128)S(1)}, u32[]{:S(2)}, u32[]{:S(2)}) %all-to-all-start.10) | async-done | bytes 16416 | tf_op jit(solution)/shard_map/all_to_all | solution.py:22
  123.3 0.9 shard_map.88
  (50 shorter events, 9.0 us)
Async XLA Ops:
  2.7 10.7 %copy-start.1 = (bf16[1,16,128,128]{3,2,1,0:T(8,128)(2,1)S(1)}, bf16[1,16,128,128]{3,2,1,0:T(8,128)(2,1)}, u32[]{:S(2)}) copy-start(bf16[1,16,128,128]{3,2,1,0:T(8,128)(2,1)} %param.9) | copy-start | bytes 1572868
  2.8 17.3 %copy-start.4 = (f32[64,1,2048]{2,1,0:T(1,128)S(1)}, f32[64,1,2048]{2,1,0:T(1,128)}, u32[]{:S(2)}) copy-start(f32[64,1,2048]{2,1,0:T(1,128)} %param.12) | copy-start | bytes 1572868
  6.1 18.6 %all-to-all-start = ((f32[32,1,256]{2,1,0:T(1,128)}), f32[32,1,256]{2,1,0:T(1,128)S(1)}, u32[]{:S(2)}, u32[]{:S(2)}) async-start(f32[32,1,256]{2,1,0:T(1,128)} %bitcast.8), calls=%async_computation | async-start | bytes 65536 | tf_op jit(solution)/shard_map/all_to_all | solution.py:22
  13.4 0.8 copy-start.2
  13.5 0.8 copy-start.3
  15.3 9.3 %copy-start = (f32[64,4096]{1,0:T(8,128)S(1)}, f32[64,4096]{1,0:T(8,128)}, u32[]{:S(2)}) copy-start(f32[64,4096]{1,0:T(8,128)} %basis_ref.7) | copy-start | bytes 3145732
  15.3 5.6 %collective-permute-start.2 = (f32[1,32,128]{2,1,0:T(8,128)S(1)}, f32[1,32,128]{2,1,0:T(8,128)S(1)}, u32[]{:S(2)}, u32[]{:S(2)}) collective-permute-start(f32[1,32,128]{2,1,0:T(8,128)S(1)} %get-tuple-element.72), channel_id=1, source_target_pairs={{0,3},{1,0},{2,1},{3,2},{4,7},{5,4},{6,5},{7,6},{8,11},{9,8},{10,9... | collective-permute-start | bytes 49160 | tf_op jit(solution)/shard_map/ppermute | solution.py:193
  19.0 4.6 %collective-permute-start.1 = (f32[1,32,128]{2,1,0:T(8,128)S(1)}, f32[1,32,128]{2,1,0:T(8,128)S(1)}, u32[]{:S(2)}, u32[]{:S(2)}) collective-permute-start(f32[1,32,128]{2,1,0:T(8,128)S(1)} %get-tuple-element.73), channel_id=1, source_target_pairs={{0,2},{1,3},{2,0},{3,1},{4,6},{5,7},{6,4},{7,5},{8,10},{9,11},{10,... | collective-permute-start | bytes 49160 | tf_op jit(solution)/shard_map/ppermute | solution.py:193
  19.0 5.5 %collective-permute-start = (f32[1,32,128]{2,1,0:T(8,128)S(1)}, f32[1,32,128]{2,1,0:T(8,128)S(1)}, u32[]{:S(2)}, u32[]{:S(2)}) collective-permute-start(f32[1,32,128]{2,1,0:T(8,128)S(1)} %get-tuple-element.74), channel_id=1, source_target_pairs={{0,1},{1,2},{2,3},{3,0},{4,5},{5,6},{6,7},{7,4},{8,9},{9,10},{10,1... | collective-permute-start | bytes 49160 | tf_op jit(solution)/shard_map/ppermute | solution.py:193
  25.5 10.8 %all-to-all-start.1 = ((f32[32,4,128]{2,1,0:T(4,128)}), f32[32,4,128]{2,1,0:T(4,128)S(1)}, u32[]{:S(2)}, u32[]{:S(2)}) async-start(f32[32,4,128]{2,1,0:T(4,128)} %pad_maximum_fusion.1), calls=%async_computation.1 | async-start | bytes 131072 | tf_op jit(solution)/shard_map/all_to_all | solution.py:22
  37.4 9.0 %all-to-all-start.2 = ((f32[4,32,128]{2,1,0:T(8,128)}), f32[4,32,128]{2,1,0:T(8,128)S(1)}, u32[]{:S(2)}, u32[]{:S(2)}) async-start(f32[4,32,128]{2,1,0:T(8,128)} %get-tuple-element.49), calls=%async_computation.2 | async-start | bytes 131072 | tf_op jit(solution)/shard_map/all_to_all | solution.py:22
  47.9 8.3 %all-to-all-start.3 = ((f32[8,16,128]{2,1,0:T(8,128)}), f32[8,16,128]{2,1,0:T(8,128)S(1)}, u32[]{:S(2)}, u32[]{:S(2)}) async-start(f32[8,16,128]{2,1,0:T(8,128)} %bitcast.14), calls=%async_computation.3 | async-start | bytes 131072 | tf_op jit(solution)/shard_map/all_to_all | solution.py:22
  57.0 9.7 %all-to-all-start.4 = ((f32[32,1,128]{2,1,0:T(1,128)}), f32[32,1,128]{2,1,0:T(1,128)S(1)}, u32[]{:S(2)}, u32[]{:S(2)}) async-start(f32[32,1,128]{2,1,0:T(1,128)} %bitcast.16), calls=%async_computation.4 | async-start | bytes 32768 | tf_op jit(solution)/shard_map/all_to_all | solution.py:22
  76.0 9.0 %all-to-all-start.6 = ((f32[4,32,128]{2,1,0:T(8,128)}), f32[4,32,128]{2,1,0:T(8,128)S(1)}, u32[]{:S(2)}, u32[]{:S(2)}) async-start(f32[4,32,128]{2,1,0:T(8,128)} %bitcast.21), calls=%async_computation.6 | async-start | bytes 131072 | tf_op jit(solution)/shard_map/all_to_all | solution.py:22
  104.6 8.3 %all-to-all-start.9 = ((f32[8,16,128]{2,1,0:T(8,128)}), f32[8,16,128]{2,1,0:T(8,128)S(1)}, u32[]{:S(2)}, u32[]{:S(2)}) async-start(f32[8,16,128]{2,1,0:T(8,128)} %bitcast.29), calls=%async_computation.9 | async-start | bytes 131072 | tf_op jit(solution)/shard_map/all_to_all | solution.py:22
  113.6 9.7 %all-to-all-start.10 = ((f32[32,1,128]{2,1,0:T(1,128)}), f32[32,1,128]{2,1,0:T(1,128)S(1)}, u32[]{:S(2)}, u32[]{:S(2)}) async-start(f32[32,1,128]{2,1,0:T(1,128)} %bitcast.32), calls=%async_computation.10 | async-start | bytes 32768 | tf_op jit(solution)/shard_map/all_to_all | solution.py:22

commit v3 on v2

v3 whole, which is shorter than its diff:
```python
import jax
import jax.numpy as jnp
from jax import lax
from jax.experimental import pallas as pl
from jax.experimental.pallas import tpu as pltpu
from jax.sharding import PartitionSpec as P

ITERS = 2


HIGHEST = lax.Precision.HIGHEST
EPSILON = 1e-06
BOTH = ("row", "col")
LANES = 128
GROUP = 8
PARAMS = pltpu.CompilerParams(vmem_limit_bytes=8 * 2**20)
VMEM = pl.BlockSpec(memory_space=pltpu.VMEM)
SMEM = pl.BlockSpec(memory_space=pltpu.SMEM)


def swap(chunks, axis):
    return lax.all_to_all(chunks, axis, 0, 0, tiled=True)


def call(kernel, outs, args, specs=None):
    shapes = tuple(jax.ShapeDtypeStruct(shape, jnp.float32) for shape in outs)
    return pl.pallas_call(
        kernel,
        out_shape=shapes,
        in_specs=specs or [VMEM] * len(args),
        out_specs=tuple([VMEM] * len(outs)),
        compiler_params=PARAMS,
    )(*args)


def three_parts(x):
    high = x.astype(jnp.bfloat16)
    rest = x - high.astype(jnp.float32)
    middle = rest.astype(jnp.bfloat16)
    low = (rest - middle.astype(jnp.float32)).astype(jnp.bfloat16)
    return jnp.concatenate([high, middle, low], 0)


def multiply_tiles(tiles, slots, vector, in_blocks, out_blocks, is_forward):
    count, width = tiles.shape[0], tiles.shape[1]
    divisor = in_blocks if is_forward else out_blocks
    limit = in_blocks * out_blocks
    contract = (((1,), (1,)), ((), ())) if is_forward else (((1,), (0,)), ((), ()))

    def kernel(slots_ref, tiles_ref, vector_ref, dense_ref, picked_ref, product_ref):
        targets = []
        for t in range(count):
            slot = slots_ref[t]
            live = slot < limit
            slot = jnp.where(live, slot, 0)
            row = lax.div(slot, divisor)
            column = slot - row * divisor
            source = column if is_forward else row
            targets.append(row if is_forward else column)
            line = vector_ref[pl.ds(source, 1), :]
            picked_ref[pl.ds(t, 1), :] = jnp.where(live, line, 0.0)
        parts = three_parts(picked_ref[...])
        dense_ref[...] = jnp.zeros_like(dense_ref)
        for t in range(count):
            result = lax.dot_general(parts, tiles_ref[t], contract, preferred_element_type=jnp.float32)
            product_ref[pl.ds(t, 1), :] = (
                result[t : t + 1]
                + result[count + t : count + t + 1]
                + result[2 * count + t : 2 * count + t + 1]
            )
        for t in range(count):
            line = pl.ds(targets[t], 1)
            dense_ref[line, :] = dense_ref[line, :] + product_ref[pl.ds(t, 1), :]

    return pl.pallas_call(
        kernel,
        out_shape=jax.ShapeDtypeStruct((out_blocks, width), jnp.float32),
        in_specs=[SMEM, VMEM, VMEM],
        out_specs=VMEM,
        scratch_shapes=[pltpu.VMEM((count, width), jnp.float32)] * 2,
        compiler_params=PARAMS,
    )(slots, tiles, vector)


def diagonal(rows):
    shape = (rows, LANES)
    return lax.broadcasted_iota(jnp.int32, shape, 0) == lax.broadcasted_iota(jnp.int32, shape, 1)


def as_row(column):
    return jnp.sum(jnp.where(diagonal(column.shape[0]), column, 0.0), 0, keepdims=True)


def total_sum(x):
    return jnp.sum(jnp.sum(x, 0, keepdims=True), 1, keepdims=True)


def basis_products(piece, basis_ref, extra_pieces):
    kept = basis_ref.shape[0]
    total = jnp.zeros((kept, LANES), jnp.float32)
    for k in range(piece.shape[0]):
        total = total + basis_ref[:, k * LANES : (k + 1) * LANES] * piece[k : k + 1, :]
    row = as_row(jnp.sum(total, 1, keepdims=True))
    lane = lax.broadcasted_iota(jnp.int32, (1, LANES), 1)
    for e, extra in enumerate(extra_pieces):
        row = row + jnp.where(lane == kept + e, total_sum(extra * piece), 0.0)
    return row + jnp.where(lane == LANES - 1, total_sum(piece * piece), 0.0)


def first_grams(u_basis, right_basis, start_share, after, total_left, total_right):
    kept = u_basis.shape[0]
    contract = (((1,), (1,)), ((), ()))

    def kernel(u_ref, v_ref, start_ref, after_ref, grams_ref, row_ref):
        for at, ref, total in ((0, u_ref, total_left), (kept, v_ref, total_right)):
            basis = ref[...]
            gram = lax.dot_general(
                basis, basis, contract, precision=HIGHEST, preferred_element_type=jnp.float32
            )
            grams_ref[:, at : at + kept] = gram * (1.0 / total)
        start = start_ref[...]
        row_ref[...] = basis_products(start, v_ref, [start])

    return call(
        kernel, [(kept, 2 * kept), (1, LANES)], [u_basis, right_basis, start_share, after]
    )


def first_products(mine, chunks, arrived, basis, start_row, gram_rows, copies):
    rows = chunks.shape[1]
    lines = 2 + gram_rows.shape[0]

    def kernel(mine_ref, chunks_ref, *refs):
        arrived_refs = refs[: len(arrived)]
        basis_ref, start_ref, gram_ref, piece_ref, sent_ref = refs[len(arrived) :]
        piece = chunks_ref[mine_ref[0]]
        for ref in arrived_refs:
            piece = piece + ref[0]
        piece_ref[...] = piece
        row = basis_products(piece, basis_ref, [])
        sent = jnp.concatenate([row, start_ref[...], gram_ref[...]], 0)
        sent_ref[...] = jnp.broadcast_to(sent[None], sent_ref.shape)

    args = [mine, chunks, *arrived, basis, start_row, gram_rows]
    return call(
        kernel,
        [(rows, LANES), (copies, lines, LANES)],
        args,
        [SMEM] + [VMEM] * (len(args) - 1),
    )


def inner_products(received, basis, extras, copies):
    rows = received.shape[1]

    def kernel(received_ref, basis_ref, *refs):
        extra_refs, piece_ref, row_ref = refs[: len(extras)], refs[-2], refs[-1]
        piece = jnp.sum(received_ref[...], 0)
        piece_ref[...] = piece
        row = basis_products(piece, basis_ref, [ref[...] for ref in extra_refs])
        row_ref[...] = jnp.broadcast_to(row, row_ref.shape)

    return call(kernel, [(rows, LANES), (copies, LANES)], [received, basis, *extras])


def coefficients(sums, products, size):
    lane = lax.broadcasted_iota(jnp.int32, (1, LANES), 1)
    coeffs = jnp.where(lane < size, sums, 0.0)
    squares = jnp.sum(jnp.where(lane == LANES - 1, sums, 0.0), 1, keepdims=True)
    eye = diagonal(products.shape[0])
    coeffs_col = jnp.sum(jnp.where(eye, coeffs, 0.0), 1, keepdims=True)
    combined = 2.0 * coeffs_col - jnp.sum(products * coeffs, 1, keepdims=True)
    gram_comb = jnp.sum(products * as_row(combined), 1, keepdims=True)
    squared = squares + jnp.sum(combined * (gram_comb - 2.0 * coeffs_col), 0, keepdims=True)
    squared = jnp.maximum(squared, 0.0)
    return combined, coeffs_col - gram_comb, squared, jnp.sqrt(squared + EPSILON)


def unit_lines(piece, combined, basis_ref, extra_pieces, inverse):
    kept = basis_ref.shape[0]
    spread = jnp.broadcast_to(combined[:kept], (kept, LANES))
    for e, extra in enumerate(extra_pieces):
        piece = piece - combined[kept + e : kept + e + 1] * extra
    for k in range(piece.shape[0]):
        part = jnp.sum(spread * basis_ref[:, k * LANES : (k + 1) * LANES], 0, keepdims=True)
        yield k, (piece[k : k + 1, :] - part) * inverse


def wider_gram(products, size, remaining, squared, inverse):
    shape = products.shape
    remaining = remaining * inverse
    sub_at = lax.broadcasted_iota(jnp.int32, shape, 0)
    lane_at = lax.broadcasted_iota(jnp.int32, shape, 1)
    wider = jnp.where((lane_at == size) & (sub_at < size), remaining, products)
    wider = jnp.where((sub_at == size) & (lane_at < size), as_row(remaining), wider)
    return jnp.where((sub_at == size) & (lane_at == size), squared * inverse * inverse, wider)


def first_vector(received, whole, piece, basis, total, total_right, copies):
    kept = basis.shape[0]
    rows = piece.shape[0]
    padded = kept + GROUP

    def kernel(received_ref, whole_ref, piece_ref, basis_ref, *outs):
        copies_ref, unit_ref, gram_ref, right_gram_ref, scale_ref = outs
        lines = jnp.sum(received_ref[...], 0)
        lane_at = lax.broadcasted_iota(jnp.int32, (padded, LANES), 1)
        sub_at = lax.broadcasted_iota(jnp.int32, (padded, LANES), 0)
        grams = jnp.concatenate([whole_ref[...], jnp.zeros((GROUP, LANES), jnp.float32)], 0)
        products = jnp.where(lane_at < kept, grams, 0.0)
        combined, remaining, squared, scale = coefficients(lines[0:1] * (1.0 / total), products, kept)
        inverse = 1.0 / scale
        for k, line in unit_lines(piece_ref[...], combined, basis_ref, [], inverse):
            unit_ref[pl.ds(k, 1), :] = line
            for copy in range(copies):
                copies_ref[copy, pl.ds(k, 1), :] = line
        gram_ref[...] = wider_gram(products, kept, remaining, squared, inverse)
        start_row = lines[1:2] * (1.0 / total_right)
        start_row = jnp.where(lax.broadcasted_iota(jnp.int32, (1, LANES), 1) <= kept, start_row, 0.0)
        start_row = jnp.broadcast_to(start_row, (padded, LANES))
        start_col = jnp.sum(jnp.where(lane_at == sub_at, start_row, 0.0), 1, keepdims=True)
        right = jnp.where(lane_at < kept, pltpu.roll(grams, LANES - kept, 1), 0.0)
        right = jnp.where(lane_at == kept, start_col, right)
        right_gram_ref[...] = jnp.where(sub_at == kept, start_row, right)
        scale_ref[...] = jnp.broadcast_to(scale, scale_ref.shape)

    outs = [(copies, rows, LANES), (rows, LANES), (padded, LANES), (padded, LANES), (1, LANES)]
    return call(kernel, outs, [received, whole, piece, basis])


def new_vector(received, gram, piece, basis, extras, total, copies):
    kept = basis.shape[0]
    rows = piece.shape[0]
    size = kept + len(extras)

    def kernel(received_ref, gram_ref, piece_ref, basis_ref, *refs):
        extra_refs = refs[: len(extras)]
        copies_ref, unit_ref, gram_out_ref, scale_ref = refs[len(extras) :]
        sums = jnp.sum(received_ref[...], 0, keepdims=True) * (1.0 / total)
        products = gram_ref[...]
        combined, remaining, squared, scale = coefficients(sums, products, size)
        inverse = 1.0 / scale
        extra_pieces = [ref[...] for ref in extra_refs]
        for k, line in unit_lines(piece_ref[...], combined, basis_ref, extra_pieces, inverse):
            unit_ref[pl.ds(k, 1), :] = line
            for copy in range(copies):
                copies_ref[copy, pl.ds(k, 1), :] = line
        gram_out_ref[...] = wider_gram(products, size, remaining, squared, inverse)
        scale_ref[...] = jnp.broadcast_to(scale, scale_ref.shape)

    outs = [(copies, rows, LANES), (rows, LANES), gram.shape, (1, LANES)]
    return call(kernel, outs, [received, gram, piece, basis, *extras])


def last_vector(received, gram, piece, basis, extras, total, lefts, rights, scales):
    kept = basis.shape[0]
    rows = piece.shape[0]
    left_rows = lefts[0].shape[0]
    size = kept + len(extras)
    steps = len(lefts)

    def kernel(received_ref, gram_ref, piece_ref, basis_ref, *refs):
        refs = list(refs)
        groups = []
        for members in (extras, lefts, rights, scales):
            groups.append(refs[: len(members)])
            refs = refs[len(members) :]
        extra_refs, left_refs, right_refs, scale_refs = groups
        left_out, right_out, scales_out = refs
        sums = jnp.sum(received_ref[...], 0, keepdims=True) * (1.0 / total)
        combined, _, _, scale = coefficients(sums, gram_ref[...], size)
        extra_pieces = [ref[...] for ref in extra_refs]
        for k, line in unit_lines(piece_ref[...], combined, basis_ref, extra_pieces, 1.0 / scale):
            right_out[steps - 1, :, k * LANES : (k + 1) * LANES] = line
        for step, ref in enumerate(right_refs):
            for k in range(rows):
                right_out[step, :, k * LANES : (k + 1) * LANES] = ref[k : k + 1, :]
        for step, ref in enumerate(left_refs):
            for k in range(left_rows):
                left_out[step : step + 1, k * LANES : (k + 1) * LANES] = ref[k : k + 1, :]
        values = [ref[:, 0:1] for ref in scale_refs] + [scale]
        sub_at = lax.broadcasted_iota(jnp.int32, (2, steps), 0)
        lane_at = lax.broadcasted_iota(jnp.int32, (2, steps), 1)
        table = jnp.zeros((2, steps), jnp.float32)
        for at, value in enumerate(values):
            table = jnp.where((sub_at == at % 2) & (lane_at == at // 2), value, table)
        scales_out[...] = table

    outs = [(steps, left_rows * LANES), (steps, 1, rows * LANES), (2, steps)]
    return call(kernel, outs, [received, gram, piece, basis, *extras, *lefts, *rights, *scales])


def shards(tiles, tile_index, u_basis, v_basis, v_start):
    blocks = tiles[0]
    slots = tile_index[0]
    width = blocks.shape[1]
    cols_len = v_start.shape[0]
    col_blocks = cols_len // width
    row_count = lax.axis_size("row")
    col_count = lax.axis_size("col")
    devices = row_count * col_count
    kept = u_basis.shape[0]
    left_piece = u_basis.shape[1]
    right_piece = v_basis.shape[2]
    rows_len = left_piece * col_count
    row_blocks = rows_len // width
    left_rows = left_piece // width
    right_rows = right_piece // width
    total_left = rows_len * row_count
    total_right = cols_len * col_count

    whole_start = v_start.reshape(col_blocks, width)
    dense = multiply_tiles(blocks, slots, whole_start, col_blocks, row_blocks, True)
    chunks = dense.reshape(col_count, left_rows, width)
    mine = lax.axis_index("col")
    arrived = []
    for shift in range(1, col_count):
        pairs = [(i, (i + shift) % col_count) for i in range(col_count)]
        chunk = lax.dynamic_index_in_dim(chunks, (mine + shift) % col_count, 0, True)
        arrived.append(lax.ppermute(chunk, "col", pairs))

    right_basis = v_basis[:, 0, :]
    start_share = lax.dynamic_slice_in_dim(
        whole_start, lax.axis_index("row") * right_rows, right_rows, 0
    )
    grams, start_row = first_grams(
        u_basis, right_basis, start_share, dense, total_left, total_right
    )
    chunk = grams.size // devices
    chunk_rows = -(-chunk // LANES)
    gram_rows = jnp.sum(swap(grams.reshape(devices, chunk), BOTH), 0)
    gram_rows = jnp.pad(gram_rows, (0, chunk_rows * LANES - chunk)).reshape(chunk_rows, LANES)

    lefts, rights, scales = ([], [], [])
    right_extras = [start_share]
    received = None
    for iteration in range(ITERS):
        if iteration == 0:
            piece, sent = first_products(
                mine.reshape(1), chunks, arrived, u_basis, start_row, gram_rows, devices
            )
            everything = swap(sent, BOTH)
            whole = everything[:, 2:, :].reshape(devices, chunk_rows * LANES)[:, :chunk]
            copies, left_unit, left_gram, right_gram, alpha = first_vector(
                everything, whole.reshape(grams.shape), piece, u_basis, total_left, total_right, col_count
            )
        else:
            piece, row = inner_products(received, u_basis, lefts, devices)
            summed_rows = swap(row.reshape(devices, 1, LANES), BOTH).reshape(devices, LANES)
            copies, left_unit, left_gram, alpha = new_vector(
                summed_rows, left_gram, piece, u_basis, lefts, total_left, col_count
            )
        lefts = lefts + [left_unit]
        scales = scales + [alpha]
        joined = swap(copies, "col").reshape(row_blocks, width)
        dense = multiply_tiles(blocks, slots, joined, row_blocks, col_blocks, False)
        received = swap(dense.reshape(row_count, right_rows, width), "row")
        piece, row = inner_products(received, right_basis, right_extras, devices)
        summed_rows = swap(row.reshape(devices, 1, LANES), BOTH).reshape(devices, LANES)
        if iteration + 1 < ITERS:
            copies, right_unit, right_gram, beta = new_vector(
                summed_rows, right_gram, piece, right_basis, right_extras, total_right, row_count
            )
            rights = rights + [right_unit]
            right_extras = right_extras + [right_unit]
            scales = scales + [beta]
            joined = swap(copies, "row").reshape(col_blocks, width)
            dense = multiply_tiles(blocks, slots, joined, col_blocks, row_blocks, True)
            received = swap(dense.reshape(col_count, left_rows, width), "col")
    return last_vector(
        summed_rows, right_gram, piece, right_basis, right_extras, total_right, lefts, rights, scales
    )


def solution(mesh):
    placed = (
        P("row", "col", None, None),
        P("row", "col"),
        P(None, ("row", "col")),
        P(None, "col", "row"),
        P("col"),
    )
    return jax.shard_map(
        shards,
        mesh=mesh,
        in_specs=placed,
        out_specs=(P(None, ("row", "col")), P(None, "col", "row"), P()),
        check_vma=False,
    )
```

time: 126 us -> 115 us (0.913)
  blocking collectives: 24.4 us -> 83.9 us
  waiting for transfers between devices: 43.6 us -> 4.4 us
  starting transfers between devices: 33.8 us -> 12.1 us
  matrix products: 4.71 us -> 0 us
  other arithmetic: 4.2 us -> 0.05 us
  Pallas kernels: 11.1 us -> 8.77 us
  local copies, waits for them, and re-layouts: 2.81 us -> 4.58 us
    all_to_all x3 -> x10, blocking collectives: 24.4 us -> 83.9 us  [swap(): return lax.all_to_all(chunks, axis, 0, 0, tiled=True)]
    all_to_all x8 -> x1, waiting for transfers between devices: 39.9 us -> 2.57 us  [swap(): return lax.all_to_all(chunks, axis, 0, 0, tiled=True)]
    all_to_all x8 -> x1, starting transfers between devices: 29 us -> 7.33 us  [swap(): return lax.all_to_all(chunks, axis, 0, 0, tiled=True)]
    dot_general x2 -> x0, matrix products: 4.71 us -> none  [the longest x1 2.6 us: shards(): jnp.dot(u_basis, u_basis.T, precision=HIGHEST) / total_left]
    unnamed x11, local copies, waits for them, and re-layouts: 0.95 us -> 3.84 us
    another operation x6 -> x0, other arithmetic: 2.71 us -> none
    pallas_call x4, Pallas kernels: 5.74 us -> 3.71 us  [multiply_tiles(): pl.pallas_call(kernel, out_shape=jax.ShapeDtypeStruct((out_blocks, width)...]
    ppermute x3, waiting for transfers between devices: 3.64 us -> 1.83 us  [shards(): arrived.append(lax.ppermute(chunk, 'col', pairs))]
  transfers between devices with their start and end apart: 11 -> 4, of which waited for: 9 -> 3; matrix products, arithmetic and copies ran while one was open for 3% -> 0% of each run, Pallas kernels for 1% -> 0%
where the time goes in v3:
time: 115 us
  blocking collectives  83.9 us (73%)
  starting transfers between devices  12.1 us (11%)
  Pallas kernels  8.77 us (8%)
  local copies, waits for them, and re-layouts  4.58 us (4%)
  waiting for transfers between devices  4.4 us (4%)
    all_to_all x10, blocking collectives, swap(): return lax.all_to_all(chunks, axis, 0, 0, tiled=True)  83.9 us
    all_to_all x1, starting transfers between devices, swap(): return lax.all_to_all(chunks, axis, 0, 0, tiled=True)  7.33 us
    pallas_call x9, Pallas kernels, call(): pl.pallas_call(kernel, out_shape=shapes, in_specs=specs or [VMEM] * len(a...  5.06 us
    ppermute x3, starting transfers between devices, shards(): arrived.append(lax.ppermute(chunk, 'col', pairs))  4.75 us
    unnamed x11, local copies, waits for them, and re-layouts  3.84 us
    pallas_call x4, Pallas kernels, multiply_tiles(): pl.pallas_call(kernel, out_shape=jax.ShapeDtypeStruct((out_blocks, width)...  3.71 us
    all_to_all x1, waiting for transfers between devices, swap(): return lax.all_to_all(chunks, axis, 0, 0, tiled=True)  2.57 us
  transfers between devices with their start and end apart: 4, of which 3 were waited for; matrix products, arithmetic and copies ran while one was open for 0% of the time, Pallas kernels for 0%

profile of v3, /device:TPU:0, one launch (start us, length us, event | category | flops | bytes accessed | tf_op | source)
XLA Modules:
  0.0 114.5 jit_solution(3376953778668782013)
XLA Ops:
  0.6 1.3 %copy.14 = f32[64,1,2048]{2,0,1:T(8,128)S(1)} copy(f32[64,1,2048]{2,1,0:T(1,128)} %param.8) | data formatting | bytes 1048576
  1.9 0.7 constant_dynamic-slice_fusion.start_ref.refs_0_
  2.6 0.7 copy-done.4
  3.3 1.0 copy-done.1
  4.3 0.8 copy-done.3
  5.2 1.0 shard_map.76.after_ref
  6.2 2.1 %shard_map.77 = (f32[64,128]{1,0:T(8,128)}, f32[1,128]{1,0:T(1,128)S(1)}) custom-call(f32[64,4096]{1,0:T(8,128)S(1)} %copy-done, f32[64,2048]{1,0:T(8,128)S(1)} %bitcast.29, f32[16,128]{1,0:T(8,128)S(1)} %constant_dynamic-slice_fusion.start_ref.refs_0_, f32[128,128]{1,0:T(8,128)S(1)} %shard_map.76.after_ref), custom_call_target="tpu_custom_call" | custom-call | tf_op jit(solution)/shard_map/pallas_call | solution.py:27
  8.3 7.3 %all-to-all-start = ((f32[32,1,256]{2,1,0:T(1,128)}), f32[32,1,256]{2,1,0:T(1,128)S(1)}, u32[]{:S(2)}, u32[]{:S(2)}) async-start(f32[32,1,256]{2,1,0:T(1,128)} %bitcast.5), calls=%async_computation | async-start | bytes 65536 | tf_op jit(solution)/shard_map/all_to_all | solution.py:22
  15.7 3.7 %collective-permute-start.2 = (f32[1,32,128]{2,1,0:T(8,128)S(1)}, f32[1,32,128]{2,1,0:T(8,128)S(1)}, u32[]{:S(2)}, u32[]{:S(2)}) collective-permute-start(f32[1,32,128]{2,1,0:T(8,128)S(1)} %get-tuple-element.47), channel_id=1, source_target_pairs={{0,3},{1,0},{2,1},{3,2},{4,7},{5,4},{6,5},{7,6},{8,11},{9,8},{10,9... | collective-permute-start | bytes 49160 | tf_op jit(solution)/shard_map/ppermute | solution.py:320
  19.4 1.1 collective-permute-start
  20.4 2.6 %all-to-all-done = f32[32,1,256]{2,1,0:T(1,128)S(1)} async-done(((f32[32,1,256]{2,1,0:T(1,128)}), f32[32,1,256]{2,1,0:T(1,128)S(1)}, u32[]{:S(2)}, u32[]{:S(2)}) %all-to-all-start) | async-done | bytes 32800 | tf_op jit(solution)/shard_map/all_to_all | solution.py:22
  23.1 0.9 collective-permute-done.1.refs_1_
  24.0 0.9 collective-permute-done.refs_0_
  24.9 0.2 shard_map.78
  25.1 10.6 %all_to_all.59.received_ref = f32[32,4,128]{2,1,0:T(4,128)S(1)} all-to-all(f32[32,4,128]{2,1,0:T(4,128)S(1)} %get-tuple-element.27), channel_id=1, replica_groups=mesh['row'=8,'col'=4] {'row','col'}, dimensions={0} | all-to-all | bytes 131072 | tf_op jit(solution)/shard_map/all_to_all | solution.py:22
  35.8 0.3 shard_map.79
  36.1 8.1 %all_to_all.60 = f32[4,32,128]{2,1,0:T(8,128)S(1)} all-to-all(f32[4,32,128]{2,1,0:T(8,128)S(1)} %get-tuple-element.29), channel_id=1, replica_groups=mesh['row'=8,'col'=4] {'col'}, dimensions={0} | all-to-all | bytes 131072 | tf_op jit(solution)/shard_map/all_to_all | solution.py:22
  44.2 0.9 shard_map.80
  45.1 7.4 %all_to_all.61.received_ref = f32[8,16,128]{2,1,0:T(8,128)S(1)} all-to-all(f32[8,16,128]{2,1,0:T(8,128)S(1)} %bitcast.41), channel_id=1, replica_groups=mesh['row'=8,'col'=4] {'row'}, dimensions={0} | all-to-all | bytes 131072 | tf_op jit(solution)/shard_map/all_to_all | solution.py:22
  52.6 8.9 %all_to_all.62 = f32[32,1,128]{2,1,0:T(1,128)S(1)} all-to-all(f32[32,1,128]{2,1,0:T(1,128)S(1)} %bitcast.52), channel_id=1, replica_groups=mesh['row'=8,'col'=4] {'row','col'}, dimensions={0} | all-to-all | bytes 32768 | tf_op jit(solution)/shard_map/all_to_all | solution.py:22
  61.5 0.3 shard_map.82
  61.8 7.4 %all_to_all.63 = f32[8,16,128]{2,1,0:T(8,128)S(1)} all-to-all(f32[8,16,128]{2,1,0:T(8,128)S(1)} %get-tuple-element.33), channel_id=1, replica_groups=mesh['row'=8,'col'=4] {'row'}, dimensions={0} | all-to-all | bytes 131072 | tf_op jit(solution)/shard_map/all_to_all | solution.py:22
  69.2 1.0 shard_map.83
  70.2 8.1 %all_to_all.64.received_ref = f32[4,32,128]{2,1,0:T(8,128)S(1)} all-to-all(f32[4,32,128]{2,1,0:T(8,128)S(1)} %bitcast.43), channel_id=1, replica_groups=mesh['row'=8,'col'=4] {'col'}, dimensions={0} | all-to-all | bytes 131072 | tf_op jit(solution)/shard_map/all_to_all | solution.py:22
  78.3 0.2 shard_map.84
  78.5 8.9 %all_to_all.65 = f32[32,1,128]{2,1,0:T(1,128)S(1)} all-to-all(f32[32,1,128]{2,1,0:T(1,128)S(1)} %bitcast.53), channel_id=1, replica_groups=mesh['row'=8,'col'=4] {'row','col'}, dimensions={0} | all-to-all | bytes 32768 | tf_op jit(solution)/shard_map/all_to_all | solution.py:22
  87.4 0.9 shard_map.85
  88.3 8.1 %all_to_all.66 = f32[4,32,128]{2,1,0:T(8,128)S(1)} all-to-all(f32[4,32,128]{2,1,0:T(8,128)S(1)} %get-tuple-element.38), channel_id=1, replica_groups=mesh['row'=8,'col'=4] {'col'}, dimensions={0} | all-to-all | bytes 131072 | tf_op jit(solution)/shard_map/all_to_all | solution.py:22
  96.4 0.9 shard_map.86
  97.2 7.4 %all_to_all.67.received_ref = f32[8,16,128]{2,1,0:T(8,128)S(1)} all-to-all(f32[8,16,128]{2,1,0:T(8,128)S(1)} %bitcast.45), channel_id=1, replica_groups=mesh['row'=8,'col'=4] {'row'}, dimensions={0} | all-to-all | bytes 131072 | tf_op jit(solution)/shard_map/all_to_all | solution.py:22
  104.8 8.9 %all_to_all.68 = f32[32,1,128]{2,1,0:T(1,128)S(1)} all-to-all(f32[32,1,128]{2,1,0:T(1,128)S(1)} %bitcast.54), channel_id=1, replica_groups=mesh['row'=8,'col'=4] {'row','col'}, dimensions={0} | all-to-all | bytes 32768 | tf_op jit(solution)/shard_map/all_to_all | solution.py:22
  113.7 0.9 shard_map.88
  (14 shorter events, 0.4 us)
Async XLA Ops:
  0.6 5.5 %copy-start = (f32[64,4096]{1,0:T(8,128)S(1)}, f32[64,4096]{1,0:T(8,128)}, u32[]{:S(2)}) copy-start(f32[64,4096]{1,0:T(8,128)} %basis_ref.5) | copy-start | bytes 3145732
  2.6 0.7 copy-start.4
  3.3 1.0 copy-start.1
  4.3 0.8 copy-start.3
  8.3 14.7 %all-to-all-start = ((f32[32,1,256]{2,1,0:T(1,128)}), f32[32,1,256]{2,1,0:T(1,128)S(1)}, u32[]{:S(2)}, u32[]{:S(2)}) async-start(f32[32,1,256]{2,1,0:T(1,128)} %bitcast.5), calls=%async_computation | async-start | bytes 65536 | tf_op jit(solution)/shard_map/all_to_all | solution.py:22
  15.7 7.4 %collective-permute-start.2 = (f32[1,32,128]{2,1,0:T(8,128)S(1)}, f32[1,32,128]{2,1,0:T(8,128)S(1)}, u32[]{:S(2)}, u32[]{:S(2)}) collective-permute-start(f32[1,32,128]{2,1,0:T(8,128)S(1)} %get-tuple-element.47), channel_id=1, source_target_pairs={{0,3},{1,0},{2,1},{3,2},{4,7},{5,4},{6,5},{7,6},{8,11},{9,8},{10,9... | collective-permute-start | bytes 49160 | tf_op jit(solution)/shard_map/ppermute | solution.py:320
  19.4 4.6 %collective-permute-start.1 = (f32[1,32,128]{2,1,0:T(8,128)S(1)}, f32[1,32,128]{2,1,0:T(8,128)S(1)}, u32[]{:S(2)}, u32[]{:S(2)}) collective-permute-start(f32[1,32,128]{2,1,0:T(8,128)S(1)} %get-tuple-element.48), channel_id=1, source_target_pairs={{0,2},{1,3},{2,0},{3,1},{4,6},{5,7},{6,4},{7,5},{8,10},{9,11},{10,... | collective-permute-start | bytes 49160 | tf_op jit(solution)/shard_map/ppermute | solution.py:320
  19.4 5.5 %collective-permute-start = (f32[1,32,128]{2,1,0:T(8,128)S(1)}, f32[1,32,128]{2,1,0:T(8,128)S(1)}, u32[]{:S(2)}, u32[]{:S(2)}) collective-permute-start(f32[1,32,128]{2,1,0:T(8,128)S(1)} %get-tuple-element.49), channel_id=1, source_target_pairs={{0,1},{1,2},{2,3},{3,0},{4,5},{5,6},{6,7},{7,4},{8,9},{9,10},{10,1... | collective-permute-start | bytes 49160 | tf_op jit(solution)/shard_map/ppermute | solution.py:320
  35.7 8.4 %copy-start.2 = (bf16[1,16,128,128]{3,2,1,0:T(8,128)(2,1)S(1)}, bf16[1,16,128,128]{3,2,1,0:T(8,128)(2,1)}, u32[]{:S(2)}) copy-start(bf16[1,16,128,128]{3,2,1,0:T(8,128)(2,1)} %param.5) | copy-start | bytes 1572868

commit v4 on v3

v4 whole, which is shorter than its diff:
```python
import jax
import jax.numpy as jnp
from jax import lax
from jax.experimental import pallas as pl
from jax.experimental.pallas import tpu as pltpu
from jax.sharding import PartitionSpec as P

ITERS = 2


HIGHEST = lax.Precision.HIGHEST
EPSILON = 1e-06
BOTH = ("row", "col")
LANES = 128
GROUP = 8
PARAMS = pltpu.CompilerParams(vmem_limit_bytes=8 * 2**20)
VMEM = pl.BlockSpec(memory_space=pltpu.VMEM)
SMEM = pl.BlockSpec(memory_space=pltpu.SMEM)
ANY = pl.BlockSpec(memory_space=pl.ANY)


def swap(chunks, axis):
    return lax.all_to_all(chunks, axis, 0, 0, tiled=True)


def call(kernel, outs, args, specs=None, scratch=()):
    shapes = tuple(jax.ShapeDtypeStruct(shape, jnp.float32) for shape in outs)
    return pl.pallas_call(
        kernel,
        out_shape=shapes,
        in_specs=specs or [VMEM] * len(args),
        out_specs=tuple([VMEM] * len(outs)),
        scratch_shapes=list(scratch),
        compiler_params=PARAMS,
    )(*args)


def take(refs, *counts):
    refs = list(refs)
    groups = []
    for count in counts:
        groups.append(refs[:count])
        refs = refs[count:]
    return groups + [refs]


def exchange(messages, axis):
    count = lax.axis_size(axis)
    arrived = [messages[0]]
    for x in range(1, count):
        arrived.append(lax.ppermute(messages[x], axis, [(i, i ^ x) for i in range(count)]))
    return arrived


def three_parts(x):
    high = x.astype(jnp.bfloat16)
    rest = x - high.astype(jnp.float32)
    middle = rest.astype(jnp.bfloat16)
    low = (rest - middle.astype(jnp.float32)).astype(jnp.bfloat16)
    return jnp.concatenate([high, middle, low], 0)


def diagonal(rows):
    shape = (rows, LANES)
    return lax.broadcasted_iota(jnp.int32, shape, 0) == lax.broadcasted_iota(jnp.int32, shape, 1)


def as_row(column):
    return jnp.sum(jnp.where(diagonal(column.shape[0]), column, 0.0), 0, keepdims=True)


def total_sum(x):
    return jnp.sum(jnp.sum(x, 0, keepdims=True), 1, keepdims=True)


def tile_sums(slots_ref, tiles_ref, vector_ref, dense_ref, picked_ref, product_ref, divisor, is_forward):
    count = tiles_ref.shape[0]
    limit = vector_ref.shape[0] * dense_ref.shape[0]
    contract = (((1,), (1,)), ((), ())) if is_forward else (((1,), (0,)), ((), ()))
    targets = []
    for t in range(count):
        slot = slots_ref[t]
        live = slot < limit
        slot = jnp.where(live, slot, 0)
        row = lax.div(slot, divisor)
        column = slot - row * divisor
        targets.append(row if is_forward else column)
        line = vector_ref[pl.ds(column if is_forward else row, 1), :]
        picked_ref[pl.ds(t, 1), :] = jnp.where(live, line, 0.0)
    parts = three_parts(picked_ref[...])
    dense_ref[...] = jnp.zeros_like(dense_ref)
    for t in range(count):
        result = lax.dot_general(parts, tiles_ref[t], contract, preferred_element_type=jnp.float32)
        product_ref[pl.ds(t, 1), :] = (
            result[t : t + 1]
            + result[count + t : count + t + 1]
            + result[2 * count + t : 2 * count + t + 1]
        )
    for t in range(count):
        line = pl.ds(targets[t], 1)
        dense_ref[line, :] = dense_ref[line, :] + product_ref[pl.ds(t, 1), :]


def packed_gram(basis, total):
    gram = lax.dot_general(
        basis,
        basis,
        (((1,), (1,)), ((), ())),
        precision=HIGHEST,
        preferred_element_type=jnp.float32,
    )
    half = gram.shape[0] // 2
    return gram[:half] * (1.0 / total), gram[half:] * (1.0 / total)


def unpacked_gram(packed, padded):
    half = packed.shape[0]
    grams = jnp.concatenate(
        [
            packed,
            pltpu.roll(packed, LANES // 2, 1),
            jnp.zeros((padded - 2 * half, LANES), jnp.float32),
        ],
        0,
    )
    lane_at = lax.broadcasted_iota(jnp.int32, grams.shape, 1)
    return jnp.where(lane_at < 2 * half, grams, 0.0)


def start(mine, tiles, slots, vector, basis, row_blocks, total, peers):
    count, width = tiles.shape[0], tiles.shape[1]
    divisor = vector.shape[0]
    kept = basis.shape[0]
    rows = row_blocks // peers
    share = kept * kept // LANES // peers

    def kernel(mine_ref, slots_ref, tiles_hbm, vector_hbm, basis_hbm, *refs):
        outs, scratch = take(refs, peers)
        tiles_ref, vector_ref, basis_ref, dense_ref, packed_ref, picked_ref, product_ref, sems = scratch
        moves = [
            pltpu.make_async_copy(source, target, sems.at[at])
            for at, (source, target) in enumerate(
                ((vector_hbm, vector_ref), (tiles_hbm, tiles_ref), (basis_hbm, basis_ref))
            )
        ]
        for move in moves:
            move.start()
        moves[0].wait()
        moves[1].wait()
        tile_sums(slots_ref, tiles_ref, vector_ref, dense_ref, picked_ref, product_ref, divisor, True)
        moves[2].wait()
        upper, lower = packed_gram(basis_ref[...], total)
        packed_ref[:, :kept] = upper
        packed_ref[:, kept:] = lower
        for x, out in enumerate(outs):
            peer = jnp.bitwise_xor(mine_ref[0], x)
            out[:rows, :] = dense_ref[pl.ds(peer * rows, rows), :]
            out[rows:, :] = packed_ref[pl.ds(peer * share, share), :]

    scratch = [
        pltpu.VMEM(tiles.shape, tiles.dtype),
        pltpu.VMEM(vector.shape, jnp.float32),
        pltpu.VMEM(basis.shape, jnp.float32),
        pltpu.VMEM((row_blocks, width), jnp.float32),
        pltpu.VMEM((kept // 2, 2 * kept), jnp.float32),
        pltpu.VMEM((count, width), jnp.float32),
        pltpu.VMEM((count, width), jnp.float32),
        pltpu.SemaphoreType.DMA((3,)),
    ]
    return call(
        kernel,
        [(rows + share, width)] * peers,
        [mine, slots, tiles, vector, basis],
        [SMEM, SMEM, ANY, ANY, ANY],
        scratch,
    )


def right_start(mine_row, v_basis, vector, after, total):
    kept, _, length = v_basis.shape
    rows = length // LANES

    def kernel(mine_ref, basis_ref, vector_ref, after_ref, flat_ref, piece_ref, row_ref, packed_ref):
        for k in range(rows):
            at = slice(k * LANES, (k + 1) * LANES)
            flat_ref[:, at] = basis_ref[:, 0, at]
        piece = vector_ref[pl.ds(mine_ref[0] * rows, rows), :]
        piece_ref[...] = piece
        row_ref[...] = basis_products(piece, flat_ref, [piece])
        upper, lower = packed_gram(flat_ref[...], total)
        packed_ref[:, :kept] = upper
        packed_ref[:, kept:] = lower

    return call(
        kernel,
        [(kept, length), (rows, LANES), (1, LANES), (kept // 2, 2 * kept)],
        [mine_row, v_basis, vector, after],
        [SMEM, VMEM, VMEM, VMEM],
    )


def forward_messages(mine, tiles, slots, vector, row_blocks, peers):
    count, width = tiles.shape[0], tiles.shape[1]
    divisor = vector.shape[0]
    rows = row_blocks // peers

    def kernel(mine_ref, slots_ref, tiles_ref, vector_ref, *refs):
        outs, (dense_ref, picked_ref, product_ref) = take(refs, peers)
        tile_sums(slots_ref, tiles_ref, vector_ref, dense_ref, picked_ref, product_ref, divisor, True)
        for x, out in enumerate(outs):
            peer = jnp.bitwise_xor(mine_ref[0], x)
            out[...] = dense_ref[pl.ds(peer * rows, rows), :]

    scratch = [pltpu.VMEM((row_blocks, width), jnp.float32)]
    scratch += [pltpu.VMEM((count, width), jnp.float32)] * 2
    return call(
        kernel,
        [(rows, width)] * peers,
        [mine, slots, tiles, vector],
        [SMEM, SMEM, VMEM, VMEM],
        scratch,
    )


def backward_product(mine, tiles, slots, messages, rows, col_blocks):
    count, width = tiles.shape[0], tiles.shape[1]
    peers = len(messages)
    share = messages[0].shape[0] - rows

    def kernel(mine_ref, slots_ref, tiles_ref, *refs):
        sources, rest = take(refs, peers)
        outs, (vector_ref, picked_ref, product_ref) = take(rest, 2 if share else 1)
        for x, source in enumerate(sources):
            peer = jnp.bitwise_xor(mine_ref[0], x)
            vector_ref[pl.ds(peer * rows, rows), :] = source[:rows, :]
        tile_sums(
            slots_ref, tiles_ref, vector_ref, outs[0], picked_ref, product_ref, col_blocks, False
        )
        if share:
            added = sources[0][rows:, :]
            for source in sources[1:]:
                added = added + source[rows:, :]
            outs[1][...] = added

    scratch = [pltpu.VMEM((rows * peers, width), jnp.float32)]
    scratch += [pltpu.VMEM((count, width), jnp.float32)] * 2
    outs = [(col_blocks, width)] + ([(share, width)] if share else [])
    return call(
        kernel,
        outs,
        [mine, slots, tiles, *messages],
        [SMEM, SMEM] + [VMEM] * (1 + peers),
        scratch,
    )


def basis_products(piece, basis_ref, extra_pieces):
    kept = basis_ref.shape[0]
    total = jnp.zeros((kept, LANES), jnp.float32)
    for k in range(piece.shape[0]):
        total = total + basis_ref[:, k * LANES : (k + 1) * LANES] * piece[k : k + 1, :]
    row = as_row(jnp.sum(total, 1, keepdims=True))
    lane = lax.broadcasted_iota(jnp.int32, (1, LANES), 1)
    for e, extra in enumerate(extra_pieces):
        row = row + jnp.where(lane == kept + e, total_sum(extra * piece), 0.0)
    return row + jnp.where(lane == LANES - 1, total_sum(piece * piece), 0.0)


def inner_products(pieces, rows, basis, extras, riders, copies):
    listed = pieces if isinstance(pieces, (list, tuple)) else [pieces]
    stacked = listed is not pieces
    further = 0 if stacked else listed[0].shape[0] - rows
    lines = 1 + further + sum(rider.shape[0] for rider in riders)

    def kernel(*refs):
        sources, (basis_ref,), extra_refs, rider_refs, (piece_ref, sent_ref) = take(
            refs, len(listed), 1, len(extras), len(riders)
        )
        if stacked:
            summed = jnp.sum(sources[0][...], 0)
        else:
            summed = sources[0][...]
            for source in sources[1:]:
                summed = summed + source[...]
        piece = summed[:rows]
        piece_ref[...] = piece
        sent = [basis_products(piece, basis_ref, [ref[...] for ref in extra_refs])]
        sent += [summed[rows + k : rows + k + 1] for k in range(further)]
        for ref in rider_refs:
            sent += [ref[k : k + 1, :] for k in range(ref.shape[0])]
        for at, line in enumerate(sent):
            shape = (copies, 1, LANES)
            sent_ref[:, :, at * LANES : (at + 1) * LANES] = jnp.broadcast_to(line[None], shape)

    return call(
        kernel,
        [(rows, LANES), (copies, 1, lines * LANES)],
        [*listed, basis, *extras, *riders],
    )


def received_row(received_ref, at):
    lines = received_ref[:, 0, at * LANES : (at + 1) * LANES]
    return jnp.sum(lines, 0, keepdims=True)


def received_gram(received_ref, first, packed_ref, peers):
    share = packed_ref.shape[0] // peers
    devices = received_ref.shape[0]
    for k in range(share):
        at = slice((first + k) * LANES, (first + k + 1) * LANES)
        added = received_ref[0:peers, 0, at]
        for i in range(1, devices // peers):
            added = added + received_ref[i * peers : (i + 1) * peers, 0, at]
        for peer in range(peers):
            packed_ref[peer * share + k : peer * share + k + 1, :] = added[peer : peer + 1]


def first_vector(mine, received, piece, basis, right_packed, total, peers):
    kept = basis.shape[0]
    rows = piece.shape[0]
    padded = kept + GROUP
    share = right_packed.shape[0] // peers

    def kernel(mine_ref, received_ref, piece_ref, basis_ref, right_ref, *refs):
        messages, (unit_ref, gram_ref, scale_ref, packed_ref) = take(refs, peers)
        received_gram(received_ref, 1, packed_ref, peers)
        products = unpacked_gram(packed_ref[...], padded)
        sums = received_row(received_ref, 0) * (1.0 / total)
        combined, remaining, squared, scale = coefficients(sums, products, kept)
        inverse = 1.0 / scale
        for k, line in unit_lines(piece_ref[...], combined, basis_ref, [], inverse):
            unit_ref[pl.ds(k, 1), :] = line
            for message in messages:
                message[pl.ds(k, 1), :] = line
        for x, message in enumerate(messages):
            peer = jnp.bitwise_xor(mine_ref[0], x)
            message[rows:, :] = right_ref[pl.ds(peer * share, share), :]
        gram_ref[...] = wider_gram(products, kept, remaining, squared, inverse)
        scale_ref[...] = jnp.broadcast_to(scale, scale_ref.shape)

    outs = [(rows + share, LANES)] * peers + [(rows, LANES), (padded, LANES), (1, LANES)]
    return call(
        kernel,
        outs,
        [mine, received, piece, basis, right_packed],
        [SMEM] + [VMEM] * 4,
        [pltpu.VMEM(right_packed.shape, jnp.float32)],
    )


def new_vector(received, gram, piece, basis, extras, total, copies, peers, widen):
    kept = basis.shape[0]
    rows = piece.shape[0]
    size = kept + len(extras)
    padded = kept + GROUP
    grams = [] if gram is None else [gram]

    def kernel(received_ref, piece_ref, basis_ref, *refs):
        gram_refs, extra_refs, rest = take(refs, len(grams), len(extras))
        copies_refs, (unit_ref, scale_ref), wider_refs, scratch = take(
            rest, 1 if copies else 0, 2, 1 if widen else 0
        )
        if gram_refs:
            products = gram_refs[0][...]
        else:
            received_gram(received_ref, 2, scratch[0], peers)
            products = unpacked_gram(scratch[0][...], padded)
            lane_at = lax.broadcasted_iota(jnp.int32, (padded, LANES), 1)
            sub_at = lax.broadcasted_iota(jnp.int32, (padded, LANES), 0)
            row = received_row(received_ref, 1) * (1.0 / total)
            row = jnp.broadcast_to(row, (padded, LANES))
            column = jnp.sum(jnp.where(lane_at == sub_at, row, 0.0), 1, keepdims=True)
            products = jnp.where((lane_at == kept) & (sub_at <= kept), column, products)
            products = jnp.where((sub_at == kept) & (lane_at <= kept), row, products)
        sums = received_row(received_ref, 0) * (1.0 / total)
        combined, remaining, squared, scale = coefficients(sums, products, size)
        inverse = 1.0 / scale
        extra_pieces = [ref[...] for ref in extra_refs]
        for k, line in unit_lines(piece_ref[...], combined, basis_ref, extra_pieces, inverse):
            unit_ref[pl.ds(k, 1), :] = line
            for ref in copies_refs:
                for copy in range(copies):
                    ref[copy, pl.ds(k, 1), :] = line
        for ref in wider_refs:
            ref[...] = wider_gram(products, size, remaining, squared, inverse)
        scale_ref[...] = jnp.broadcast_to(scale, scale_ref.shape)

    outs = [(copies, rows, LANES)] if copies else []
    outs += [(rows, LANES), (1, LANES)] + ([(padded, LANES)] if widen else [])
    scratch = [] if grams else [pltpu.VMEM((kept // 2, LANES), jnp.float32)]
    return call(kernel, outs, [received, piece, basis, *grams, *extras], None, scratch)


def coefficients(sums, products, size):
    lane = lax.broadcasted_iota(jnp.int32, (1, LANES), 1)
    coeffs = jnp.where(lane < size, sums, 0.0)
    squares = jnp.sum(jnp.where(lane == LANES - 1, sums, 0.0), 1, keepdims=True)
    eye = diagonal(products.shape[0])
    coeffs_col = jnp.sum(jnp.where(eye, coeffs, 0.0), 1, keepdims=True)
    combined = 2.0 * coeffs_col - jnp.sum(products * coeffs, 1, keepdims=True)
    gram_comb = jnp.sum(products * as_row(combined), 1, keepdims=True)
    squared = squares + jnp.sum(combined * (gram_comb - 2.0 * coeffs_col), 0, keepdims=True)
    squared = jnp.maximum(squared, 0.0)
    return combined, coeffs_col - gram_comb, squared, jnp.sqrt(squared + EPSILON)


def unit_lines(piece, combined, basis_ref, extra_pieces, inverse):
    kept = basis_ref.shape[0]
    spread = jnp.broadcast_to(combined[:kept], (kept, LANES))
    for e, extra in enumerate(extra_pieces):
        piece = piece - combined[kept + e : kept + e + 1] * extra
    for k in range(piece.shape[0]):
        part = jnp.sum(spread * basis_ref[:, k * LANES : (k + 1) * LANES], 0, keepdims=True)
        yield k, (piece[k : k + 1, :] - part) * inverse


def wider_gram(products, size, remaining, squared, inverse):
    shape = products.shape
    remaining = remaining * inverse
    sub_at = lax.broadcasted_iota(jnp.int32, shape, 0)
    lane_at = lax.broadcasted_iota(jnp.int32, shape, 1)
    wider = jnp.where((lane_at == size) & (sub_at < size), remaining, products)
    wider = jnp.where((sub_at == size) & (lane_at < size), as_row(remaining), wider)
    return jnp.where((sub_at == size) & (lane_at == size), squared * inverse * inverse, wider)


def last_vector(received, gram, piece, basis, extras, total, lefts, rights, scales):
    kept = basis.shape[0]
    rows = piece.shape[0]
    left_rows = lefts[0].shape[0]
    size = kept + len(extras)
    steps = len(lefts)

    def kernel(received_ref, gram_ref, piece_ref, basis_ref, *refs):
        extra_refs, left_refs, right_refs, scale_refs, outs = take(
            refs, len(extras), len(lefts), len(rights), len(scales)
        )
        left_out, right_out, scales_out = outs
        sums = received_row(received_ref, 0) * (1.0 / total)
        combined, _, _, scale = coefficients(sums, gram_ref[...], size)
        extra_pieces = [ref[...] for ref in extra_refs]
        for k, line in unit_lines(piece_ref[...], combined, basis_ref, extra_pieces, 1.0 / scale):
            right_out[steps - 1, :, k * LANES : (k + 1) * LANES] = line
        for step, ref in enumerate(right_refs):
            for k in range(rows):
                right_out[step, :, k * LANES : (k + 1) * LANES] = ref[k : k + 1, :]
        for step, ref in enumerate(left_refs):
            for k in range(left_rows):
                left_out[step : step + 1, k * LANES : (k + 1) * LANES] = ref[k : k + 1, :]
        values = [ref[:, 0:1] for ref in scale_refs] + [scale]
        sub_at = lax.broadcasted_iota(jnp.int32, (2, steps), 0)
        lane_at = lax.broadcasted_iota(jnp.int32, (2, steps), 1)
        table = jnp.zeros((2, steps), jnp.float32)
        for at, value in enumerate(values):
            table = jnp.where((sub_at == at % 2) & (lane_at == at // 2), value, table)
        scales_out[...] = table

    outs = [(steps, left_rows * LANES), (steps, 1, rows * LANES), (2, steps)]
    return call(kernel, outs, [received, gram, piece, basis, *extras, *lefts, *rights, *scales])


def shards(tiles, tile_index, u_basis, v_basis, v_start):
    blocks = tiles[0]
    slots = tile_index[0]
    width = blocks.shape[1]
    cols_len = v_start.shape[0]
    col_blocks = cols_len // width
    row_count = lax.axis_size("row")
    col_count = lax.axis_size("col")
    devices = row_count * col_count
    left_piece = u_basis.shape[1]
    right_piece = v_basis.shape[2]
    rows_len = left_piece * col_count
    row_blocks = rows_len // width
    left_rows = left_piece // width
    right_rows = right_piece // width
    total_left = rows_len * row_count
    total_right = cols_len * col_count
    mine = lax.axis_index("col").reshape(1)
    mine_row = lax.axis_index("row").reshape(1)

    whole_start = v_start.reshape(col_blocks, width)
    messages = start(mine, blocks, slots, whole_start, u_basis, row_blocks, total_left, col_count)
    right_basis, start_share, start_row, right_packed = right_start(
        mine_row, v_basis, whole_start, messages[0], total_right
    )
    arrived = exchange(messages, "col")

    lefts, rights, scales = ([], [], [])
    right_extras = [start_share]
    left_gram = right_gram = None
    for iteration in range(ITERS):
        last = iteration + 1 == ITERS
        piece, sent = inner_products(arrived, left_rows, u_basis, lefts, [], devices)
        summed_rows = swap(sent, BOTH)
        if iteration == 0:
            *messages, left_unit, left_gram, alpha = first_vector(
                mine, summed_rows, piece, u_basis, right_packed, total_left, col_count
            )
        else:
            left_unit, alpha, *wider = new_vector(
                summed_rows, left_gram, piece, u_basis, lefts, total_left, 0, col_count, not last
            )
            left_gram = wider[0] if wider else None
            messages = [left_unit] * col_count
        lefts = lefts + [left_unit]
        scales = scales + [alpha]
        arrived = exchange(messages, "col")
        dense, *further = backward_product(mine, blocks, slots, arrived, left_rows, col_blocks)
        received = swap(dense.reshape(row_count, right_rows, width), "row")
        riders = [start_row, *further] if iteration == 0 else []
        piece, sent = inner_products(received, right_rows, right_basis, right_extras, riders, devices)
        summed_rows = swap(sent, BOTH)
        if not last:
            copies, right_unit, beta, right_gram = new_vector(
                summed_rows,
                right_gram,
                piece,
                right_basis,
                right_extras,
                total_right,
                row_count,
                col_count,
                True,
            )
            rights = rights + [right_unit]
            right_extras = right_extras + [right_unit]
            scales = scales + [beta]
            joined = swap(copies, "row").reshape(col_blocks, width)
            messages = forward_messages(mine, blocks, slots, joined, row_blocks, col_count)
            arrived = exchange(messages, "col")
    return last_vector(
        summed_rows, right_gram, piece, right_basis, right_extras, total_right, lefts, rights, scales
    )


def solution(mesh):
    placed = (
        P("row", "col", None, None),
        P("row", "col"),
        P(None, ("row", "col")),
        P(None, "col", "row"),
        P("col"),
    )
    return jax.shard_map(
        shards,
        mesh=mesh,
        in_specs=placed,
        out_specs=(P(None, ("row", "col")), P(None, "col", "row"), P()),
        check_vma=False,
    )
```

time: 115 us -> 111 us (0.965)
  blocking collectives: 83.9 us -> 53.4 us
  waiting for transfers between devices: 4.4 us -> 21.2 us
  starting transfers between devices: 12.1 us -> 21.9 us
    all_to_all x10 -> x6, blocking collectives: 83.9 us -> 53.4 us  [swap(): return lax.all_to_all(chunks, axis, 0, 0, tiled=True)]
    ppermute x3 -> x12, starting transfers between devices: 4.75 us -> 19 us  [exchange(): lax.ppermute(messages[x], axis, [(i, i ^ x) for i in range(count)])]
    ppermute x3 -> x12, waiting for transfers between devices: 1.83 us -> 13.4 us  [exchange(): lax.ppermute(messages[x], axis, [(i, i ^ x) for i in range(count)])]
    all_to_all x1, waiting for transfers between devices: 2.57 us -> 7.88 us  [swap(): return lax.all_to_all(chunks, axis, 0, 0, tiled=True)]
    all_to_all x1, starting transfers between devices: 7.33 us -> 2.82 us  [swap(): return lax.all_to_all(chunks, axis, 0, 0, tiled=True)]
    pallas_call x9 -> x13, Pallas kernels: 5.06 us -> 9.51 us  [call(): pl.pallas_call(kernel, out_shape=shapes, in_specs=specs or [VMEM] * len(a...]
    pallas_call x4 -> x0, Pallas kernels: 3.71 us -> none  [multiply_tiles(): pl.pallas_call(kernel, out_shape=jax.ShapeDtypeStruct((out_blocks, width)...]
    unnamed x11 -> x16, local copies, waits for them, and re-layouts: 3.84 us -> 3.77 us
  transfers between devices with their start and end apart: 4 -> 13, of which waited for: 3 -> 9; matrix products, arithmetic and copies ran while one was open for 0% -> 0% of each run, Pallas kernels for 0% -> 1%
where the time goes in v4:
time: 111 us
  blocking collectives  53.4 us (48%)
  starting transfers between devices  21.9 us (20%)
  waiting for transfers between devices  21.2 us (19%)
  Pallas kernels  9.51 us (9%)
  local copies, waits for them, and re-layouts  3.77 us (3%)
    all_to_all x6, blocking collectives, swap(): return lax.all_to_all(chunks, axis, 0, 0, tiled=True)  53.4 us
    ppermute x12, starting transfers between devices, exchange(): lax.ppermute(messages[x], axis, [(i, i ^ x) for i in range(count)])  19 us
    ppermute x12, waiting for transfers between devices, exchange(): lax.ppermute(messages[x], axis, [(i, i ^ x) for i in range(count)])  13.4 us
    pallas_call x13, Pallas kernels, call(): pl.pallas_call(kernel, out_shape=shapes, in_specs=specs or [VMEM] * len(a...  9.51 us
    all_to_all x1, waiting for transfers between devices, swap(): return lax.all_to_all(chunks, axis, 0, 0, tiled=True)  7.88 us
    unnamed x16, local copies, waits for them, and re-layouts  3.77 us
    all_to_all x1, starting transfers between devices, swap(): return lax.all_to_all(chunks, axis, 0, 0, tiled=True)  2.82 us
  transfers between devices with their start and end apart: 13, of which 9 were waited for; matrix products, arithmetic and copies ran while one was open for 0% of the time, Pallas kernels for 1%

profile of v4, /device:TPU:0, one launch (start us, length us, event | category | flops | bytes accessed | tf_op | source)
XLA Modules:
  0.0 110.5 jit_solution(16630436895614236050)
XLA Ops:
  0.6 0.6 copy-done.7
  1.3 1.2 %copy-done = f32[64,4096]{1,0:T(8,128)S(1)} copy-done((f32[64,4096]{1,0:T(8,128)S(1)}, f32[64,4096]{1,0:T(8,128)}, u32[]{:S(2)}) %copy-start) | copy-done | bytes 1048600
  2.5 1.0 copy-done.2
  3.6 0.8 copy-done.5
  4.4 2.8 %shard_map.76 = (f32[40,128]{1,0:T(8,128)S(1)}, f32[40,128]{1,0:T(8,128)S(1)}, f32[40,128]{1,0:T(8,128)S(1)}, f32[40,128]{1,0:T(8,128)S(1)}) custom-call(s32[1]{0:T(128)} %bitcast.mine_ref, s32[16]{0:T(128)S(1)} %bitcast.17, bf16[16,128,128]{2,1,0:T(8,128)(2,1)S(1)} %bitcast.8, f32[128,128]{1,0:T(8,128)S(1)} %bitcast.14, f32[64,4096]{1,0:T(8,128)S(1)} %copy-done), custom_call_target="tpu_custom_call" | custom-call | tf_op jit(solution)/shard_map/pallas_call | solution.py:28
  7.2 3.1 %collective-permute-start = (f32[40,128]{1,0:T(8,128)S(1)}, f32[40,128]{1,0:T(8,128)S(1)}, u32[]{:S(2)}, u32[]{:S(2)}) collective-permute-start(f32[40,128]{1,0:T(8,128)S(1)} %get-tuple-element.39), channel_id=1, source_target_pairs={{0,1},{1,0},{2,3},{3,2},{4,5},{5,4},{6,7},{7,6},{8,9},{9,8},{10,11... | collective-permute-start | bytes 61448 | tf_op jit(solution)/shard_map/ppermute | solution.py:51
  10.3 2.6 %collective-permute-start.1 = (f32[40,128]{1,0:T(8,128)S(1)}, f32[40,128]{1,0:T(8,128)S(1)}, u32[]{:S(2)}, u32[]{:S(2)}) collective-permute-start(f32[40,128]{1,0:T(8,128)S(1)} %get-tuple-element.40), channel_id=1, source_target_pairs={{0,2},{1,3},{2,0},{3,1},{4,6},{5,7},{6,4},{7,5},{8,10},{9,11},{10,... | collective-permute-start | bytes 61448 | tf_op jit(solution)/shard_map/ppermute | solution.py:51
  12.9 2.3 %collective-permute-done.1.refs_2_ = f32[40,128]{1,0:T(8,128)S(1)} collective-permute-done((f32[40,128]{1,0:T(8,128)S(1)}, f32[40,128]{1,0:T(8,128)S(1)}, u32[]{:S(2)}, u32[]{:S(2)}) %collective-permute-start.1) | collective-permute-done | bytes 20512 | tf_op jit(solution)/shard_map/ppermute | solution.py:51
  15.2 3.3 %collective-permute-done.2.refs_3_ = f32[40,128]{1,0:T(8,128)S(1)} collective-permute-done((f32[40,128]{1,0:T(8,128)S(1)}, f32[40,128]{1,0:T(8,128)S(1)}, u32[]{:S(2)}, u32[]{:S(2)}) %collective-permute-start.2) | collective-permute-done | bytes 20512 | tf_op jit(solution)/shard_map/ppermute | solution.py:51
  18.5 0.9 shard_map.77
  19.3 2.8 %all-to-all-start = ((f32[32,1,1152]{2,1,0:T(1,128)}), f32[32,1,1152]{2,1,0:T(1,128)S(1)}, u32[]{:S(2)}, u32[]{:S(2)}) async-start(f32[32,1,1152]{2,1,0:T(1,128)} %get-tuple-element.42), calls=%async_computation | async-start | bytes 294912 | tf_op jit(solution)/shard_map/all_to_all | solution.py:23
  22.2 0.7 shard_map.78
  22.9 7.9 %all-to-all-done.received_ref = f32[32,1,1152]{2,1,0:T(1,128)S(1)} async-done(((f32[32,1,1152]{2,1,0:T(1,128)}), f32[32,1,1152]{2,1,0:T(1,128)S(1)}, u32[]{:S(2)}, u32[]{:S(2)}) %all-to-all-start) | async-done | bytes 147488 | tf_op jit(solution)/shard_map/all_to_all | solution.py:23
  31.3 1.8 %collective-permute-start.4 = (f32[40,128]{1,0:T(8,128)S(1)}, f32[40,128]{1,0:T(8,128)S(1)}, u32[]{:S(2)}, u32[]{:S(2)}) collective-permute-start(f32[40,128]{1,0:T(8,128)S(1)} %get-tuple-element.47), channel_id=1, source_target_pairs={{0,2},{1,3},{2,0},{3,1},{4,6},{5,7},{6,4},{7,5},{8,10},{9,11},{10,... | collective-permute-start | bytes 61448 | tf_op jit(solution)/shard_map/ppermute | solution.py:51
  33.1 2.5 %collective-permute-start.5 = (f32[40,128]{1,0:T(8,128)S(1)}, f32[40,128]{1,0:T(8,128)S(1)}, u32[]{:S(2)}, u32[]{:S(2)}) collective-permute-start(f32[40,128]{1,0:T(8,128)S(1)} %get-tuple-element.48), channel_id=1, source_target_pairs={{0,3},{1,2},{2,1},{3,0},{4,7},{5,6},{6,5},{7,4},{8,11},{9,10},{10,... | collective-permute-start | bytes 61448 | tf_op jit(solution)/shard_map/ppermute | solution.py:51
  36.0 2.7 %collective-permute-done.5.refs_3_ = f32[40,128]{1,0:T(8,128)S(1)} collective-permute-done((f32[40,128]{1,0:T(8,128)S(1)}, f32[40,128]{1,0:T(8,128)S(1)}, u32[]{:S(2)}, u32[]{:S(2)}) %collective-permute-start.5) | collective-permute-done | bytes 20512 | tf_op jit(solution)/shard_map/ppermute | solution.py:51
  38.7 0.9 shard_map.80
  39.5 7.4 %all_to_all.35.refs_0_ = f32[8,16,128]{2,1,0:T(8,128)S(1)} all-to-all(f32[8,16,128]{2,1,0:T(8,128)S(1)} %bitcast.16), channel_id=1, replica_groups=mesh['row'=8,'col'=4] {'row'}, dimensions={0} | all-to-all | bytes 131072 | tf_op jit(solution)/shard_map/all_to_all | solution.py:23
  47.2 11.6 %all_to_all.36.received_ref = f32[32,1,1280]{2,1,0:T(1,128)S(1)} all-to-all(f32[32,1,1280]{2,1,0:T(1,128)S(1)} %get-tuple-element.54), channel_id=1, replica_groups=mesh['row'=8,'col'=4] {'row','col'}, dimensions={0} | all-to-all | bytes 327680 | tf_op jit(solution)/shard_map/all_to_all | solution.py:23
  59.1 7.4 %all_to_all.37 = f32[8,16,128]{2,1,0:T(8,128)S(1)} all-to-all(f32[8,16,128]{2,1,0:T(8,128)S(1)} %get-tuple-element.56), channel_id=1, replica_groups=mesh['row'=8,'col'=4] {'row'}, dimensions={0} | all-to-all | bytes 131072 | tf_op jit(solution)/shard_map/all_to_all | solution.py:23
  66.5 1.0 shard_map.83
  67.6 1.9 %collective-permute-start.7 = (f32[32,128]{1,0:T(8,128)S(1)}, f32[32,128]{1,0:T(8,128)S(1)}, u32[]{:S(2)}, u32[]{:S(2)}) collective-permute-start(f32[32,128]{1,0:T(8,128)S(1)} %get-tuple-element.59), channel_id=1, source_target_pairs={{0,2},{1,3},{2,0},{3,1},{4,6},{5,7},{6,4},{7,5},{8,10},{9,11},{10,... | collective-permute-start | bytes 49160 | tf_op jit(solution)/shard_map/ppermute | solution.py:51
  69.5 2.5 %collective-permute-start.8 = (f32[32,128]{1,0:T(8,128)S(1)}, f32[32,128]{1,0:T(8,128)S(1)}, u32[]{:S(2)}, u32[]{:S(2)}) collective-permute-start(f32[32,128]{1,0:T(8,128)S(1)} %get-tuple-element.60), channel_id=1, source_target_pairs={{0,3},{1,2},{2,1},{3,0},{4,7},{5,6},{6,5},{7,4},{8,11},{9,10},{10,... | collective-permute-start | bytes 49160 | tf_op jit(solution)/shard_map/ppermute | solution.py:51
  72.3 2.7 %collective-permute-done.8.refs_3_ = f32[32,128]{1,0:T(8,128)S(1)} collective-permute-done((f32[32,128]{1,0:T(8,128)S(1)}, f32[32,128]{1,0:T(8,128)S(1)}, u32[]{:S(2)}, u32[]{:S(2)}) %collective-permute-start.8) | collective-permute-done | bytes 16416 | tf_op jit(solution)/shard_map/ppermute | solution.py:51
  75.2 9.9 %all_to_all.38.received_ref = f32[32,1,128]{2,1,0:T(1,128)S(1)} all-to-all(f32[32,1,128]{2,1,0:T(1,128)S(1)} %get-tuple-element.62), channel_id=1, replica_groups=mesh['row'=8,'col'=4] {'row','col'}, dimensions={0} | all-to-all | bytes 32768 | tf_op jit(solution)/shard_map/all_to_all | solution.py:23
  86.0 1.4 %collective-permute-start.10 = (f32[32,128]{1,0:T(8,128)S(1)}, f32[32,128]{1,0:T(8,128)S(1)}, u32[]{:S(2)}, u32[]{:S(2)}) collective-permute-start(f32[32,128]{1,0:T(8,128)S(1)} %get-tuple-element.65.refs_0_.refs_3_), channel_id=1, source_target_pairs={{0,2},{1,3},{2,0},{3,1},{4,6},{5,7},{6,4},{7,5},{8,10},{9,11},{10,... | collective-permute-start | bytes 49160 | tf_op jit(solution)/shard_map/ppermute | solution.py:51
  87.3 2.4 %collective-permute-start.9 = (f32[32,128]{1,0:T(8,128)S(1)}, f32[32,128]{1,0:T(8,128)S(1)}, u32[]{:S(2)}, u32[]{:S(2)}) collective-permute-start(f32[32,128]{1,0:T(8,128)S(1)} %get-tuple-element.65.refs_0_.refs_3_), channel_id=1, source_target_pairs={{0,1},{1,0},{2,3},{3,2},{4,5},{5,4},{6,7},{7,6},{8,9},{9,8},{10,11... | collective-permute-start | bytes 49160 | tf_op jit(solution)/shard_map/ppermute | solution.py:51
  89.8 1.1 %collective-permute-done.11.refs_3_ = f32[32,128]{1,0:T(8,128)S(1)} collective-permute-done((f32[32,128]{1,0:T(8,128)S(1)}, f32[32,128]{1,0:T(8,128)S(1)}, u32[]{:S(2)}, u32[]{:S(2)}) %collective-permute-start.11) | collective-permute-done | bytes 16416 | tf_op jit(solution)/shard_map/ppermute | solution.py:51
  91.5 0.9 shard_map.86
  92.4 7.4 %all_to_all.39.refs_0_ = f32[8,16,128]{2,1,0:T(8,128)S(1)} all-to-all(f32[8,16,128]{2,1,0:T(8,128)S(1)} %bitcast.13), channel_id=1, replica_groups=mesh['row'=8,'col'=4] {'row'}, dimensions={0} | all-to-all | bytes 131072 | tf_op jit(solution)/shard_map/all_to_all | solution.py:23
  99.9 9.7 %all_to_all.40.received_ref = f32[32,1,128]{2,1,0:T(1,128)S(1)} all-to-all(f32[32,1,128]{2,1,0:T(1,128)S(1)} %get-tuple-element.67), channel_id=1, replica_groups=mesh['row'=8,'col'=4] {'row','col'}, dimensions={0} | all-to-all | bytes 32768 | tf_op jit(solution)/shard_map/all_to_all | solution.py:23
  109.7 0.9 shard_map.88
  (29 shorter events, 3.6 us)
Async XLA Ops:
  0.6 0.7 copy-start.7
  1.3 1.2 %copy-start = (f32[64,4096]{1,0:T(8,128)S(1)}, f32[64,4096]{1,0:T(8,128)}, u32[]{:S(2)}) copy-start(f32[64,4096]{1,0:T(8,128)} %basis_ref.5) | copy-start | bytes 3145732
  2.5 1.0 copy-start.2
  3.6 0.8 copy-start.5
  4.4 14.1 %copy-start.1 = (f32[64,4096]{1,0:T(8,128)S(1)}, f32[64,4096]{1,0:T(8,128)}, u32[]{:S(2)}) copy-start(f32[64,4096]{1,0:T(8,128)} %basis_ref.5) | copy-start | bytes 3145732
  7.2 5.7 %collective-permute-start = (f32[40,128]{1,0:T(8,128)S(1)}, f32[40,128]{1,0:T(8,128)S(1)}, u32[]{:S(2)}, u32[]{:S(2)}) collective-permute-start(f32[40,128]{1,0:T(8,128)S(1)} %get-tuple-element.39), channel_id=1, source_target_pairs={{0,1},{1,0},{2,3},{3,2},{4,5},{5,4},{6,7},{7,6},{8,9},{9,8},{10,11... | collective-permute-start | bytes 61448 | tf_op jit(solution)/shard_map/ppermute | solution.py:51
  10.3 4.9 %collective-permute-start.1 = (f32[40,128]{1,0:T(8,128)S(1)}, f32[40,128]{1,0:T(8,128)S(1)}, u32[]{:S(2)}, u32[]{:S(2)}) collective-permute-start(f32[40,128]{1,0:T(8,128)S(1)} %get-tuple-element.40), channel_id=1, source_target_pairs={{0,2},{1,3},{2,0},{3,1},{4,6},{5,7},{6,4},{7,5},{8,10},{9,11},{10,... | collective-permute-start | bytes 61448 | tf_op jit(solution)/shard_map/ppermute | solution.py:51
  12.9 5.6 %collective-permute-start.2 = (f32[40,128]{1,0:T(8,128)S(1)}, f32[40,128]{1,0:T(8,128)S(1)}, u32[]{:S(2)}, u32[]{:S(2)}) collective-permute-start(f32[40,128]{1,0:T(8,128)S(1)} %get-tuple-element.41), channel_id=1, source_target_pairs={{0,3},{1,2},{2,1},{3,0},{4,7},{5,6},{6,5},{7,4},{8,11},{9,10},{10,... | collective-permute-start | bytes 61448 | tf_op jit(solution)/shard_map/ppermute | solution.py:51
  18.5 3.7 %copy-start.4 = (f32[64,1,2048]{2,1,0:T(1,128)S(1)}, f32[64,1,2048]{2,1,0:T(1,128)}, u32[]{:S(2)}) copy-start(f32[64,1,2048]{2,1,0:T(1,128)} %basis_ref.3) | copy-start | bytes 1572868
  19.3 2.8 %copy-start.6 = (f32[16384]{0:T(1024)S(1)}, f32[16384]{0:T(1024)}, u32[]{:S(2)}) copy-start(f32[16384]{0:T(1024)} %param.9) | copy-start | bytes 196612
  19.3 11.4 %all-to-all-start = ((f32[32,1,1152]{2,1,0:T(1,128)}), f32[32,1,1152]{2,1,0:T(1,128)S(1)}, u32[]{:S(2)}, u32[]{:S(2)}) async-start(f32[32,1,1152]{2,1,0:T(1,128)} %get-tuple-element.42), calls=%async_computation | async-start | bytes 294912 | tf_op jit(solution)/shard_map/all_to_all | solution.py:23
  30.8 7.9 %copy-start.3 = (bf16[1,16,128,128]{3,2,1,0:T(8,128)(2,1)S(1)}, bf16[1,16,128,128]{3,2,1,0:T(8,128)(2,1)}, u32[]{:S(2)}) copy-start(bf16[1,16,128,128]{3,2,1,0:T(8,128)(2,1)} %param.5) | copy-start | bytes 1572868
  31.2 4.5 %collective-permute-start.3 = (f32[40,128]{1,0:T(8,128)S(1)}, f32[40,128]{1,0:T(8,128)S(1)}, u32[]{:S(2)}, u32[]{:S(2)}) collective-permute-start(f32[40,128]{1,0:T(8,128)S(1)} %get-tuple-element.46), channel_id=1, source_target_pairs={{0,1},{1,0},{2,3},{3,2},{4,5},{5,4},{6,7},{7,6},{8,9},{9,8},{10,11... | collective-permute-start | bytes 61448 | tf_op jit(solution)/shard_map/ppermute | solution.py:51
  31.3 4.7 %collective-permute-start.4 = (f32[40,128]{1,0:T(8,128)S(1)}, f32[40,128]{1,0:T(8,128)S(1)}, u32[]{:S(2)}, u32[]{:S(2)}) collective-permute-start(f32[40,128]{1,0:T(8,128)S(1)} %get-tuple-element.47), channel_id=1, source_target_pairs={{0,2},{1,3},{2,0},{3,1},{4,6},{5,7},{6,4},{7,5},{8,10},{9,11},{10,... | collective-permute-start | bytes 61448 | tf_op jit(solution)/shard_map/ppermute | solution.py:51
  33.1 5.6 %collective-permute-start.5 = (f32[40,128]{1,0:T(8,128)S(1)}, f32[40,128]{1,0:T(8,128)S(1)}, u32[]{:S(2)}, u32[]{:S(2)}) collective-permute-start(f32[40,128]{1,0:T(8,128)S(1)} %get-tuple-element.48), channel_id=1, source_target_pairs={{0,3},{1,2},{2,1},{3,0},{4,7},{5,6},{6,5},{7,4},{8,11},{9,10},{10,... | collective-permute-start | bytes 61448 | tf_op jit(solution)/shard_map/ppermute | solution.py:51
  67.5 4.5 %collective-permute-start.6 = (f32[32,128]{1,0:T(8,128)S(1)}, f32[32,128]{1,0:T(8,128)S(1)}, u32[]{:S(2)}, u32[]{:S(2)}) collective-permute-start(f32[32,128]{1,0:T(8,128)S(1)} %get-tuple-element.58), channel_id=1, source_target_pairs={{0,1},{1,0},{2,3},{3,2},{4,5},{5,4},{6,7},{7,6},{8,9},{9,8},{10,11... | collective-permute-start | bytes 49160 | tf_op jit(solution)/shard_map/ppermute | solution.py:51
  67.6 4.7 %collective-permute-start.7 = (f32[32,128]{1,0:T(8,128)S(1)}, f32[32,128]{1,0:T(8,128)S(1)}, u32[]{:S(2)}, u32[]{:S(2)}) collective-permute-start(f32[32,128]{1,0:T(8,128)S(1)} %get-tuple-element.59), channel_id=1, source_target_pairs={{0,2},{1,3},{2,0},{3,1},{4,6},{5,7},{6,4},{7,5},{8,10},{9,11},{10,... | collective-permute-start | bytes 49160 | tf_op jit(solution)/shard_map/ppermute | solution.py:51
  69.5 5.5 %collective-permute-start.8 = (f32[32,128]{1,0:T(8,128)S(1)}, f32[32,128]{1,0:T(8,128)S(1)}, u32[]{:S(2)}, u32[]{:S(2)}) collective-permute-start(f32[32,128]{1,0:T(8,128)S(1)} %get-tuple-element.60), channel_id=1, source_target_pairs={{0,3},{1,2},{2,1},{3,0},{4,7},{5,6},{6,5},{7,4},{8,11},{9,10},{10,... | collective-permute-start | bytes 49160 | tf_op jit(solution)/shard_map/ppermute | solution.py:51
  85.3 5.6 %collective-permute-start.11 = (f32[32,128]{1,0:T(8,128)S(1)}, f32[32,128]{1,0:T(8,128)S(1)}, u32[]{:S(2)}, u32[]{:S(2)}) collective-permute-start(f32[32,128]{1,0:T(8,128)S(1)} %get-tuple-element.65.refs_0_.refs_3_), channel_id=1, source_target_pairs={{0,3},{1,2},{2,1},{3,0},{4,7},{5,6},{6,5},{7,4},{8,11},{9,10},{10,... | collective-permute-start | bytes 49160 | tf_op jit(solution)/shard_map/ppermute | solution.py:51
  86.0 5.0 %collective-permute-start.10 = (f32[32,128]{1,0:T(8,128)S(1)}, f32[32,128]{1,0:T(8,128)S(1)}, u32[]{:S(2)}, u32[]{:S(2)}) collective-permute-start(f32[32,128]{1,0:T(8,128)S(1)} %get-tuple-element.65.refs_0_.refs_3_), channel_id=1, source_target_pairs={{0,2},{1,3},{2,0},{3,1},{4,6},{5,7},{6,4},{7,5},{8,10},{9,11},{10,... | collective-permute-start | bytes 49160 | tf_op jit(solution)/shard_map/ppermute | solution.py:51
  87.3 4.2 %collective-permute-start.9 = (f32[32,128]{1,0:T(8,128)S(1)}, f32[32,128]{1,0:T(8,128)S(1)}, u32[]{:S(2)}, u32[]{:S(2)}) collective-permute-start(f32[32,128]{1,0:T(8,128)S(1)} %get-tuple-element.65.refs_0_.refs_3_), channel_id=1, source_target_pairs={{0,1},{1,0},{2,3},{3,2},{4,5},{5,4},{6,7},{7,6},{8,9},{9,8},{10,11... | collective-permute-start | bytes 49160 | tf_op jit(solution)/shard_map/ppermute | solution.py:51

commit v5 on v4

--- a/solution.py
+++ b/solution.py
@@ -14,16 +14,17 @@
 LANES = 128
 GROUP = 8
 PARAMS = pltpu.CompilerParams(vmem_limit_bytes=8 * 2**20)
+WIDE = pltpu.CompilerParams(vmem_limit_bytes=63950 * 2**10)
 VMEM = pl.BlockSpec(memory_space=pltpu.VMEM)
 SMEM = pl.BlockSpec(memory_space=pltpu.SMEM)
-ANY = pl.BlockSpec(memory_space=pl.ANY)
+HBM = pl.BlockSpec(memory_space=pltpu.HBM)
 
 
 def swap(chunks, axis):
     return lax.all_to_all(chunks, axis, 0, 0, tiled=True)
 
 
-def call(kernel, outs, args, specs=None, scratch=()):
+def call(kernel, outs, args, specs=None, scratch=(), params=PARAMS):
     shapes = tuple(jax.ShapeDtypeStruct(shape, jnp.float32) for shape in outs)
     return pl.pallas_call(
         kernel,
@@ -31,7 +32,7 @@
         in_specs=specs or [VMEM] * len(args),
         out_specs=tuple([VMEM] * len(outs)),
         scratch_shapes=list(scratch),
-        compiler_params=PARAMS,
+        compiler_params=params,
     )(*args)
 
 
@@ -44,10 +45,10 @@
     return groups + [refs]
 
 
-def exchange(messages, axis):
+def exchange(messages, hops, axis):
     count = lax.axis_size(axis)
     arrived = [messages[0]]
-    for x in range(1, count):
+    for x in hops:
         arrived.append(lax.ppermute(messages[x], axis, [(i, i ^ x) for i in range(count)]))
     return arrived
 
@@ -171,8 +172,9 @@
         kernel,
         [(rows + share, width)] * peers,
         [mine, slots, tiles, vector, basis],
-        [SMEM, SMEM, ANY, ANY, ANY],
+        [SMEM, SMEM, HBM, HBM, HBM],
         scratch,
+        WIDE,
     )
 
 
@@ -222,29 +224,40 @@
     )
 
 
-def backward_product(mine, tiles, slots, messages, rows, col_blocks):
+def backward_product(mine, tiles, slots, messages, hops, rows, col_blocks, peers_row):
     count, width = tiles.shape[0], tiles.shape[1]
     peers = len(messages)
     share = messages[0].shape[0] - rows
+    chunk = col_blocks // peers_row
+    joined = share // peers_row if share % peers_row == 0 else 0
+    apart = share and not joined
 
     def kernel(mine_ref, slots_ref, tiles_ref, *refs):
         sources, rest = take(refs, peers)
-        outs, (vector_ref, picked_ref, product_ref) = take(rest, 2 if share else 1)
-        for x, source in enumerate(sources):
-            peer = jnp.bitwise_xor(mine_ref[0], x)
+        (chunks_ref,), apart_refs, scratch = take(rest, 1, 1 if apart else 0)
+        vector_ref, dense_ref, picked_ref, product_ref = scratch
+        for at, source in enumerate(sources):
+            peer = jnp.bitwise_xor(mine_ref[0], ([0] + hops)[at])
             vector_ref[pl.ds(peer * rows, rows), :] = source[:rows, :]
         tile_sums(
-            slots_ref, tiles_ref, vector_ref, outs[0], picked_ref, product_ref, col_blocks, False
+            slots_ref, tiles_ref, vector_ref, dense_ref, picked_ref, product_ref, col_blocks, False
         )
+        for i in range(peers_row):
+            chunks_ref[i, :chunk, :] = dense_ref[i * chunk : (i + 1) * chunk, :]
         if share:
             added = sources[0][rows:, :]
             for source in sources[1:]:
                 added = added + source[rows:, :]
-            outs[1][...] = added
+            for ref in apart_refs:
+                ref[...] = added
+            if joined:
+                for i in range(peers_row):
+                    chunks_ref[i, chunk:, :] = added[i * joined : (i + 1) * joined]
 
     scratch = [pltpu.VMEM((rows * peers, width), jnp.float32)]
+    scratch += [pltpu.VMEM((col_blocks, width), jnp.float32)]
     scratch += [pltpu.VMEM((count, width), jnp.float32)] * 2
-    outs = [(col_blocks, width)] + ([(share, width)] if share else [])
+    outs = [(peers_row, chunk + joined, width)] + ([(share, width)] if apart else [])
     return call(
         kernel,
         outs,
@@ -266,15 +279,15 @@
     return row + jnp.where(lane == LANES - 1, total_sum(piece * piece), 0.0)
 
 
-def inner_products(pieces, rows, basis, extras, riders, copies):
+def inner_products(pieces, rows, basis, extras, riders, copies, after=()):
     listed = pieces if isinstance(pieces, (list, tuple)) else [pieces]
     stacked = listed is not pieces
-    further = 0 if stacked else listed[0].shape[0] - rows
+    further = listed[0].shape[-2] - rows
     lines = 1 + further + sum(rider.shape[0] for rider in riders)
 
     def kernel(*refs):
-        sources, (basis_ref,), extra_refs, rider_refs, (piece_ref, sent_ref) = take(
-            refs, len(listed), 1, len(extras), len(riders)
+        sources, (basis_ref,), extra_refs, rider_refs, _, (piece_ref, sent_ref) = take(
+            refs, len(listed), 1, len(extras), len(riders), len(after)
         )
         if stacked:
             summed = jnp.sum(sources[0][...], 0)
@@ -285,9 +298,9 @@
         piece = summed[:rows]
         piece_ref[...] = piece
         sent = [basis_products(piece, basis_ref, [ref[...] for ref in extra_refs])]
-        sent += [summed[rows + k : rows + k + 1] for k in range(further)]
         for ref in rider_refs:
             sent += [ref[k : k + 1, :] for k in range(ref.shape[0])]
+        sent += [summed[rows + k : rows + k + 1] for k in range(further)]
         for at, line in enumerate(sent):
             shape = (copies, 1, LANES)
             sent_ref[:, :, at * LANES : (at + 1) * LANES] = jnp.broadcast_to(line[None], shape)
@@ -295,7 +308,7 @@
     return call(
         kernel,
         [(rows, LANES), (copies, 1, lines * LANES)],
-        [*listed, basis, *extras, *riders],
+        [*listed, basis, *extras, *riders, *after],
     )
 
 
@@ -307,6 +320,15 @@
 def received_gram(received_ref, first, packed_ref, peers):
     share = packed_ref.shape[0] // peers
     devices = received_ref.shape[0]
+    lines = received_ref.shape[2] // LANES - first
+    if lines < share:
+        for k in range(lines):
+            at = slice((first + k) * LANES, (first + k + 1) * LANES)
+            for device in range(devices):
+                i, peer = divmod(device, peers)
+                to = peer * share + i * lines + k
+                packed_ref[to : to + 1, :] = received_ref[device, :, at]
+        return
     for k in range(share):
         at = slice((first + k) * LANES, (first + k + 1) * LANES)
         added = received_ref[0:peers, 0, at]
@@ -479,20 +501,22 @@
     total_right = cols_len * col_count
     mine = lax.axis_index("col").reshape(1)
     mine_row = lax.axis_index("row").reshape(1)
+    far_first = list(range(col_count - 1, 0, -1))
 
     whole_start = v_start.reshape(col_blocks, width)
     messages = start(mine, blocks, slots, whole_start, u_basis, row_blocks, total_left, col_count)
     right_basis, start_share, start_row, right_packed = right_start(
         mine_row, v_basis, whole_start, messages[0], total_right
     )
-    arrived = exchange(messages, "col")
+    arrived = exchange(messages, far_first, "col")
 
     lefts, rights, scales = ([], [], [])
     right_extras = [start_share]
     left_gram = right_gram = None
     for iteration in range(ITERS):
         last = iteration + 1 == ITERS
-        piece, sent = inner_products(arrived, left_rows, u_basis, lefts, [], devices)
+        after = [right_packed] if iteration == 0 else []
+        piece, sent = inner_products(arrived, left_rows, u_basis, lefts, [], devices, after)
         summed_rows = swap(sent, BOTH)
         if iteration == 0:
             *messages, left_unit, left_gram, alpha = first_vector(
@@ -506,9 +530,12 @@
             messages = [left_unit] * col_count
         lefts = lefts + [left_unit]
         scales = scales + [alpha]
-        arrived = exchange(messages, "col")
-        dense, *further = backward_product(mine, blocks, slots, arrived, left_rows, col_blocks)
-        received = swap(dense.reshape(row_count, right_rows, width), "row")
+        hops = far_first if iteration == 0 else far_first[::-1]
+        arrived = exchange(messages, hops, "col")
+        chunks, *further = backward_product(
+            mine, blocks, slots, arrived, hops, left_rows, col_blocks, row_count
+        )
+        received = swap(chunks, "row")
         riders = [start_row, *further] if iteration == 0 else []
         piece, sent = inner_products(received, right_rows, right_basis, right_extras, riders, devices)
         summed_rows = swap(sent, BOTH)
@@ -529,7 +556,7 @@
             scales = scales + [beta]
             joined = swap(copies, "row").reshape(col_blocks, width)
             messages = forward_messages(mine, blocks, slots, joined, row_blocks, col_count)
-            arrived = exchange(messages, "col")
+            arrived = exchange(messages, far_first, "col")
     return last_vector(
         summed_rows, right_gram, piece, right_basis, right_extras, total_right, lefts, rights, scales
     )

time: 111 us -> 104 us (0.937)
  waiting for transfers between devices: 21.2 us -> 6.98 us
  blocking collectives: 53.4 us -> 64.4 us
  starting transfers between devices: 21.9 us -> 19.1 us
  local copies, waits for them, and re-layouts: 3.77 us -> 1.78 us
  Pallas kernels: 9.51 us -> 10.7 us
    all_to_all x6 -> x7, blocking collectives: 53.4 us -> 64.4 us  [swap(): return lax.all_to_all(chunks, axis, 0, 0, tiled=True)]
    all_to_all x1 -> x0, waiting for transfers between devices: 7.88 us -> none  [swap(): return lax.all_to_all(chunks, axis, 0, 0, tiled=True)]
    ppermute x12, waiting for transfers between devices: 13.4 us -> 6.98 us  [exchange(): lax.ppermute(messages[x], axis, [(i, i ^ x) for i in range(count)])]
    all_to_all x1 -> x0, starting transfers between devices: 2.82 us -> none  [swap(): return lax.all_to_all(chunks, axis, 0, 0, tiled=True)]
    unnamed x16 -> x12, local copies, waits for them, and re-layouts: 3.77 us -> 1.78 us
    pallas_call x13, Pallas kernels: 9.51 us -> 10.7 us  [call(): pl.pallas_call(kernel, out_shape=shapes, in_specs=specs or [VMEM] * len(a...]
  transfers between devices with their start and end apart: 13 -> 12, of which waited for: 9 -> 8; matrix products, arithmetic and copies ran while one was open for 0% -> 0% of each run, Pallas kernels for 1% -> 1%
where the time goes in v5:
time: 104 us
  blocking collectives  64.4 us (62%)
  starting transfers between devices  19.1 us (18%)
  Pallas kernels  10.7 us (10%)
  waiting for transfers between devices  6.98 us (7%)
  local copies, waits for them, and re-layouts  1.78 us (2%)
    all_to_all x7, blocking collectives, swap(): return lax.all_to_all(chunks, axis, 0, 0, tiled=True)  64.4 us
    ppermute x12, starting transfers between devices, exchange(): lax.ppermute(messages[x], axis, [(i, i ^ x) for i in range(count)])  19.1 us
    pallas_call x13, Pallas kernels, call(): pl.pallas_call(kernel, out_shape=shapes, in_specs=specs or [VMEM] * len(a...  10.7 us
    ppermute x12, waiting for transfers between devices, exchange(): lax.ppermute(messages[x], axis, [(i, i ^ x) for i in range(count)])  6.98 us
  transfers between devices with their start and end apart: 12, of which 8 were waited for; matrix products, arithmetic and copies ran while one was open for 0% of the time, Pallas kernels for 1%

profile of v5, /device:TPU:0, one launch (start us, length us, event | category | flops | bytes accessed | tf_op | source)
XLA Modules:
  0.0 103.7 jit_solution(17688830793541717110)
XLA Ops:
  0.7 4.6 %shard_map.76 = (f32[40,128]{1,0:T(8,128)}, f32[40,128]{1,0:T(8,128)}, f32[40,128]{1,0:T(8,128)}, f32[40,128]{1,0:T(8,128)}) custom-call(s32[1]{0:T(128)} %bitcast.mine_ref, s32[16]{0:T(128)} %bitcast.13, bf16[16,128,128]{2,1,0:T(8,128)(2,1)} %bitcast.6, f32[128,128]{1,0:T(8,128)} %bitcast.11, f32[64,4096]{1,0:T(8,128)} %basis_ref.5), custom_call_target="tpu_custom_call" | custom-call | tf_op jit(solution)/shard_map/pallas_call | solution.py:29
  5.2 5.1 %collective-permute-start = (f32[40,128]{1,0:T(8,128)}, f32[40,128]{1,0:T(8,128)S(1)}, u32[]{:S(2)}, u32[]{:S(2)}) collective-permute-start(f32[40,128]{1,0:T(8,128)} %get-tuple-element.37), channel_id=1, source_target_pairs={{0,3},{1,2},{2,1},{3,0},{4,7},{5,6},{6,5},{7,4},{8,11},{9,10},{10,... | collective-permute-start | bytes 61448 | tf_op jit(solution)/shard_map/ppermute | solution.py:52
  10.4 0.6 collective-permute-start.2
  11.0 1.0 %copy-done.2 = f32[64,1,2048]{2,1,0:T(1,128)S(1)} copy-done((f32[64,1,2048]{2,1,0:T(1,128)S(1)}, f32[64,1,2048]{2,1,0:T(1,128)}, u32[]{:S(2)}) %copy-start.2) | copy-done | bytes 524312
  12.0 0.7 copy-done.4
  12.8 0.8 shard_map.77
  13.6 1.7 %collective-permute-done.1.refs_2_ = f32[40,128]{1,0:T(8,128)S(1)} collective-permute-done((f32[40,128]{1,0:T(8,128)}, f32[40,128]{1,0:T(8,128)S(1)}, u32[]{:S(2)}, u32[]{:S(2)}) %collective-permute-start.1) | collective-permute-done | bytes 20512 | tf_op jit(solution)/shard_map/ppermute | solution.py:52
  15.4 12.7 %all_to_all.35.received_ref = f32[32,1,1152]{2,1,0:T(1,128)S(1)} all-to-all(f32[32,1,1152]{2,1,0:T(1,128)S(1)} %get-tuple-element.41), channel_id=1, replica_groups=mesh['row'=8,'col'=4] {'row','col'}, dimensions={0} | all-to-all | bytes 294912 | tf_op jit(solution)/shard_map/all_to_all | solution.py:24
  28.6 1.3 %collective-permute-start.3 = (f32[40,128]{1,0:T(8,128)S(1)}, f32[40,128]{1,0:T(8,128)S(1)}, u32[]{:S(2)}, u32[]{:S(2)}) collective-permute-start(f32[40,128]{1,0:T(8,128)S(1)} %get-tuple-element.44), channel_id=1, source_target_pairs={{0,3},{1,2},{2,1},{3,0},{4,7},{5,6},{6,5},{7,4},{8,11},{9,10},{10,... | collective-permute-start | bytes 61448 | tf_op jit(solution)/shard_map/ppermute | solution.py:52
  29.9 3.1 %collective-permute-start.5 = (f32[40,128]{1,0:T(8,128)S(1)}, f32[40,128]{1,0:T(8,128)S(1)}, u32[]{:S(2)}, u32[]{:S(2)}) collective-permute-start(f32[40,128]{1,0:T(8,128)S(1)} %get-tuple-element.46), channel_id=1, source_target_pairs={{0,1},{1,0},{2,3},{3,2},{4,5},{5,4},{6,7},{7,6},{8,9},{9,8},{10,11... | collective-permute-start | bytes 61448 | tf_op jit(solution)/shard_map/ppermute | solution.py:52
  33.0 1.2 %collective-permute-done.3.refs_1_ = f32[40,128]{1,0:T(8,128)S(1)} collective-permute-done((f32[40,128]{1,0:T(8,128)S(1)}, f32[40,128]{1,0:T(8,128)S(1)}, u32[]{:S(2)}, u32[]{:S(2)}) %collective-permute-start.3) | collective-permute-done | bytes 20512 | tf_op jit(solution)/shard_map/ppermute | solution.py:52
  34.2 0.4 collective-permute-done.4.refs_2_
  34.9 0.9 shard_map.80
  35.8 7.6 %all_to_all.36.refs_0_ = f32[8,17,128]{2,1,0:T(8,128)S(1)} all-to-all(f32[8,17,128]{2,1,0:T(8,128)S(1)} %shard_map.80), channel_id=1, replica_groups=mesh['row'=8,'col'=4] {'row'}, dimensions={0} | all-to-all | bytes 139264 | tf_op jit(solution)/shard_map/all_to_all | solution.py:24
  43.5 9.8 %all_to_all.37.received_ref = f32[32,1,384]{2,1,0:T(1,128)S(1)} all-to-all(f32[32,1,384]{2,1,0:T(1,128)S(1)} %get-tuple-element.50), channel_id=1, replica_groups=mesh['row'=8,'col'=4] {'row','col'}, dimensions={0} | all-to-all | bytes 98304 | tf_op jit(solution)/shard_map/all_to_all | solution.py:24
  53.7 7.4 %all_to_all.38 = f32[8,16,128]{2,1,0:T(8,128)S(1)} all-to-all(f32[8,16,128]{2,1,0:T(8,128)S(1)} %get-tuple-element.52), channel_id=1, replica_groups=mesh['row'=8,'col'=4] {'row'}, dimensions={0} | all-to-all | bytes 131072 | tf_op jit(solution)/shard_map/all_to_all | solution.py:24
  61.1 1.0 shard_map.83
  62.1 0.7 collective-permute-start.6
  62.8 1.2 %collective-permute-start.7 = (f32[32,128]{1,0:T(8,128)S(1)}, f32[32,128]{1,0:T(8,128)S(1)}, u32[]{:S(2)}, u32[]{:S(2)}) collective-permute-start(f32[32,128]{1,0:T(8,128)S(1)} %get-tuple-element.55), channel_id=1, source_target_pairs={{0,2},{1,3},{2,0},{3,1},{4,6},{5,7},{6,4},{7,5},{8,10},{9,11},{10,... | collective-permute-start | bytes 49160 | tf_op jit(solution)/shard_map/ppermute | solution.py:52
  64.0 2.6 %collective-permute-start.8 = (f32[32,128]{1,0:T(8,128)S(1)}, f32[32,128]{1,0:T(8,128)S(1)}, u32[]{:S(2)}, u32[]{:S(2)}) collective-permute-start(f32[32,128]{1,0:T(8,128)S(1)} %get-tuple-element.56), channel_id=1, source_target_pairs={{0,1},{1,0},{2,3},{3,2},{4,5},{5,4},{6,7},{7,6},{8,9},{9,8},{10,11... | collective-permute-start | bytes 49160 | tf_op jit(solution)/shard_map/ppermute | solution.py:52
  66.6 1.1 %collective-permute-done.6.refs_1_ = f32[32,128]{1,0:T(8,128)S(1)} collective-permute-done((f32[32,128]{1,0:T(8,128)S(1)}, f32[32,128]{1,0:T(8,128)S(1)}, u32[]{:S(2)}, u32[]{:S(2)}) %collective-permute-start.6) | collective-permute-done | bytes 16416 | tf_op jit(solution)/shard_map/ppermute | solution.py:52
  67.8 0.6 collective-permute-done.8.refs_3_
  68.5 9.7 %all_to_all.39.received_ref = f32[32,1,128]{2,1,0:T(1,128)S(1)} all-to-all(f32[32,1,128]{2,1,0:T(1,128)S(1)} %get-tuple-element.58), channel_id=1, replica_groups=mesh['row'=8,'col'=4] {'row','col'}, dimensions={0} | all-to-all | bytes 32768 | tf_op jit(solution)/shard_map/all_to_all | solution.py:24
  78.5 0.6 collective-permute-start.11
  79.1 1.4 %collective-permute-start.10 = (f32[32,128]{1,0:T(8,128)S(1)}, f32[32,128]{1,0:T(8,128)S(1)}, u32[]{:S(2)}, u32[]{:S(2)}) collective-permute-start(f32[32,128]{1,0:T(8,128)S(1)} %get-tuple-element.61.refs_0_.refs_3_), channel_id=1, source_target_pairs={{0,2},{1,3},{2,0},{3,1},{4,6},{5,7},{6,4},{7,5},{8,10},{9,11},{10,... | collective-permute-start | bytes 49160 | tf_op jit(solution)/shard_map/ppermute | solution.py:52
  80.5 2.4 %collective-permute-start.9 = (f32[32,128]{1,0:T(8,128)S(1)}, f32[32,128]{1,0:T(8,128)S(1)}, u32[]{:S(2)}, u32[]{:S(2)}) collective-permute-start(f32[32,128]{1,0:T(8,128)S(1)} %get-tuple-element.61.refs_0_.refs_3_), channel_id=1, source_target_pairs={{0,1},{1,0},{2,3},{3,2},{4,5},{5,4},{6,7},{7,6},{8,9},{9,8},{10,11... | collective-permute-start | bytes 49160 | tf_op jit(solution)/shard_map/ppermute | solution.py:52
  82.9 1.1 %collective-permute-done.11.refs_3_ = f32[32,128]{1,0:T(8,128)S(1)} collective-permute-done((f32[32,128]{1,0:T(8,128)S(1)}, f32[32,128]{1,0:T(8,128)S(1)}, u32[]{:S(2)}, u32[]{:S(2)}) %collective-permute-start.11) | collective-permute-done | bytes 16416 | tf_op jit(solution)/shard_map/ppermute | solution.py:52
  84.1 0.6 collective-permute-done.9.refs_1_
  84.7 0.9 shard_map.86
  85.6 7.4 %all_to_all.40.refs_0_ = f32[8,16,128]{2,1,0:T(8,128)S(1)} all-to-all(f32[8,16,128]{2,1,0:T(8,128)S(1)} %shard_map.86), channel_id=1, replica_groups=mesh['row'=8,'col'=4] {'row'}, dimensions={0} | all-to-all | bytes 131072 | tf_op jit(solution)/shard_map/all_to_all | solution.py:24
  93.1 9.7 %all_to_all.41.received_ref = f32[32,1,128]{2,1,0:T(1,128)S(1)} all-to-all(f32[32,1,128]{2,1,0:T(1,128)S(1)} %get-tuple-element.63), channel_id=1, replica_groups=mesh['row'=8,'col'=4] {'row','col'}, dimensions={0} | all-to-all | bytes 32768 | tf_op jit(solution)/shard_map/all_to_all | solution.py:24
  102.8 0.9 shard_map.88
  (24 shorter events, 1.9 us)
Async XLA Ops:
  0.6 10.4 %copy-start.3 = (f32[16384]{0:T(1024)S(1)}, f32[16384]{0:T(1024)}, u32[]{:S(2)}) copy-start(f32[16384]{0:T(1024)} %param.9) | copy-start | bytes 196612
  0.6 14.6 %copy-start = (f32[64,4096]{1,0:T(8,128)S(1)}, f32[64,4096]{1,0:T(8,128)}, u32[]{:S(2)}) copy-start(f32[64,4096]{1,0:T(8,128)} %basis_ref.5) | copy-start | bytes 3145732
  5.2 8.3 %collective-permute-start = (f32[40,128]{1,0:T(8,128)}, f32[40,128]{1,0:T(8,128)S(1)}, u32[]{:S(2)}, u32[]{:S(2)}) collective-permute-start(f32[40,128]{1,0:T(8,128)} %get-tuple-element.37), channel_id=1, source_target_pairs={{0,3},{1,2},{2,1},{3,0},{4,7},{5,6},{6,5},{7,4},{8,11},{9,10},{10,... | collective-permute-start | bytes 61448 | tf_op jit(solution)/shard_map/ppermute | solution.py:52
  10.4 4.9 %collective-permute-start.1 = (f32[40,128]{1,0:T(8,128)}, f32[40,128]{1,0:T(8,128)S(1)}, u32[]{:S(2)}, u32[]{:S(2)}) collective-permute-start(f32[40,128]{1,0:T(8,128)} %get-tuple-element.38), channel_id=1, source_target_pairs={{0,2},{1,3},{2,0},{3,1},{4,6},{5,7},{6,4},{7,5},{8,10},{9,11},{10,... | collective-permute-start | bytes 61448 | tf_op jit(solution)/shard_map/ppermute | solution.py:52
  10.4 4.9 %collective-permute-start.2 = (f32[40,128]{1,0:T(8,128)}, f32[40,128]{1,0:T(8,128)S(1)}, u32[]{:S(2)}, u32[]{:S(2)}) collective-permute-start(f32[40,128]{1,0:T(8,128)} %get-tuple-element.39), channel_id=1, source_target_pairs={{0,1},{1,0},{2,3},{3,2},{4,5},{5,4},{6,7},{7,6},{8,9},{9,8},{10,11... | collective-permute-start | bytes 61448 | tf_op jit(solution)/shard_map/ppermute | solution.py:52
  11.0 1.0 %copy-start.2 = (f32[64,1,2048]{2,1,0:T(1,128)S(1)}, f32[64,1,2048]{2,1,0:T(1,128)}, u32[]{:S(2)}) copy-start(f32[64,1,2048]{2,1,0:T(1,128)} %basis_ref.3) | copy-start | bytes 1572868
  12.0 0.7 copy-start.4
  28.2 6.7 %copy-start.1 = (bf16[1,16,128,128]{3,2,1,0:T(8,128)(2,1)S(1)}, bf16[1,16,128,128]{3,2,1,0:T(8,128)(2,1)}, u32[]{:S(2)}) copy-start(bf16[1,16,128,128]{3,2,1,0:T(8,128)(2,1)} %param.5) | copy-start | bytes 1572868
  28.6 5.6 %collective-permute-start.3 = (f32[40,128]{1,0:T(8,128)S(1)}, f32[40,128]{1,0:T(8,128)S(1)}, u32[]{:S(2)}, u32[]{:S(2)}) collective-permute-start(f32[40,128]{1,0:T(8,128)S(1)} %get-tuple-element.44), channel_id=1, source_target_pairs={{0,3},{1,2},{2,1},{3,0},{4,7},{5,6},{6,5},{7,4},{8,11},{9,10},{10,... | collective-permute-start | bytes 61448 | tf_op jit(solution)/shard_map/ppermute | solution.py:52
  29.9 4.8 %collective-permute-start.4 = (f32[40,128]{1,0:T(8,128)S(1)}, f32[40,128]{1,0:T(8,128)S(1)}, u32[]{:S(2)}, u32[]{:S(2)}) collective-permute-start(f32[40,128]{1,0:T(8,128)S(1)} %get-tuple-element.45), channel_id=1, source_target_pairs={{0,2},{1,3},{2,0},{3,1},{4,6},{5,7},{6,4},{7,5},{8,10},{9,11},{10,... | collective-permute-start | bytes 61448 | tf_op jit(solution)/shard_map/ppermute | solution.py:52
  29.9 5.0 %copy-start.5 = (s32[1,16]{1,0:T(1,128)S(1)}, s32[1,16]{1,0:T(1,128)}, u32[]{:S(2)}) copy-start(s32[1,16]{1,0:T(1,128)} %param.6) | copy-start | bytes 196
  29.9 5.0 %collective-permute-start.5 = (f32[40,128]{1,0:T(8,128)S(1)}, f32[40,128]{1,0:T(8,128)S(1)}, u32[]{:S(2)}, u32[]{:S(2)}) collective-permute-start(f32[40,128]{1,0:T(8,128)S(1)} %get-tuple-element.46), channel_id=1, source_target_pairs={{0,1},{1,0},{2,3},{3,2},{4,5},{5,4},{6,7},{7,6},{8,9},{9,8},{10,11... | collective-permute-start | bytes 61448 | tf_op jit(solution)/shard_map/ppermute | solution.py:52
  62.1 5.6 %collective-permute-start.6 = (f32[32,128]{1,0:T(8,128)S(1)}, f32[32,128]{1,0:T(8,128)S(1)}, u32[]{:S(2)}, u32[]{:S(2)}) collective-permute-start(f32[32,128]{1,0:T(8,128)S(1)} %get-tuple-element.54), channel_id=1, source_target_pairs={{0,3},{1,2},{2,1},{3,0},{4,7},{5,6},{6,5},{7,4},{8,11},{9,10},{10,... | collective-permute-start | bytes 49160 | tf_op jit(solution)/shard_map/ppermute | solution.py:52
  62.8 4.9 %collective-permute-start.7 = (f32[32,128]{1,0:T(8,128)S(1)}, f32[32,128]{1,0:T(8,128)S(1)}, u32[]{:S(2)}, u32[]{:S(2)}) collective-permute-start(f32[32,128]{1,0:T(8,128)S(1)} %get-tuple-element.55), channel_id=1, source_target_pairs={{0,2},{1,3},{2,0},{3,1},{4,6},{5,7},{6,4},{7,5},{8,10},{9,11},{10,... | collective-permute-start | bytes 49160 | tf_op jit(solution)/shard_map/ppermute | solution.py:52
  64.0 4.3 %collective-permute-start.8 = (f32[32,128]{1,0:T(8,128)S(1)}, f32[32,128]{1,0:T(8,128)S(1)}, u32[]{:S(2)}, u32[]{:S(2)}) collective-permute-start(f32[32,128]{1,0:T(8,128)S(1)} %get-tuple-element.56), channel_id=1, source_target_pairs={{0,1},{1,0},{2,3},{3,2},{4,5},{5,4},{6,7},{7,6},{8,9},{9,8},{10,11... | collective-permute-start | bytes 49160 | tf_op jit(solution)/shard_map/ppermute | solution.py:52
  78.5 5.6 %collective-permute-start.11 = (f32[32,128]{1,0:T(8,128)S(1)}, f32[32,128]{1,0:T(8,128)S(1)}, u32[]{:S(2)}, u32[]{:S(2)}) collective-permute-start(f32[32,128]{1,0:T(8,128)S(1)} %get-tuple-element.61.refs_0_.refs_3_), channel_id=1, source_target_pairs={{0,3},{1,2},{2,1},{3,0},{4,7},{5,6},{6,5},{7,4},{8,11},{9,10},{10,... | collective-permute-start | bytes 49160 | tf_op jit(solution)/shard_map/ppermute | solution.py:52
  79.1 5.0 %collective-permute-start.10 = (f32[32,128]{1,0:T(8,128)S(1)}, f32[32,128]{1,0:T(8,128)S(1)}, u32[]{:S(2)}, u32[]{:S(2)}) collective-permute-start(f32[32,128]{1,0:T(8,128)S(1)} %get-tuple-element.61.refs_0_.refs_3_), channel_id=1, source_target_pairs={{0,2},{1,3},{2,0},{3,1},{4,6},{5,7},{6,4},{7,5},{8,10},{9,11},{10,... | collective-permute-start | bytes 49160 | tf_op jit(solution)/shard_map/ppermute | solution.py:52
  80.5 4.2 %collective-permute-start.9 = (f32[32,128]{1,0:T(8,128)S(1)}, f32[32,128]{1,0:T(8,128)S(1)}, u32[]{:S(2)}, u32[]{:S(2)}) collective-permute-start(f32[32,128]{1,0:T(8,128)S(1)} %get-tuple-element.61.refs_0_.refs_3_), channel_id=1, source_target_pairs={{0,1},{1,0},{2,3},{3,2},{4,5},{5,4},{6,7},{7,6},{8,9},{9,8},{10,11... | collective-permute-start | bytes 49160 | tf_op jit(solution)/shard_map/ppermute | solution.py:52

commit v6 on v5

--- a/solution.py
+++ b/solution.py
@@ -16,7 +16,6 @@
 PARAMS = pltpu.CompilerParams(vmem_limit_bytes=8 * 2**20)
 WIDE = pltpu.CompilerParams(vmem_limit_bytes=63950 * 2**10)
 VMEM = pl.BlockSpec(memory_space=pltpu.VMEM)
-SMEM = pl.BlockSpec(memory_space=pltpu.SMEM)
 HBM = pl.BlockSpec(memory_space=pltpu.HBM)
 
 
@@ -53,12 +52,12 @@
     return arrived
 
 
-def three_parts(x):
+def three_parts(x, axis):
     high = x.astype(jnp.bfloat16)
     rest = x - high.astype(jnp.float32)
     middle = rest.astype(jnp.bfloat16)
     low = (rest - middle.astype(jnp.float32)).astype(jnp.bfloat16)
-    return jnp.concatenate([high, middle, low], 0)
+    return jnp.concatenate([high, middle, low], axis)
 
 
 def diagonal(rows):
@@ -74,22 +73,31 @@
     return jnp.sum(jnp.sum(x, 0, keepdims=True), 1, keepdims=True)
 
 
-def tile_sums(slots_ref, tiles_ref, vector_ref, dense_ref, picked_ref, product_ref, divisor, is_forward):
-    count = tiles_ref.shape[0]
-    limit = vector_ref.shape[0] * dense_ref.shape[0]
+def tile_sums(slots, tiles_ref, vector, product_ref, out_blocks, is_forward):
+    count, width = tiles_ref.shape[0], tiles_ref.shape[1]
+    in_blocks = vector.shape[0]
+    divisor = in_blocks if is_forward else out_blocks
+    row_blocks = out_blocks if is_forward else in_blocks
+    slots = slots.astype(jnp.float32)
+    at = lax.broadcasted_iota(jnp.int32, (count, count), 0)
+    to = lax.broadcasted_iota(jnp.int32, (count, count), 1)
+    slots = jnp.sum(jnp.where(at == to, slots, 0.0), 1, keepdims=True)
+    starts = lax.broadcasted_iota(jnp.int32, (count, row_blocks), 1) * divisor
+    passed = jnp.where(slots >= starts.astype(jnp.float32), 1.0, 0.0)
+    row = jnp.sum(passed, 1, keepdims=True) - 1.0
+    column = slots - row * divisor
+    live = slots < row_blocks * divisor
+
+    def hot(place, blocks):
+        lane = lax.broadcasted_iota(jnp.int32, (count, blocks), 1).astype(jnp.float32)
+        return jnp.where((lane == place) & live, 1.0, 0.0).astype(jnp.bfloat16)
+
+    source = hot(column if is_forward else row, in_blocks)
+    target = hot(row if is_forward else column, out_blocks)
+    picked = jnp.dot(source, three_parts(vector, 1), preferred_element_type=jnp.float32)
+    parts = [picked[:, k * width : (k + 1) * width] for k in range(3)]
+    parts = jnp.concatenate(parts, 0).astype(jnp.bfloat16)
     contract = (((1,), (1,)), ((), ())) if is_forward else (((1,), (0,)), ((), ()))
-    targets = []
-    for t in range(count):
-        slot = slots_ref[t]
-        live = slot < limit
-        slot = jnp.where(live, slot, 0)
-        row = lax.div(slot, divisor)
-        column = slot - row * divisor
-        targets.append(row if is_forward else column)
-        line = vector_ref[pl.ds(column if is_forward else row, 1), :]
-        picked_ref[pl.ds(t, 1), :] = jnp.where(live, line, 0.0)
-    parts = three_parts(picked_ref[...])
-    dense_ref[...] = jnp.zeros_like(dense_ref)
     for t in range(count):
         result = lax.dot_general(parts, tiles_ref[t], contract, preferred_element_type=jnp.float32)
         product_ref[pl.ds(t, 1), :] = (
@@ -97,9 +105,13 @@
             + result[count + t : count + t + 1]
             + result[2 * count + t : 2 * count + t + 1]
         )
-    for t in range(count):
-        line = pl.ds(targets[t], 1)
-        dense_ref[line, :] = dense_ref[line, :] + product_ref[pl.ds(t, 1), :]
+    placed = lax.dot_general(
+        target,
+        three_parts(product_ref[...], 1),
+        (((0,), (0,)), ((), ())),
+        preferred_element_type=jnp.float32,
+    )
+    return placed[:, :width] + placed[:, width : 2 * width] + placed[:, 2 * width :]
 
 
 def packed_gram(basis, total):
@@ -128,65 +140,71 @@
     return jnp.where(lane_at < 2 * half, grams, 0.0)
 
 
-def start(mine, tiles, slots, vector, basis, row_blocks, total, peers):
+def start(tiles, slots, vector, basis, row_blocks, total, peers):
     count, width = tiles.shape[0], tiles.shape[1]
-    divisor = vector.shape[0]
     kept = basis.shape[0]
     rows = row_blocks // peers
     share = kept * kept // LANES // peers
 
-    def kernel(mine_ref, slots_ref, tiles_hbm, vector_hbm, basis_hbm, *refs):
+    def kernel(slots_hbm, tiles_hbm, vector_hbm, basis_hbm, *refs):
         outs, scratch = take(refs, peers)
-        tiles_ref, vector_ref, basis_ref, dense_ref, packed_ref, picked_ref, product_ref, sems = scratch
+        slots_ref, tiles_ref, vector_ref, basis_ref, dense_ref, packed_ref, product_ref, sems = scratch
         moves = [
             pltpu.make_async_copy(source, target, sems.at[at])
             for at, (source, target) in enumerate(
-                ((vector_hbm, vector_ref), (tiles_hbm, tiles_ref), (basis_hbm, basis_ref))
+                (
+                    (slots_hbm, slots_ref),
+                    (vector_hbm, vector_ref),
+                    (tiles_hbm, tiles_ref),
+                    (basis_hbm, basis_ref),
+                )
             )
         ]
         for move in moves:
             move.start()
-        moves[0].wait()
-        moves[1].wait()
-        tile_sums(slots_ref, tiles_ref, vector_ref, dense_ref, picked_ref, product_ref, divisor, True)
-        moves[2].wait()
+        for move in moves[:3]:
+            move.wait()
+        dense_ref[...] = tile_sums(
+            slots_ref[...], tiles_ref, vector_ref[...], product_ref, row_blocks, True
+        )
+        moves[3].wait()
         upper, lower = packed_gram(basis_ref[...], total)
         packed_ref[:, :kept] = upper
         packed_ref[:, kept:] = lower
         for x, out in enumerate(outs):
-            peer = jnp.bitwise_xor(mine_ref[0], x)
+            peer = jnp.bitwise_xor(lax.axis_index("col"), x)
             out[:rows, :] = dense_ref[pl.ds(peer * rows, rows), :]
             out[rows:, :] = packed_ref[pl.ds(peer * share, share), :]
 
     scratch = [
+        pltpu.VMEM(slots.shape, slots.dtype),
         pltpu.VMEM(tiles.shape, tiles.dtype),
         pltpu.VMEM(vector.shape, jnp.float32),
         pltpu.VMEM(basis.shape, jnp.float32),
         pltpu.VMEM((row_blocks, width), jnp.float32),
         pltpu.VMEM((kept // 2, 2 * kept), jnp.float32),
         pltpu.VMEM((count, width), jnp.float32),
-        pltpu.VMEM((count, width), jnp.float32),
-        pltpu.SemaphoreType.DMA((3,)),
+        pltpu.SemaphoreType.DMA((4,)),
     ]
     return call(
         kernel,
         [(rows + share, width)] * peers,
-        [mine, slots, tiles, vector, basis],
-        [SMEM, SMEM, HBM, HBM, HBM],
+        [slots, tiles, vector, basis],
+        [HBM] * 4,
         scratch,
         WIDE,
     )
 
 
-def right_start(mine_row, v_basis, vector, after, total):
+def right_start(v_basis, vector, after, total):
     kept, _, length = v_basis.shape
     rows = length // LANES
 
-    def kernel(mine_ref, basis_ref, vector_ref, after_ref, flat_ref, piece_ref, row_ref, packed_ref):
+    def kernel(basis_ref, vector_ref, after_ref, flat_ref, piece_ref, row_ref, packed_ref):
         for k in range(rows):
             at = slice(k * LANES, (k + 1) * LANES)
             flat_ref[:, at] = basis_ref[:, 0, at]
-        piece = vector_ref[pl.ds(mine_ref[0] * rows, rows), :]
+        piece = vector_ref[pl.ds(lax.axis_index("row") * rows, rows), :]
         piece_ref[...] = piece
         row_ref[...] = basis_products(piece, flat_ref, [piece])
         upper, lower = packed_gram(flat_ref[...], total)
@@ -196,35 +214,35 @@
     return call(
         kernel,
         [(kept, length), (rows, LANES), (1, LANES), (kept // 2, 2 * kept)],
-        [mine_row, v_basis, vector, after],
-        [SMEM, VMEM, VMEM, VMEM],
-    )
-
-
-def forward_messages(mine, tiles, slots, vector, row_blocks, peers):
+        [v_basis, vector, after],
+    )
+
+
+def forward_messages(tiles, slots, vector, row_blocks, peers):
     count, width = tiles.shape[0], tiles.shape[1]
-    divisor = vector.shape[0]
     rows = row_blocks // peers
 
-    def kernel(mine_ref, slots_ref, tiles_ref, vector_ref, *refs):
-        outs, (dense_ref, picked_ref, product_ref) = take(refs, peers)
-        tile_sums(slots_ref, tiles_ref, vector_ref, dense_ref, picked_ref, product_ref, divisor, True)
+    def kernel(slots_ref, tiles_ref, vector_ref, *refs):
+        outs, (dense_ref, product_ref) = take(refs, peers)
+        dense_ref[...] = tile_sums(
+            slots_ref[...], tiles_ref, vector_ref[...], product_ref, row_blocks, True
+        )
         for x, out in enumerate(outs):
-            peer = jnp.bitwise_xor(mine_ref[0], x)
+            peer = jnp.bitwise_xor(lax.axis_index("col"), x)
             out[...] = dense_ref[pl.ds(peer * rows, rows), :]
 
     scratch = [pltpu.VMEM((row_blocks, width), jnp.float32)]
-    scratch += [pltpu.VMEM((count, width), jnp.float32)] * 2
+    scratch += [pltpu.VMEM((count, width), jnp.float32)]
     return call(
         kernel,
         [(rows, width)] * peers,
-        [mine, slots, tiles, vector],
-        [SMEM, SMEM, VMEM, VMEM],
+        [slots, tiles, vector],
+        None,
         scratch,
     )
 
 
-def backward_product(mine, tiles, slots, messages, hops, rows, col_blocks, peers_row):
+def backward_product(tiles, slots, messages, hops, rows, col_blocks, peers_row):
     count, width = tiles.shape[0], tiles.shape[1]
     peers = len(messages)
     share = messages[0].shape[0] - rows
@@ -232,18 +250,18 @@
     joined = share // peers_row if share % peers_row == 0 else 0
     apart = share and not joined
 
-    def kernel(mine_ref, slots_ref, tiles_ref, *refs):
+    def kernel(slots_ref, tiles_ref, *refs):
         sources, rest = take(refs, peers)
         (chunks_ref,), apart_refs, scratch = take(rest, 1, 1 if apart else 0)
-        vector_ref, dense_ref, picked_ref, product_ref = scratch
+        vector_ref, product_ref = scratch
         for at, source in enumerate(sources):
-            peer = jnp.bitwise_xor(mine_ref[0], ([0] + hops)[at])
+            peer = jnp.bitwise_xor(lax.axis_index("col"), ([0] + hops)[at])
             vector_ref[pl.ds(peer * rows, rows), :] = source[:rows, :]
-        tile_sums(
-            slots_ref, tiles_ref, vector_ref, dense_ref, picked_ref, product_ref, col_blocks, False
+        dense = tile_sums(
+            slots_ref[...], tiles_ref, vector_ref[...], product_ref, col_blocks, False
         )
         for i in range(peers_row):
-            chunks_ref[i, :chunk, :] = dense_ref[i * chunk : (i + 1) * chunk, :]
+            chunks_ref[i, :chunk, :] = dense[i * chunk : (i + 1) * chunk, :]
         if share:
             added = sources[0][rows:, :]
             for source in sources[1:]:
@@ -255,14 +273,13 @@
                     chunks_ref[i, chunk:, :] = added[i * joined : (i + 1) * joined]
 
     scratch = [pltpu.VMEM((rows * peers, width), jnp.float32)]
-    scratch += [pltpu.VMEM((col_blocks, width), jnp.float32)]
-    scratch += [pltpu.VMEM((count, width), jnp.float32)] * 2
+    scratch += [pltpu.VMEM((count, width), jnp.float32)]
     outs = [(peers_row, chunk + joined, width)] + ([(share, width)] if apart else [])
     return call(
         kernel,
         outs,
-        [mine, slots, tiles, *messages],
-        [SMEM, SMEM] + [VMEM] * (1 + peers),
+        [slots, tiles, *messages],
+        None,
         scratch,
     )
 
@@ -338,13 +355,13 @@
             packed_ref[peer * share + k : peer * share + k + 1, :] = added[peer : peer + 1]
 
 
-def first_vector(mine, received, piece, basis, right_packed, total, peers):
+def first_vector(received, piece, basis, right_packed, total, peers):
     kept = basis.shape[0]
     rows = piece.shape[0]
     padded = kept + GROUP
     share = right_packed.shape[0] // peers
 
-    def kernel(mine_ref, received_ref, piece_ref, basis_ref, right_ref, *refs):
+    def kernel(received_ref, piece_ref, basis_ref, right_ref, *refs):
         messages, (unit_ref, gram_ref, scale_ref, packed_ref) = take(refs, peers)
         received_gram(received_ref, 1, packed_ref, peers)
         products = unpacked_gram(packed_ref[...], padded)
@@ -356,7 +373,7 @@
             for message in messages:
                 message[pl.ds(k, 1), :] = line
         for x, message in enumerate(messages):
-            peer = jnp.bitwise_xor(mine_ref[0], x)
+            peer = jnp.bitwise_xor(lax.axis_index("col"), x)
             message[rows:, :] = right_ref[pl.ds(peer * share, share), :]
         gram_ref[...] = wider_gram(products, kept, remaining, squared, inverse)
         scale_ref[...] = jnp.broadcast_to(scale, scale_ref.shape)
@@ -365,8 +382,8 @@
     return call(
         kernel,
         outs,
-        [mine, received, piece, basis, right_packed],
-        [SMEM] + [VMEM] * 4,
+        [received, piece, basis, right_packed],
+        None,
         [pltpu.VMEM(right_packed.shape, jnp.float32)],
     )
 
@@ -484,7 +501,7 @@
 
 def shards(tiles, tile_index, u_basis, v_basis, v_start):
     blocks = tiles[0]
-    slots = tile_index[0]
+    slots = tile_index
     width = blocks.shape[1]
     cols_len = v_start.shape[0]
     col_blocks = cols_len // width
@@ -499,16 +516,14 @@
     right_rows = right_piece // width
     total_left = rows_len * row_count
     total_right = cols_len * col_count
-    mine = lax.axis_index("col").reshape(1)
-    mine_row = lax.axis_index("row").reshape(1)
-    far_first = list(range(col_count - 1, 0, -1))
+    hop_order = list(range(2, col_count)) + [1]
 
     whole_start = v_start.reshape(col_blocks, width)
-    messages = start(mine, blocks, slots, whole_start, u_basis, row_blocks, total_left, col_count)
+    messages = start(blocks, slots, whole_start, u_basis, row_blocks, total_left, col_count)
     right_basis, start_share, start_row, right_packed = right_start(
-        mine_row, v_basis, whole_start, messages[0], total_right
-    )
-    arrived = exchange(messages, far_first, "col")
+        v_basis, whole_start, messages[0], total_right
+    )
+    arrived = exchange(messages, hop_order, "col")
 
     lefts, rights, scales = ([], [], [])
     right_extras = [start_share]
@@ -520,7 +535,7 @@
         summed_rows = swap(sent, BOTH)
         if iteration == 0:
             *messages, left_unit, left_gram, alpha = first_vector(
-                mine, summed_rows, piece, u_basis, right_packed, total_left, col_count
+                summed_rows, piece, u_basis, right_packed, total_left, col_count
             )
         else:
             left_unit, alpha, *wider = new_vector(
@@ -530,10 +545,10 @@
             messages = [left_unit] * col_count
         lefts = lefts + [left_unit]
         scales = scales + [alpha]
-        hops = far_first if iteration == 0 else far_first[::-1]
+        hops = hop_order if iteration == 0 else hop_order[::-1]
         arrived = exchange(messages, hops, "col")
         chunks, *further = backward_product(
-            mine, blocks, slots, arrived, hops, left_rows, col_blocks, row_count
+            blocks, slots, arrived, hops, left_rows, col_blocks, row_count
         )
         received = swap(chunks, "row")
         riders = [start_row, *further] if iteration == 0 else []
@@ -555,8 +570,8 @@
             right_extras = right_extras + [right_unit]
             scales = scales + [beta]
             joined = swap(copies, "row").reshape(col_blocks, width)
-            messages = forward_messages(mine, blocks, slots, joined, row_blocks, col_count)
-            arrived = exchange(messages, far_first, "col")
+            messages = forward_messages(blocks, slots, joined, row_blocks, col_count)
+            arrived = exchange(messages, hop_order, "col")
     return last_vector(
         summed_rows, right_gram, piece, right_basis, right_extras, total_right, lefts, rights, scales
     )

time: 104 us -> 102 us (0.981)
  waiting for transfers between devices: 6.98 us -> 10.2 us
  starting transfers between devices: 19.1 us -> 16.4 us
  blocking collectives: 64.4 us -> 63 us
    ppermute x12, waiting for transfers between devices: 6.98 us -> 10.2 us  [exchange(): lax.ppermute(messages[x], axis, [(i, i ^ x) for i in range(count)])]
    ppermute x12, starting transfers between devices: 19.1 us -> 16.4 us  [exchange(): lax.ppermute(messages[x], axis, [(i, i ^ x) for i in range(count)])]
    all_to_all x7, blocking collectives: 64.4 us -> 63 us  [swap(): return lax.all_to_all(chunks, axis, 0, 0, tiled=True)]
  transfers between devices with their start and end apart: 12 -> 12, of which waited for: 8 -> 9; matrix products, arithmetic and copies ran while one was open for 0% -> 0% of each run, Pallas kernels for 1% -> 1%
where the time goes in v6:
time: 102 us
  blocking collectives  63 us (62%)
  starting transfers between devices  16.4 us (16%)
  waiting for transfers between devices  10.2 us (10%)
  Pallas kernels  9.68 us (9%)
  local copies, waits for them, and re-layouts  1.78 us (2%)
    all_to_all x7, blocking collectives, swap(): return lax.all_to_all(chunks, axis, 0, 0, tiled=True)  63 us
    ppermute x12, starting transfers between devices, exchange(): lax.ppermute(messages[x], axis, [(i, i ^ x) for i in range(count)])  16.4 us
    ppermute x12, waiting for transfers between devices, exchange(): lax.ppermute(messages[x], axis, [(i, i ^ x) for i in range(count)])  10.2 us
    pallas_call x13, Pallas kernels, call(): pl.pallas_call(kernel, out_shape=shapes, in_specs=specs or [VMEM] * len(a...  9.68 us
  transfers between devices with their start and end apart: 12, of which 9 were waited for; matrix products, arithmetic and copies ran while one was open for 0% of the time, Pallas kernels for 1%

profile of v6, /device:TPU:0, one launch (start us, length us, event | category | flops | bytes accessed | tf_op | source)
XLA Modules:
  0.0 101.7 jit_solution(4300400627832145593)
XLA Ops:
  0.7 4.2 %shard_map.76 = (f32[40,128]{1,0:T(8,128)}, f32[40,128]{1,0:T(8,128)}, f32[40,128]{1,0:T(8,128)}, f32[40,128]{1,0:T(8,128)}) custom-call(s32[1,16]{1,0:T(1,128)} %slots_ref.5, bf16[16,128,128]{2,1,0:T(8,128)(2,1)} %bitcast.3, f32[128,128]{1,0:T(8,128)} %bitcast.7, f32[64,4096]{1,0:T(8,128)} %basis_ref.5), custom_call_target="tpu_custom_call" | custom-call | tf_op jit(solution)/shard_map/pallas_call | solution.py:28
  4.9 4.1 %collective-permute-start = (f32[40,128]{1,0:T(8,128)}, f32[40,128]{1,0:T(8,128)S(1)}, u32[]{:S(2)}, u32[]{:S(2)}) collective-permute-start(f32[40,128]{1,0:T(8,128)} %get-tuple-element.37), channel_id=1, source_target_pairs={{0,2},{1,3},{2,0},{3,1},{4,6},{5,7},{6,4},{7,5},{8,10},{9,11},{10,... | collective-permute-start | bytes 61448 | tf_op jit(solution)/shard_map/ppermute | solution.py:51
  9.0 1.3 %collective-permute-start.1 = (f32[40,128]{1,0:T(8,128)}, f32[40,128]{1,0:T(8,128)S(1)}, u32[]{:S(2)}, u32[]{:S(2)}) collective-permute-start(f32[40,128]{1,0:T(8,128)} %get-tuple-element.38), channel_id=1, source_target_pairs={{0,3},{1,2},{2,1},{3,0},{4,7},{5,6},{6,5},{7,4},{8,11},{9,10},{10,... | collective-permute-start | bytes 61448 | tf_op jit(solution)/shard_map/ppermute | solution.py:51
  10.6 1.0 %copy-done.2 = f32[64,1,2048]{2,1,0:T(1,128)S(1)} copy-done((f32[64,1,2048]{2,1,0:T(1,128)S(1)}, f32[64,1,2048]{2,1,0:T(1,128)}, u32[]{:S(2)}) %copy-start.2) | copy-done | bytes 524312
  11.7 0.7 copy-done.4
  12.4 0.7 shard_map.77
  13.1 1.7 %collective-permute-done.1.refs_2_ = f32[40,128]{1,0:T(8,128)S(1)} collective-permute-done((f32[40,128]{1,0:T(8,128)}, f32[40,128]{1,0:T(8,128)S(1)}, u32[]{:S(2)}, u32[]{:S(2)}) %collective-permute-start.1) | collective-permute-done | bytes 20512 | tf_op jit(solution)/shard_map/ppermute | solution.py:51
  15.0 12.7 %all_to_all.35.received_ref = f32[32,1,1152]{2,1,0:T(1,128)S(1)} all-to-all(f32[32,1,1152]{2,1,0:T(1,128)S(1)} %get-tuple-element.41), channel_id=1, replica_groups=mesh['row'=8,'col'=4] {'row','col'}, dimensions={0} | all-to-all | bytes 294912 | tf_op jit(solution)/shard_map/all_to_all | solution.py:23
  28.5 1.4 %collective-permute-start.4 = (f32[40,128]{1,0:T(8,128)S(1)}, f32[40,128]{1,0:T(8,128)S(1)}, u32[]{:S(2)}, u32[]{:S(2)}) collective-permute-start(f32[40,128]{1,0:T(8,128)S(1)} %get-tuple-element.45), channel_id=1, source_target_pairs={{0,3},{1,2},{2,1},{3,0},{4,7},{5,6},{6,5},{7,4},{8,11},{9,10},{10,... | collective-permute-start | bytes 61448 | tf_op jit(solution)/shard_map/ppermute | solution.py:51
  29.9 1.8 %collective-permute-start.5 = (f32[40,128]{1,0:T(8,128)S(1)}, f32[40,128]{1,0:T(8,128)S(1)}, u32[]{:S(2)}, u32[]{:S(2)}) collective-permute-start(f32[40,128]{1,0:T(8,128)S(1)} %get-tuple-element.46), channel_id=1, source_target_pairs={{0,1},{1,0},{2,3},{3,2},{4,5},{5,4},{6,7},{7,6},{8,9},{9,8},{10,11... | collective-permute-start | bytes 61448 | tf_op jit(solution)/shard_map/ppermute | solution.py:51
  31.7 1.4 %collective-permute-done.3.refs_1_ = f32[40,128]{1,0:T(8,128)S(1)} collective-permute-done((f32[40,128]{1,0:T(8,128)S(1)}, f32[40,128]{1,0:T(8,128)S(1)}, u32[]{:S(2)}, u32[]{:S(2)}) %collective-permute-start.3) | collective-permute-done | bytes 20512 | tf_op jit(solution)/shard_map/ppermute | solution.py:51
  33.1 1.0 collective-permute-done.4.refs_2_
  34.1 0.7 shard_map.80
  34.8 7.6 %all_to_all.36.refs_0_ = f32[8,17,128]{2,1,0:T(8,128)S(1)} all-to-all(f32[8,17,128]{2,1,0:T(8,128)S(1)} %shard_map.80), channel_id=1, replica_groups=mesh['row'=8,'col'=4] {'row'}, dimensions={0} | all-to-all | bytes 139264 | tf_op jit(solution)/shard_map/all_to_all | solution.py:23
  42.5 9.6 %all_to_all.37.received_ref = f32[32,1,384]{2,1,0:T(1,128)S(1)} all-to-all(f32[32,1,384]{2,1,0:T(1,128)S(1)} %get-tuple-element.50), channel_id=1, replica_groups=mesh['row'=8,'col'=4] {'row','col'}, dimensions={0} | all-to-all | bytes 98304 | tf_op jit(solution)/shard_map/all_to_all | solution.py:23
  52.5 7.4 %all_to_all.38 = f32[8,16,128]{2,1,0:T(8,128)S(1)} all-to-all(f32[8,16,128]{2,1,0:T(8,128)S(1)} %get-tuple-element.52), channel_id=1, replica_groups=mesh['row'=8,'col'=4] {'row'}, dimensions={0} | all-to-all | bytes 131072 | tf_op jit(solution)/shard_map/all_to_all | solution.py:23
  59.9 0.8 shard_map.83
  60.7 0.5 collective-permute-start.6
  61.2 2.2 %collective-permute-start.7 = (f32[32,128]{1,0:T(8,128)S(1)}, f32[32,128]{1,0:T(8,128)S(1)}, u32[]{:S(2)}, u32[]{:S(2)}) collective-permute-start(f32[32,128]{1,0:T(8,128)S(1)} %get-tuple-element.55), channel_id=1, source_target_pairs={{0,3},{1,2},{2,1},{3,0},{4,7},{5,6},{6,5},{7,4},{8,11},{9,10},{10,... | collective-permute-start | bytes 49160 | tf_op jit(solution)/shard_map/ppermute | solution.py:51
  63.4 0.8 collective-permute-start.8
  64.2 1.3 %collective-permute-done.6.refs_1_ = f32[32,128]{1,0:T(8,128)S(1)} collective-permute-done((f32[32,128]{1,0:T(8,128)S(1)}, f32[32,128]{1,0:T(8,128)S(1)}, u32[]{:S(2)}, u32[]{:S(2)}) %collective-permute-start.6) | collective-permute-done | bytes 16416 | tf_op jit(solution)/shard_map/ppermute | solution.py:51
  65.6 1.2 %collective-permute-done.7.refs_2_ = f32[32,128]{1,0:T(8,128)S(1)} collective-permute-done((f32[32,128]{1,0:T(8,128)S(1)}, f32[32,128]{1,0:T(8,128)S(1)}, u32[]{:S(2)}, u32[]{:S(2)}) %collective-permute-start.7) | collective-permute-done | bytes 16416 | tf_op jit(solution)/shard_map/ppermute | solution.py:51
  67.4 9.2 %all_to_all.39.received_ref = f32[32,1,128]{2,1,0:T(1,128)S(1)} all-to-all(f32[32,1,128]{2,1,0:T(1,128)S(1)} %get-tuple-element.58), channel_id=1, replica_groups=mesh['row'=8,'col'=4] {'row','col'}, dimensions={0} | all-to-all | bytes 32768 | tf_op jit(solution)/shard_map/all_to_all | solution.py:23
  76.8 0.6 collective-permute-start.11
  77.4 2.3 %collective-permute-start.10 = (f32[32,128]{1,0:T(8,128)S(1)}, f32[32,128]{1,0:T(8,128)S(1)}, u32[]{:S(2)}, u32[]{:S(2)}) collective-permute-start(f32[32,128]{1,0:T(8,128)S(1)} %get-tuple-element.61.refs_0_.refs_3_), channel_id=1, source_target_pairs={{0,3},{1,2},{2,1},{3,0},{4,7},{5,6},{6,5},{7,4},{8,11},{9,10},{10,... | collective-permute-start | bytes 49160 | tf_op jit(solution)/shard_map/ppermute | solution.py:51
  79.7 0.6 collective-permute-start.9
  80.3 1.4 %collective-permute-done.11.refs_3_ = f32[32,128]{1,0:T(8,128)S(1)} collective-permute-done((f32[32,128]{1,0:T(8,128)S(1)}, f32[32,128]{1,0:T(8,128)S(1)}, u32[]{:S(2)}, u32[]{:S(2)}) %collective-permute-start.11) | collective-permute-done | bytes 16416 | tf_op jit(solution)/shard_map/ppermute | solution.py:51
  81.8 1.2 %collective-permute-done.10.refs_2_ = f32[32,128]{1,0:T(8,128)S(1)} collective-permute-done((f32[32,128]{1,0:T(8,128)S(1)}, f32[32,128]{1,0:T(8,128)S(1)}, u32[]{:S(2)}, u32[]{:S(2)}) %collective-permute-start.10) | collective-permute-done | bytes 16416 | tf_op jit(solution)/shard_map/ppermute | solution.py:51
  83.4 0.7 shard_map.86
  84.1 7.4 %all_to_all.40.refs_0_ = f32[8,16,128]{2,1,0:T(8,128)S(1)} all-to-all(f32[8,16,128]{2,1,0:T(8,128)S(1)} %shard_map.86), channel_id=1, replica_groups=mesh['row'=8,'col'=4] {'row'}, dimensions={0} | all-to-all | bytes 131072 | tf_op jit(solution)/shard_map/all_to_all | solution.py:23
  91.7 9.2 %all_to_all.41.received_ref = f32[32,1,128]{2,1,0:T(1,128)S(1)} all-to-all(f32[32,1,128]{2,1,0:T(1,128)S(1)} %get-tuple-element.63), channel_id=1, replica_groups=mesh['row'=8,'col'=4] {'row','col'}, dimensions={0} | all-to-all | bytes 32768 | tf_op jit(solution)/shard_map/all_to_all | solution.py:23
  100.9 0.9 shard_map.88
  (24 shorter events, 3.2 us)
Async XLA Ops:
  0.6 10.0 %copy-start.3 = (f32[16384]{0:T(1024)S(1)}, f32[16384]{0:T(1024)}, u32[]{:S(2)}) copy-start(f32[16384]{0:T(1024)} %param.9) | copy-start | bytes 196612
  0.6 14.2 %copy-start = (f32[64,4096]{1,0:T(8,128)S(1)}, f32[64,4096]{1,0:T(8,128)}, u32[]{:S(2)}) copy-start(f32[64,4096]{1,0:T(8,128)} %basis_ref.5) | copy-start | bytes 3145732
  4.9 8.2 %collective-permute-start = (f32[40,128]{1,0:T(8,128)}, f32[40,128]{1,0:T(8,128)S(1)}, u32[]{:S(2)}, u32[]{:S(2)}) collective-permute-start(f32[40,128]{1,0:T(8,128)} %get-tuple-element.37), channel_id=1, source_target_pairs={{0,2},{1,3},{2,0},{3,1},{4,6},{5,7},{6,4},{7,5},{8,10},{9,11},{10,... | collective-permute-start | bytes 61448 | tf_op jit(solution)/shard_map/ppermute | solution.py:51
  9.0 5.8 %collective-permute-start.1 = (f32[40,128]{1,0:T(8,128)}, f32[40,128]{1,0:T(8,128)S(1)}, u32[]{:S(2)}, u32[]{:S(2)}) collective-permute-start(f32[40,128]{1,0:T(8,128)} %get-tuple-element.38), channel_id=1, source_target_pairs={{0,3},{1,2},{2,1},{3,0},{4,7},{5,6},{6,5},{7,4},{8,11},{9,10},{10,... | collective-permute-start | bytes 61448 | tf_op jit(solution)/shard_map/ppermute | solution.py:51
  10.4 4.4 %collective-permute-start.2 = (f32[40,128]{1,0:T(8,128)}, f32[40,128]{1,0:T(8,128)S(1)}, u32[]{:S(2)}, u32[]{:S(2)}) collective-permute-start(f32[40,128]{1,0:T(8,128)} %get-tuple-element.39), channel_id=1, source_target_pairs={{0,1},{1,0},{2,3},{3,2},{4,5},{5,4},{6,7},{7,6},{8,9},{9,8},{10,11... | collective-permute-start | bytes 61448 | tf_op jit(solution)/shard_map/ppermute | solution.py:51
  10.6 1.0 %copy-start.2 = (f32[64,1,2048]{2,1,0:T(1,128)S(1)}, f32[64,1,2048]{2,1,0:T(1,128)}, u32[]{:S(2)}) copy-start(f32[64,1,2048]{2,1,0:T(1,128)} %basis_ref.3) | copy-start | bytes 1572868
  11.6 0.7 copy-start.4
  27.7 6.4 %copy-start.1 = (bf16[1,16,128,128]{3,2,1,0:T(8,128)(2,1)S(1)}, bf16[1,16,128,128]{3,2,1,0:T(8,128)(2,1)}, u32[]{:S(2)}) copy-start(bf16[1,16,128,128]{3,2,1,0:T(8,128)(2,1)} %param.5) | copy-start | bytes 1572868
  28.1 5.0 %collective-permute-start.3 = (f32[40,128]{1,0:T(8,128)S(1)}, f32[40,128]{1,0:T(8,128)S(1)}, u32[]{:S(2)}, u32[]{:S(2)}) collective-permute-start(f32[40,128]{1,0:T(8,128)S(1)} %get-tuple-element.44), channel_id=1, source_target_pairs={{0,2},{1,3},{2,0},{3,1},{4,6},{5,7},{6,4},{7,5},{8,10},{9,11},{10,... | collective-permute-start | bytes 61448 | tf_op jit(solution)/shard_map/ppermute | solution.py:51
  28.5 5.6 %collective-permute-start.4 = (f32[40,128]{1,0:T(8,128)S(1)}, f32[40,128]{1,0:T(8,128)S(1)}, u32[]{:S(2)}, u32[]{:S(2)}) collective-permute-start(f32[40,128]{1,0:T(8,128)S(1)} %get-tuple-element.45), channel_id=1, source_target_pairs={{0,3},{1,2},{2,1},{3,0},{4,7},{5,6},{6,5},{7,4},{8,11},{9,10},{10,... | collective-permute-start | bytes 61448 | tf_op jit(solution)/shard_map/ppermute | solution.py:51
  29.9 4.2 %copy-start.5 = (s32[1,16]{1,0:T(1,128)S(1)}, s32[1,16]{1,0:T(1,128)}, u32[]{:S(2)}) copy-start(s32[1,16]{1,0:T(1,128)} %slots_ref.5) | copy-start | bytes 196
  29.9 4.2 %collective-permute-start.5 = (f32[40,128]{1,0:T(8,128)S(1)}, f32[40,128]{1,0:T(8,128)S(1)}, u32[]{:S(2)}, u32[]{:S(2)}) collective-permute-start(f32[40,128]{1,0:T(8,128)S(1)} %get-tuple-element.46), channel_id=1, source_target_pairs={{0,1},{1,0},{2,3},{3,2},{4,5},{5,4},{6,7},{7,6},{8,9},{9,8},{10,11... | collective-permute-start | bytes 61448 | tf_op jit(solution)/shard_map/ppermute | solution.py:51
  60.7 4.9 %collective-permute-start.6 = (f32[32,128]{1,0:T(8,128)S(1)}, f32[32,128]{1,0:T(8,128)S(1)}, u32[]{:S(2)}, u32[]{:S(2)}) collective-permute-start(f32[32,128]{1,0:T(8,128)S(1)} %get-tuple-element.54), channel_id=1, source_target_pairs={{0,2},{1,3},{2,0},{3,1},{4,6},{5,7},{6,4},{7,5},{8,10},{9,11},{10,... | collective-permute-start | bytes 49160 | tf_op jit(solution)/shard_map/ppermute | solution.py:51
  61.2 5.5 %collective-permute-start.7 = (f32[32,128]{1,0:T(8,128)S(1)}, f32[32,128]{1,0:T(8,128)S(1)}, u32[]{:S(2)}, u32[]{:S(2)}) collective-permute-start(f32[32,128]{1,0:T(8,128)S(1)} %get-tuple-element.55), channel_id=1, source_target_pairs={{0,3},{1,2},{2,1},{3,0},{4,7},{5,6},{6,5},{7,4},{8,11},{9,10},{10,... | collective-permute-start | bytes 49160 | tf_op jit(solution)/shard_map/ppermute | solution.py:51
  63.4 3.7 %collective-permute-start.8 = (f32[32,128]{1,0:T(8,128)S(1)}, f32[32,128]{1,0:T(8,128)S(1)}, u32[]{:S(2)}, u32[]{:S(2)}) collective-permute-start(f32[32,128]{1,0:T(8,128)S(1)} %get-tuple-element.56), channel_id=1, source_target_pairs={{0,1},{1,0},{2,3},{3,2},{4,5},{5,4},{6,7},{7,6},{8,9},{9,8},{10,11... | collective-permute-start | bytes 49160 | tf_op jit(solution)/shard_map/ppermute | solution.py:51
  76.8 5.0 %collective-permute-start.11 = (f32[32,128]{1,0:T(8,128)S(1)}, f32[32,128]{1,0:T(8,128)S(1)}, u32[]{:S(2)}, u32[]{:S(2)}) collective-permute-start(f32[32,128]{1,0:T(8,128)S(1)} %get-tuple-element.61.refs_0_.refs_3_), channel_id=1, source_target_pairs={{0,2},{1,3},{2,0},{3,1},{4,6},{5,7},{6,4},{7,5},{8,10},{9,11},{10,... | collective-permute-start | bytes 49160 | tf_op jit(solution)/shard_map/ppermute | solution.py:51
  77.4 5.5 %collective-permute-start.10 = (f32[32,128]{1,0:T(8,128)S(1)}, f32[32,128]{1,0:T(8,128)S(1)}, u32[]{:S(2)}, u32[]{:S(2)}) collective-permute-start(f32[32,128]{1,0:T(8,128)S(1)} %get-tuple-element.61.refs_0_.refs_3_), channel_id=1, source_target_pairs={{0,3},{1,2},{2,1},{3,0},{4,7},{5,6},{6,5},{7,4},{8,11},{9,10},{10,... | collective-permute-start | bytes 49160 | tf_op jit(solution)/shard_map/ppermute | solution.py:51
  79.7 3.7 %collective-permute-start.9 = (f32[32,128]{1,0:T(8,128)S(1)}, f32[32,128]{1,0:T(8,128)S(1)}, u32[]{:S(2)}, u32[]{:S(2)}) collective-permute-start(f32[32,128]{1,0:T(8,128)S(1)} %get-tuple-element.61.refs_0_.refs_3_), channel_id=1, source_target_pairs={{0,1},{1,0},{2,3},{3,2},{4,5},{5,4},{6,7},{7,6},{8,9},{9,8},{10,11... | collective-permute-start | bytes 49160 | tf_op jit(solution)/shard_map/ppermute | solution.py:51

commit v7 on v6

--- a/solution.py
+++ b/solution.py
@@ -73,7 +73,7 @@
     return jnp.sum(jnp.sum(x, 0, keepdims=True), 1, keepdims=True)
 
 
-def tile_sums(slots, tiles_ref, vector, product_ref, out_blocks, is_forward):
+def tile_sums(slots, tiles_ref, vector, out_blocks, is_forward):
     count, width = tiles_ref.shape[0], tiles_ref.shape[1]
     in_blocks = vector.shape[0]
     divisor = in_blocks if is_forward else out_blocks
@@ -95,19 +95,24 @@
     source = hot(column if is_forward else row, in_blocks)
     target = hot(row if is_forward else column, out_blocks)
     picked = jnp.dot(source, three_parts(vector, 1), preferred_element_type=jnp.float32)
-    parts = [picked[:, k * width : (k + 1) * width] for k in range(3)]
-    parts = jnp.concatenate(parts, 0).astype(jnp.bfloat16)
-    contract = (((1,), (1,)), ((), ())) if is_forward else (((1,), (0,)), ((), ()))
-    for t in range(count):
-        result = lax.dot_general(parts, tiles_ref[t], contract, preferred_element_type=jnp.float32)
-        product_ref[pl.ds(t, 1), :] = (
-            result[t : t + 1]
-            + result[count + t : count + t + 1]
-            + result[2 * count + t : 2 * count + t + 1]
-        )
+    own = lax.broadcasted_iota(jnp.int32, (count, width), 0)
+    spread = []
+    for k in range(3):
+        part = picked[:, k * width : (k + 1) * width]
+        blocks = [jnp.where(own == t, part, 0.0) for t in range(count)]
+        spread.append(jnp.concatenate(blocks, 1))
+    spread = jnp.concatenate(spread, 0).astype(jnp.bfloat16)
+    if is_forward:
+        flat = jnp.concatenate([tiles_ref[t] for t in range(count)], 1)
+        contract = (((1,), (1,)), ((), ()))
+    else:
+        flat = tiles_ref[...].reshape(count * width, width)
+        contract = (((1,), (0,)), ((), ()))
+    result = lax.dot_general(spread, flat, contract, preferred_element_type=jnp.float32)
+    product = result[:count] + result[count : 2 * count] + result[2 * count :]
     placed = lax.dot_general(
         target,
-        three_parts(product_ref[...], 1),
+        three_parts(product, 1),
         (((0,), (0,)), ((), ())),
         preferred_element_type=jnp.float32,
     )
@@ -115,14 +120,18 @@
 
 
 def packed_gram(basis, total):
-    gram = lax.dot_general(
-        basis,
-        basis,
-        (((1,), (1,)), ((), ())),
-        precision=HIGHEST,
-        preferred_element_type=jnp.float32,
-    )
-    half = gram.shape[0] // 2
+    kept = basis.shape[0]
+    contract = (((1,), (1,)), ((), ()))
+    parts = three_parts(basis, 0)
+    high = lax.dot_general(
+        parts, parts[:kept], contract, preferred_element_type=jnp.float32
+    )
+    middle = lax.dot_general(
+        parts[kept : 2 * kept], parts[kept : 2 * kept], contract, preferred_element_type=jnp.float32
+    )
+    cross = high[kept : 2 * kept] + high[2 * kept :]
+    gram = high[:kept] + middle + cross + jnp.transpose(cross)
+    half = kept // 2
     return gram[:half] * (1.0 / total), gram[half:] * (1.0 / total)
 
 
@@ -148,7 +157,7 @@
 
     def kernel(slots_hbm, tiles_hbm, vector_hbm, basis_hbm, *refs):
         outs, scratch = take(refs, peers)
-        slots_ref, tiles_ref, vector_ref, basis_ref, dense_ref, packed_ref, product_ref, sems = scratch
+        slots_ref, tiles_ref, vector_ref, basis_ref, dense_ref, packed_ref, sems = scratch
         moves = [
             pltpu.make_async_copy(source, target, sems.at[at])
             for at, (source, target) in enumerate(
@@ -165,7 +174,7 @@
         for move in moves[:3]:
             move.wait()
         dense_ref[...] = tile_sums(
-            slots_ref[...], tiles_ref, vector_ref[...], product_ref, row_blocks, True
+            slots_ref[...], tiles_ref, vector_ref[...], row_blocks, True
         )
         moves[3].wait()
         upper, lower = packed_gram(basis_ref[...], total)
@@ -183,7 +192,6 @@
         pltpu.VMEM(basis.shape, jnp.float32),
         pltpu.VMEM((row_blocks, width), jnp.float32),
         pltpu.VMEM((kept // 2, 2 * kept), jnp.float32),
-        pltpu.VMEM((count, width), jnp.float32),
         pltpu.SemaphoreType.DMA((4,)),
     ]
     return call(
@@ -223,16 +231,15 @@
     rows = row_blocks // peers
 
     def kernel(slots_ref, tiles_ref, vector_ref, *refs):
-        outs, (dense_ref, product_ref) = take(refs, peers)
+        outs, (dense_ref,) = take(refs, peers)
         dense_ref[...] = tile_sums(
-            slots_ref[...], tiles_ref, vector_ref[...], product_ref, row_blocks, True
+            slots_ref[...], tiles_ref, vector_ref[...], row_blocks, True
         )
         for x, out in enumerate(outs):
             peer = jnp.bitwise_xor(lax.axis_index("col"), x)
             out[...] = dense_ref[pl.ds(peer * rows, rows), :]
 
     scratch = [pltpu.VMEM((row_blocks, width), jnp.float32)]
-    scratch += [pltpu.VMEM((count, width), jnp.float32)]
     return call(
         kernel,
         [(rows, width)] * peers,
@@ -253,12 +260,12 @@
     def kernel(slots_ref, tiles_ref, *refs):
         sources, rest = take(refs, peers)
         (chunks_ref,), apart_refs, scratch = take(rest, 1, 1 if apart else 0)
-        vector_ref, product_ref = scratch
+        (vector_ref,) = scratch
         for at, source in enumerate(sources):
             peer = jnp.bitwise_xor(lax.axis_index("col"), ([0] + hops)[at])
             vector_ref[pl.ds(peer * rows, rows), :] = source[:rows, :]
         dense = tile_sums(
-            slots_ref[...], tiles_ref, vector_ref[...], product_ref, col_blocks, False
+            slots_ref[...], tiles_ref, vector_ref[...], col_blocks, False
         )
         for i in range(peers_row):
             chunks_ref[i, :chunk, :] = dense[i * chunk : (i + 1) * chunk, :]
@@ -273,7 +280,6 @@
                     chunks_ref[i, chunk:, :] = added[i * joined : (i + 1) * joined]
 
     scratch = [pltpu.VMEM((rows * peers, width), jnp.float32)]
-    scratch += [pltpu.VMEM((count, width), jnp.float32)]
     outs = [(peers_row, chunk + joined, width)] + ([(share, width)] if apart else [])
     return call(
         kernel,

time: 102 us -> 101 us (level)
  no operation moved by 1% of the time
where the time goes in v7:
time: 101 us
  blocking collectives  63 us (62%)
  starting transfers between devices  16.4 us (16%)
  waiting for transfers between devices  10.2 us (10%)
  Pallas kernels  8.78 us (9%)
  local copies, waits for them, and re-layouts  1.78 us (2%)
    all_to_all x7, blocking collectives, swap(): return lax.all_to_all(chunks, axis, 0, 0, tiled=True)  63 us
    ppermute x12, starting transfers between devices, exchange(): lax.ppermute(messages[x], axis, [(i, i ^ x) for i in range(count)])  16.4 us
    ppermute x12, waiting for transfers between devices, exchange(): lax.ppermute(messages[x], axis, [(i, i ^ x) for i in range(count)])  10.2 us
    pallas_call x13, Pallas kernels, call(): pl.pallas_call(kernel, out_shape=shapes, in_specs=specs or [VMEM] * len(a...  8.78 us
  transfers between devices with their start and end apart: 12, of which 9 were waited for; matrix products, arithmetic and copies ran while one was open for 0% of the time, Pallas kernels for 1%

profile of v7, /device:TPU:0, one launch (start us, length us, event | category | flops | bytes accessed | tf_op | source)
XLA Modules:
  0.0 100.8 jit_solution(1556363840884406977)
XLA Ops:
  0.7 3.6 %shard_map.76 = (f32[40,128]{1,0:T(8,128)}, f32[40,128]{1,0:T(8,128)}, f32[40,128]{1,0:T(8,128)}, f32[40,128]{1,0:T(8,128)}) custom-call(s32[1,16]{1,0:T(1,128)} %slots_ref.5, bf16[16,128,128]{2,1,0:T(8,128)(2,1)} %bitcast.3, f32[128,128]{1,0:T(8,128)} %bitcast.7, f32[64,4096]{1,0:T(8,128)} %basis_ref.5), custom_call_target="tpu_custom_call" | custom-call | tf_op jit(solution)/shard_map/pallas_call | solution.py:28
  4.3 4.1 %collective-permute-start = (f32[40,128]{1,0:T(8,128)}, f32[40,128]{1,0:T(8,128)S(1)}, u32[]{:S(2)}, u32[]{:S(2)}) collective-permute-start(f32[40,128]{1,0:T(8,128)} %get-tuple-element.37), channel_id=1, source_target_pairs={{0,2},{1,3},{2,0},{3,1},{4,6},{5,7},{6,4},{7,5},{8,10},{9,11},{10,... | collective-permute-start | bytes 61448 | tf_op jit(solution)/shard_map/ppermute | solution.py:51
  8.4 1.3 %collective-permute-start.1 = (f32[40,128]{1,0:T(8,128)}, f32[40,128]{1,0:T(8,128)S(1)}, u32[]{:S(2)}, u32[]{:S(2)}) collective-permute-start(f32[40,128]{1,0:T(8,128)} %get-tuple-element.38), channel_id=1, source_target_pairs={{0,3},{1,2},{2,1},{3,0},{4,7},{5,6},{6,5},{7,4},{8,11},{9,10},{10,... | collective-permute-start | bytes 61448 | tf_op jit(solution)/shard_map/ppermute | solution.py:51
  10.0 1.0 %copy-done.2 = f32[64,1,2048]{2,1,0:T(1,128)S(1)} copy-done((f32[64,1,2048]{2,1,0:T(1,128)S(1)}, f32[64,1,2048]{2,1,0:T(1,128)}, u32[]{:S(2)}) %copy-start.2) | copy-done | bytes 524312
  11.0 0.7 copy-done.4
  11.8 0.7 shard_map.77
  12.4 1.8 %collective-permute-done.1.refs_2_ = f32[40,128]{1,0:T(8,128)S(1)} collective-permute-done((f32[40,128]{1,0:T(8,128)}, f32[40,128]{1,0:T(8,128)S(1)}, u32[]{:S(2)}, u32[]{:S(2)}) %collective-permute-start.1) | collective-permute-done | bytes 20512 | tf_op jit(solution)/shard_map/ppermute | solution.py:51
  14.4 12.7 %all_to_all.35.received_ref = f32[32,1,1152]{2,1,0:T(1,128)S(1)} all-to-all(f32[32,1,1152]{2,1,0:T(1,128)S(1)} %get-tuple-element.41), channel_id=1, replica_groups=mesh['row'=8,'col'=4] {'row','col'}, dimensions={0} | all-to-all | bytes 294912 | tf_op jit(solution)/shard_map/all_to_all | solution.py:23
  27.8 1.4 %collective-permute-start.4 = (f32[40,128]{1,0:T(8,128)S(1)}, f32[40,128]{1,0:T(8,128)S(1)}, u32[]{:S(2)}, u32[]{:S(2)}) collective-permute-start(f32[40,128]{1,0:T(8,128)S(1)} %get-tuple-element.45), channel_id=1, source_target_pairs={{0,3},{1,2},{2,1},{3,0},{4,7},{5,6},{6,5},{7,4},{8,11},{9,10},{10,... | collective-permute-start | bytes 61448 | tf_op jit(solution)/shard_map/ppermute | solution.py:51
  29.3 1.8 %collective-permute-start.5 = (f32[40,128]{1,0:T(8,128)S(1)}, f32[40,128]{1,0:T(8,128)S(1)}, u32[]{:S(2)}, u32[]{:S(2)}) collective-permute-start(f32[40,128]{1,0:T(8,128)S(1)} %get-tuple-element.46), channel_id=1, source_target_pairs={{0,1},{1,0},{2,3},{3,2},{4,5},{5,4},{6,7},{7,6},{8,9},{9,8},{10,11... | collective-permute-start | bytes 61448 | tf_op jit(solution)/shard_map/ppermute | solution.py:51
  31.0 1.4 %collective-permute-done.3.refs_1_ = f32[40,128]{1,0:T(8,128)S(1)} collective-permute-done((f32[40,128]{1,0:T(8,128)S(1)}, f32[40,128]{1,0:T(8,128)S(1)}, u32[]{:S(2)}, u32[]{:S(2)}) %collective-permute-start.3) | collective-permute-done | bytes 20512 | tf_op jit(solution)/shard_map/ppermute | solution.py:51
  32.5 1.0 collective-permute-done.4.refs_2_
  33.4 0.6 shard_map.80
  34.1 7.6 %all_to_all.36.refs_0_ = f32[8,17,128]{2,1,0:T(8,128)S(1)} all-to-all(f32[8,17,128]{2,1,0:T(8,128)S(1)} %shard_map.80), channel_id=1, replica_groups=mesh['row'=8,'col'=4] {'row'}, dimensions={0} | all-to-all | bytes 139264 | tf_op jit(solution)/shard_map/all_to_all | solution.py:23
  41.8 9.6 %all_to_all.37.received_ref = f32[32,1,384]{2,1,0:T(1,128)S(1)} all-to-all(f32[32,1,384]{2,1,0:T(1,128)S(1)} %get-tuple-element.50), channel_id=1, replica_groups=mesh['row'=8,'col'=4] {'row','col'}, dimensions={0} | all-to-all | bytes 98304 | tf_op jit(solution)/shard_map/all_to_all | solution.py:23
  51.7 7.4 %all_to_all.38 = f32[8,16,128]{2,1,0:T(8,128)S(1)} all-to-all(f32[8,16,128]{2,1,0:T(8,128)S(1)} %get-tuple-element.52), channel_id=1, replica_groups=mesh['row'=8,'col'=4] {'row'}, dimensions={0} | all-to-all | bytes 131072 | tf_op jit(solution)/shard_map/all_to_all | solution.py:23
  59.1 0.7 shard_map.83
  59.9 0.5 collective-permute-start.6
  60.4 2.2 %collective-permute-start.7 = (f32[32,128]{1,0:T(8,128)S(1)}, f32[32,128]{1,0:T(8,128)S(1)}, u32[]{:S(2)}, u32[]{:S(2)}) collective-permute-start(f32[32,128]{1,0:T(8,128)S(1)} %get-tuple-element.55), channel_id=1, source_target_pairs={{0,3},{1,2},{2,1},{3,0},{4,7},{5,6},{6,5},{7,4},{8,11},{9,10},{10,... | collective-permute-start | bytes 49160 | tf_op jit(solution)/shard_map/ppermute | solution.py:51
  62.6 0.8 collective-permute-start.8
  63.4 1.3 %collective-permute-done.6.refs_1_ = f32[32,128]{1,0:T(8,128)S(1)} collective-permute-done((f32[32,128]{1,0:T(8,128)S(1)}, f32[32,128]{1,0:T(8,128)S(1)}, u32[]{:S(2)}, u32[]{:S(2)}) %collective-permute-start.6) | collective-permute-done | bytes 16416 | tf_op jit(solution)/shard_map/ppermute | solution.py:51
  64.8 1.2 %collective-permute-done.7.refs_2_ = f32[32,128]{1,0:T(8,128)S(1)} collective-permute-done((f32[32,128]{1,0:T(8,128)S(1)}, f32[32,128]{1,0:T(8,128)S(1)}, u32[]{:S(2)}, u32[]{:S(2)}) %collective-permute-start.7) | collective-permute-done | bytes 16416 | tf_op jit(solution)/shard_map/ppermute | solution.py:51
  66.5 9.2 %all_to_all.39.received_ref = f32[32,1,128]{2,1,0:T(1,128)S(1)} all-to-all(f32[32,1,128]{2,1,0:T(1,128)S(1)} %get-tuple-element.58), channel_id=1, replica_groups=mesh['row'=8,'col'=4] {'row','col'}, dimensions={0} | all-to-all | bytes 32768 | tf_op jit(solution)/shard_map/all_to_all | solution.py:23
  76.0 0.6 collective-permute-start.11
  76.6 2.3 %collective-permute-start.10 = (f32[32,128]{1,0:T(8,128)S(1)}, f32[32,128]{1,0:T(8,128)S(1)}, u32[]{:S(2)}, u32[]{:S(2)}) collective-permute-start(f32[32,128]{1,0:T(8,128)S(1)} %get-tuple-element.61.refs_0_.refs_3_), channel_id=1, source_target_pairs={{0,3},{1,2},{2,1},{3,0},{4,7},{5,6},{6,5},{7,4},{8,11},{9,10},{10,... | collective-permute-start | bytes 49160 | tf_op jit(solution)/shard_map/ppermute | solution.py:51
  78.9 0.6 collective-permute-start.9
  79.5 1.4 %collective-permute-done.11.refs_3_ = f32[32,128]{1,0:T(8,128)S(1)} collective-permute-done((f32[32,128]{1,0:T(8,128)S(1)}, f32[32,128]{1,0:T(8,128)S(1)}, u32[]{:S(2)}, u32[]{:S(2)}) %collective-permute-start.11) | collective-permute-done | bytes 16416 | tf_op jit(solution)/shard_map/ppermute | solution.py:51
  81.0 1.2 %collective-permute-done.10.refs_2_ = f32[32,128]{1,0:T(8,128)S(1)} collective-permute-done((f32[32,128]{1,0:T(8,128)S(1)}, f32[32,128]{1,0:T(8,128)S(1)}, u32[]{:S(2)}, u32[]{:S(2)}) %collective-permute-start.10) | collective-permute-done | bytes 16416 | tf_op jit(solution)/shard_map/ppermute | solution.py:51
  82.6 0.6 shard_map.86
  83.2 7.4 %all_to_all.40.refs_0_ = f32[8,16,128]{2,1,0:T(8,128)S(1)} all-to-all(f32[8,16,128]{2,1,0:T(8,128)S(1)} %shard_map.86), channel_id=1, replica_groups=mesh['row'=8,'col'=4] {'row'}, dimensions={0} | all-to-all | bytes 131072 | tf_op jit(solution)/shard_map/all_to_all | solution.py:23
  90.8 9.2 %all_to_all.41.received_ref = f32[32,1,128]{2,1,0:T(1,128)S(1)} all-to-all(f32[32,1,128]{2,1,0:T(1,128)S(1)} %get-tuple-element.63), channel_id=1, replica_groups=mesh['row'=8,'col'=4] {'row','col'}, dimensions={0} | all-to-all | bytes 32768 | tf_op jit(solution)/shard_map/all_to_all | solution.py:23
  100.0 0.9 shard_map.88
  (24 shorter events, 3.2 us)
Async XLA Ops:
  0.6 9.4 %copy-start.3 = (f32[16384]{0:T(1024)S(1)}, f32[16384]{0:T(1024)}, u32[]{:S(2)}) copy-start(f32[16384]{0:T(1024)} %param.9) | copy-start | bytes 196612
  0.6 13.6 %copy-start = (f32[64,4096]{1,0:T(8,128)S(1)}, f32[64,4096]{1,0:T(8,128)}, u32[]{:S(2)}) copy-start(f32[64,4096]{1,0:T(8,128)} %basis_ref.5) | copy-start | bytes 3145732
  4.3 8.2 %collective-permute-start = (f32[40,128]{1,0:T(8,128)}, f32[40,128]{1,0:T(8,128)S(1)}, u32[]{:S(2)}, u32[]{:S(2)}) collective-permute-start(f32[40,128]{1,0:T(8,128)} %get-tuple-element.37), channel_id=1, source_target_pairs={{0,2},{1,3},{2,0},{3,1},{4,6},{5,7},{6,4},{7,5},{8,10},{9,11},{10,... | collective-permute-start | bytes 61448 | tf_op jit(solution)/shard_map/ppermute | solution.py:51
  8.4 5.8 %collective-permute-start.1 = (f32[40,128]{1,0:T(8,128)}, f32[40,128]{1,0:T(8,128)S(1)}, u32[]{:S(2)}, u32[]{:S(2)}) collective-permute-start(f32[40,128]{1,0:T(8,128)} %get-tuple-element.38), channel_id=1, source_target_pairs={{0,3},{1,2},{2,1},{3,0},{4,7},{5,6},{6,5},{7,4},{8,11},{9,10},{10,... | collective-permute-start | bytes 61448 | tf_op jit(solution)/shard_map/ppermute | solution.py:51
  9.7 4.4 %collective-permute-start.2 = (f32[40,128]{1,0:T(8,128)}, f32[40,128]{1,0:T(8,128)S(1)}, u32[]{:S(2)}, u32[]{:S(2)}) collective-permute-start(f32[40,128]{1,0:T(8,128)} %get-tuple-element.39), channel_id=1, source_target_pairs={{0,1},{1,0},{2,3},{3,2},{4,5},{5,4},{6,7},{7,6},{8,9},{9,8},{10,11... | collective-permute-start | bytes 61448 | tf_op jit(solution)/shard_map/ppermute | solution.py:51
  10.0 1.0 %copy-start.2 = (f32[64,1,2048]{2,1,0:T(1,128)S(1)}, f32[64,1,2048]{2,1,0:T(1,128)}, u32[]{:S(2)}) copy-start(f32[64,1,2048]{2,1,0:T(1,128)} %basis_ref.3) | copy-start | bytes 1572868
  11.0 0.7 copy-start.4
  27.1 6.4 %copy-start.1 = (bf16[1,16,128,128]{3,2,1,0:T(8,128)(2,1)S(1)}, bf16[1,16,128,128]{3,2,1,0:T(8,128)(2,1)}, u32[]{:S(2)}) copy-start(bf16[1,16,128,128]{3,2,1,0:T(8,128)(2,1)} %param.5) | copy-start | bytes 1572868
  27.5 5.0 %collective-permute-start.3 = (f32[40,128]{1,0:T(8,128)S(1)}, f32[40,128]{1,0:T(8,128)S(1)}, u32[]{:S(2)}, u32[]{:S(2)}) collective-permute-start(f32[40,128]{1,0:T(8,128)S(1)} %get-tuple-element.44), channel_id=1, source_target_pairs={{0,2},{1,3},{2,0},{3,1},{4,6},{5,7},{6,4},{7,5},{8,10},{9,11},{10,... | collective-permute-start | bytes 61448 | tf_op jit(solution)/shard_map/ppermute | solution.py:51
  27.8 5.6 %collective-permute-start.4 = (f32[40,128]{1,0:T(8,128)S(1)}, f32[40,128]{1,0:T(8,128)S(1)}, u32[]{:S(2)}, u32[]{:S(2)}) collective-permute-start(f32[40,128]{1,0:T(8,128)S(1)} %get-tuple-element.45), channel_id=1, source_target_pairs={{0,3},{1,2},{2,1},{3,0},{4,7},{5,6},{6,5},{7,4},{8,11},{9,10},{10,... | collective-permute-start | bytes 61448 | tf_op jit(solution)/shard_map/ppermute | solution.py:51
  29.2 4.2 %copy-start.5 = (s32[1,16]{1,0:T(1,128)S(1)}, s32[1,16]{1,0:T(1,128)}, u32[]{:S(2)}) copy-start(s32[1,16]{1,0:T(1,128)} %slots_ref.5) | copy-start | bytes 196
  29.3 4.2 %collective-permute-start.5 = (f32[40,128]{1,0:T(8,128)S(1)}, f32[40,128]{1,0:T(8,128)S(1)}, u32[]{:S(2)}, u32[]{:S(2)}) collective-permute-start(f32[40,128]{1,0:T(8,128)S(1)} %get-tuple-element.46), channel_id=1, source_target_pairs={{0,1},{1,0},{2,3},{3,2},{4,5},{5,4},{6,7},{7,6},{8,9},{9,8},{10,11... | collective-permute-start | bytes 61448 | tf_op jit(solution)/shard_map/ppermute | solution.py:51
  59.9 4.9 %collective-permute-start.6 = (f32[32,128]{1,0:T(8,128)S(1)}, f32[32,128]{1,0:T(8,128)S(1)}, u32[]{:S(2)}, u32[]{:S(2)}) collective-permute-start(f32[32,128]{1,0:T(8,128)S(1)} %get-tuple-element.54), channel_id=1, source_target_pairs={{0,2},{1,3},{2,0},{3,1},{4,6},{5,7},{6,4},{7,5},{8,10},{9,11},{10,... | collective-permute-start | bytes 49160 | tf_op jit(solution)/shard_map/ppermute | solution.py:51
  60.4 5.5 %collective-permute-start.7 = (f32[32,128]{1,0:T(8,128)S(1)}, f32[32,128]{1,0:T(8,128)S(1)}, u32[]{:S(2)}, u32[]{:S(2)}) collective-permute-start(f32[32,128]{1,0:T(8,128)S(1)} %get-tuple-element.55), channel_id=1, source_target_pairs={{0,3},{1,2},{2,1},{3,0},{4,7},{5,6},{6,5},{7,4},{8,11},{9,10},{10,... | collective-permute-start | bytes 49160 | tf_op jit(solution)/shard_map/ppermute | solution.py:51
  62.6 3.7 %collective-permute-start.8 = (f32[32,128]{1,0:T(8,128)S(1)}, f32[32,128]{1,0:T(8,128)S(1)}, u32[]{:S(2)}, u32[]{:S(2)}) collective-permute-start(f32[32,128]{1,0:T(8,128)S(1)} %get-tuple-element.56), channel_id=1, source_target_pairs={{0,1},{1,0},{2,3},{3,2},{4,5},{5,4},{6,7},{7,6},{8,9},{9,8},{10,11... | collective-permute-start | bytes 49160 | tf_op jit(solution)/shard_map/ppermute | solution.py:51
  76.0 5.0 %collective-permute-start.11 = (f32[32,128]{1,0:T(8,128)S(1)}, f32[32,128]{1,0:T(8,128)S(1)}, u32[]{:S(2)}, u32[]{:S(2)}) collective-permute-start(f32[32,128]{1,0:T(8,128)S(1)} %get-tuple-element.61.refs_0_.refs_3_), channel_id=1, source_target_pairs={{0,2},{1,3},{2,0},{3,1},{4,6},{5,7},{6,4},{7,5},{8,10},{9,11},{10,... | collective-permute-start | bytes 49160 | tf_op jit(solution)/shard_map/ppermute | solution.py:51
  76.6 5.5 %collective-permute-start.10 = (f32[32,128]{1,0:T(8,128)S(1)}, f32[32,128]{1,0:T(8,128)S(1)}, u32[]{:S(2)}, u32[]{:S(2)}) collective-permute-start(f32[32,128]{1,0:T(8,128)S(1)} %get-tuple-element.61.refs_0_.refs_3_), channel_id=1, source_target_pairs={{0,3},{1,2},{2,1},{3,0},{4,7},{5,6},{6,5},{7,4},{8,11},{9,10},{10,... | collective-permute-start | bytes 49160 | tf_op jit(solution)/shard_map/ppermute | solution.py:51
  78.9 3.7 %collective-permute-start.9 = (f32[32,128]{1,0:T(8,128)S(1)}, f32[32,128]{1,0:T(8,128)S(1)}, u32[]{:S(2)}, u32[]{:S(2)}) collective-permute-start(f32[32,128]{1,0:T(8,128)S(1)} %get-tuple-element.61.refs_0_.refs_3_), channel_id=1, source_target_pairs={{0,1},{1,0},{2,3},{3,2},{4,5},{5,4},{6,7},{7,6},{8,9},{9,8},{10,11... | collective-permute-start | bytes 49160 | tf_op jit(solution)/shard_map/ppermute | solution.py:51

commit v8 on v7

--- a/solution.py
+++ b/solution.py
@@ -354,9 +354,14 @@
         return
     for k in range(share):
         at = slice((first + k) * LANES, (first + k + 1) * LANES)
-        added = received_ref[0:peers, 0, at]
-        for i in range(1, devices // peers):
-            added = added + received_ref[i * peers : (i + 1) * peers, 0, at]
+        group = max(peers, GROUP)
+        lines_at = received_ref[:, 0, at]
+        summed = lines_at[0:group]
+        for i in range(1, devices // group):
+            summed = summed + lines_at[i * group : (i + 1) * group]
+        added = summed[0:peers]
+        for i in range(1, group // peers):
+            added = added + summed[i * peers : (i + 1) * peers]
         for peer in range(peers):
             packed_ref[peer * share + k : peer * share + k + 1, :] = added[peer : peer + 1]
 

time: 101 us -> 101 us (level)
  no operation moved by 1% of the time
where the time goes in v8:
time: 101 us
  blocking collectives  63 us (62%)
  starting transfers between devices  16.4 us (16%)
  waiting for transfers between devices  10.2 us (10%)
  Pallas kernels  8.77 us (9%)
  local copies, waits for them, and re-layouts  1.78 us (2%)
    all_to_all x7, blocking collectives, swap(): return lax.all_to_all(chunks, axis, 0, 0, tiled=True)  63 us
    ppermute x12, starting transfers between devices, exchange(): lax.ppermute(messages[x], axis, [(i, i ^ x) for i in range(count)])  16.4 us
    ppermute x12, waiting for transfers between devices, exchange(): lax.ppermute(messages[x], axis, [(i, i ^ x) for i in range(count)])  10.2 us
    pallas_call x13, Pallas kernels, call(): pl.pallas_call(kernel, out_shape=shapes, in_specs=specs or [VMEM] * len(a...  8.77 us
  transfers between devices with their start and end apart: 12, of which 9 were waited for; matrix products, arithmetic and copies ran while one was open for 0% of the time, Pallas kernels for 1%

profile of v8, /device:TPU:0, one launch (start us, length us, event | category | flops | bytes accessed | tf_op | source)
XLA Modules:
  0.0 100.8 jit_solution(3968065608388215647)
XLA Ops:
  0.7 3.6 %shard_map.76 = (f32[40,128]{1,0:T(8,128)}, f32[40,128]{1,0:T(8,128)}, f32[40,128]{1,0:T(8,128)}, f32[40,128]{1,0:T(8,128)}) custom-call(s32[1,16]{1,0:T(1,128)} %slots_ref.5, bf16[16,128,128]{2,1,0:T(8,128)(2,1)} %bitcast.3, f32[128,128]{1,0:T(8,128)} %bitcast.7, f32[64,4096]{1,0:T(8,128)} %basis_ref.5), custom_call_target="tpu_custom_call" | custom-call | tf_op jit(solution)/shard_map/pallas_call | solution.py:28
  4.3 4.1 %collective-permute-start = (f32[40,128]{1,0:T(8,128)}, f32[40,128]{1,0:T(8,128)S(1)}, u32[]{:S(2)}, u32[]{:S(2)}) collective-permute-start(f32[40,128]{1,0:T(8,128)} %get-tuple-element.37), channel_id=1, source_target_pairs={{0,2},{1,3},{2,0},{3,1},{4,6},{5,7},{6,4},{7,5},{8,10},{9,11},{10,... | collective-permute-start | bytes 61448 | tf_op jit(solution)/shard_map/ppermute | solution.py:51
  8.4 1.3 %collective-permute-start.1 = (f32[40,128]{1,0:T(8,128)}, f32[40,128]{1,0:T(8,128)S(1)}, u32[]{:S(2)}, u32[]{:S(2)}) collective-permute-start(f32[40,128]{1,0:T(8,128)} %get-tuple-element.38), channel_id=1, source_target_pairs={{0,3},{1,2},{2,1},{3,0},{4,7},{5,6},{6,5},{7,4},{8,11},{9,10},{10,... | collective-permute-start | bytes 61448 | tf_op jit(solution)/shard_map/ppermute | solution.py:51
  10.0 1.0 %copy-done.2 = f32[64,1,2048]{2,1,0:T(1,128)S(1)} copy-done((f32[64,1,2048]{2,1,0:T(1,128)S(1)}, f32[64,1,2048]{2,1,0:T(1,128)}, u32[]{:S(2)}) %copy-start.2) | copy-done | bytes 524312
  11.0 0.7 copy-done.4
  11.8 0.7 shard_map.77
  12.4 1.8 %collective-permute-done.1.refs_2_ = f32[40,128]{1,0:T(8,128)S(1)} collective-permute-done((f32[40,128]{1,0:T(8,128)}, f32[40,128]{1,0:T(8,128)S(1)}, u32[]{:S(2)}, u32[]{:S(2)}) %collective-permute-start.1) | collective-permute-done | bytes 20512 | tf_op jit(solution)/shard_map/ppermute | solution.py:51
  14.4 12.7 %all_to_all.35.received_ref = f32[32,1,1152]{2,1,0:T(1,128)S(1)} all-to-all(f32[32,1,1152]{2,1,0:T(1,128)S(1)} %get-tuple-element.41), channel_id=1, replica_groups=mesh['row'=8,'col'=4] {'row','col'}, dimensions={0} | all-to-all | bytes 294912 | tf_op jit(solution)/shard_map/all_to_all | solution.py:23
  27.8 1.4 %collective-permute-start.4 = (f32[40,128]{1,0:T(8,128)S(1)}, f32[40,128]{1,0:T(8,128)S(1)}, u32[]{:S(2)}, u32[]{:S(2)}) collective-permute-start(f32[40,128]{1,0:T(8,128)S(1)} %get-tuple-element.45), channel_id=1, source_target_pairs={{0,3},{1,2},{2,1},{3,0},{4,7},{5,6},{6,5},{7,4},{8,11},{9,10},{10,... | collective-permute-start | bytes 61448 | tf_op jit(solution)/shard_map/ppermute | solution.py:51
  29.3 1.8 %collective-permute-start.5 = (f32[40,128]{1,0:T(8,128)S(1)}, f32[40,128]{1,0:T(8,128)S(1)}, u32[]{:S(2)}, u32[]{:S(2)}) collective-permute-start(f32[40,128]{1,0:T(8,128)S(1)} %get-tuple-element.46), channel_id=1, source_target_pairs={{0,1},{1,0},{2,3},{3,2},{4,5},{5,4},{6,7},{7,6},{8,9},{9,8},{10,11... | collective-permute-start | bytes 61448 | tf_op jit(solution)/shard_map/ppermute | solution.py:51
  31.0 1.4 %collective-permute-done.3.refs_1_ = f32[40,128]{1,0:T(8,128)S(1)} collective-permute-done((f32[40,128]{1,0:T(8,128)S(1)}, f32[40,128]{1,0:T(8,128)S(1)}, u32[]{:S(2)}, u32[]{:S(2)}) %collective-permute-start.3) | collective-permute-done | bytes 20512 | tf_op jit(solution)/shard_map/ppermute | solution.py:51
  32.5 1.0 collective-permute-done.4.refs_2_
  33.4 0.6 shard_map.80
  34.1 7.6 %all_to_all.36.refs_0_ = f32[8,17,128]{2,1,0:T(8,128)S(1)} all-to-all(f32[8,17,128]{2,1,0:T(8,128)S(1)} %shard_map.80), channel_id=1, replica_groups=mesh['row'=8,'col'=4] {'row'}, dimensions={0} | all-to-all | bytes 139264 | tf_op jit(solution)/shard_map/all_to_all | solution.py:23
  41.8 9.6 %all_to_all.37.received_ref = f32[32,1,384]{2,1,0:T(1,128)S(1)} all-to-all(f32[32,1,384]{2,1,0:T(1,128)S(1)} %get-tuple-element.50), channel_id=1, replica_groups=mesh['row'=8,'col'=4] {'row','col'}, dimensions={0} | all-to-all | bytes 98304 | tf_op jit(solution)/shard_map/all_to_all | solution.py:23
  51.7 7.4 %all_to_all.38 = f32[8,16,128]{2,1,0:T(8,128)S(1)} all-to-all(f32[8,16,128]{2,1,0:T(8,128)S(1)} %get-tuple-element.52), channel_id=1, replica_groups=mesh['row'=8,'col'=4] {'row'}, dimensions={0} | all-to-all | bytes 131072 | tf_op jit(solution)/shard_map/all_to_all | solution.py:23
  59.1 0.7 shard_map.83
  59.9 0.5 collective-permute-start.6
  60.4 2.2 %collective-permute-start.7 = (f32[32,128]{1,0:T(8,128)S(1)}, f32[32,128]{1,0:T(8,128)S(1)}, u32[]{:S(2)}, u32[]{:S(2)}) collective-permute-start(f32[32,128]{1,0:T(8,128)S(1)} %get-tuple-element.55), channel_id=1, source_target_pairs={{0,3},{1,2},{2,1},{3,0},{4,7},{5,6},{6,5},{7,4},{8,11},{9,10},{10,... | collective-permute-start | bytes 49160 | tf_op jit(solution)/shard_map/ppermute | solution.py:51
  62.6 0.8 collective-permute-start.8
  63.4 1.3 %collective-permute-done.6.refs_1_ = f32[32,128]{1,0:T(8,128)S(1)} collective-permute-done((f32[32,128]{1,0:T(8,128)S(1)}, f32[32,128]{1,0:T(8,128)S(1)}, u32[]{:S(2)}, u32[]{:S(2)}) %collective-permute-start.6) | collective-permute-done | bytes 16416 | tf_op jit(solution)/shard_map/ppermute | solution.py:51
  64.8 1.2 %collective-permute-done.7.refs_2_ = f32[32,128]{1,0:T(8,128)S(1)} collective-permute-done((f32[32,128]{1,0:T(8,128)S(1)}, f32[32,128]{1,0:T(8,128)S(1)}, u32[]{:S(2)}, u32[]{:S(2)}) %collective-permute-start.7) | collective-permute-done | bytes 16416 | tf_op jit(solution)/shard_map/ppermute | solution.py:51
  66.5 9.2 %all_to_all.39.received_ref = f32[32,1,128]{2,1,0:T(1,128)S(1)} all-to-all(f32[32,1,128]{2,1,0:T(1,128)S(1)} %get-tuple-element.58), channel_id=1, replica_groups=mesh['row'=8,'col'=4] {'row','col'}, dimensions={0} | all-to-all | bytes 32768 | tf_op jit(solution)/shard_map/all_to_all | solution.py:23
  76.0 0.6 collective-permute-start.11
  76.6 2.3 %collective-permute-start.10 = (f32[32,128]{1,0:T(8,128)S(1)}, f32[32,128]{1,0:T(8,128)S(1)}, u32[]{:S(2)}, u32[]{:S(2)}) collective-permute-start(f32[32,128]{1,0:T(8,128)S(1)} %get-tuple-element.61.refs_0_.refs_3_), channel_id=1, source_target_pairs={{0,3},{1,2},{2,1},{3,0},{4,7},{5,6},{6,5},{7,4},{8,11},{9,10},{10,... | collective-permute-start | bytes 49160 | tf_op jit(solution)/shard_map/ppermute | solution.py:51
  78.9 0.6 collective-permute-start.9
  79.5 1.4 %collective-permute-done.11.refs_3_ = f32[32,128]{1,0:T(8,128)S(1)} collective-permute-done((f32[32,128]{1,0:T(8,128)S(1)}, f32[32,128]{1,0:T(8,128)S(1)}, u32[]{:S(2)}, u32[]{:S(2)}) %collective-permute-start.11) | collective-permute-done | bytes 16416 | tf_op jit(solution)/shard_map/ppermute | solution.py:51
  81.0 1.2 %collective-permute-done.10.refs_2_ = f32[32,128]{1,0:T(8,128)S(1)} collective-permute-done((f32[32,128]{1,0:T(8,128)S(1)}, f32[32,128]{1,0:T(8,128)S(1)}, u32[]{:S(2)}, u32[]{:S(2)}) %collective-permute-start.10) | collective-permute-done | bytes 16416 | tf_op jit(solution)/shard_map/ppermute | solution.py:51
  82.6 0.6 shard_map.86
  83.2 7.4 %all_to_all.40.refs_0_ = f32[8,16,128]{2,1,0:T(8,128)S(1)} all-to-all(f32[8,16,128]{2,1,0:T(8,128)S(1)} %shard_map.86), channel_id=1, replica_groups=mesh['row'=8,'col'=4] {'row'}, dimensions={0} | all-to-all | bytes 131072 | tf_op jit(solution)/shard_map/all_to_all | solution.py:23
  90.8 9.2 %all_to_all.41.received_ref = f32[32,1,128]{2,1,0:T(1,128)S(1)} all-to-all(f32[32,1,128]{2,1,0:T(1,128)S(1)} %get-tuple-element.63), channel_id=1, replica_groups=mesh['row'=8,'col'=4] {'row','col'}, dimensions={0} | all-to-all | bytes 32768 | tf_op jit(solution)/shard_map/all_to_all | solution.py:23
  100.0 0.9 shard_map.88
  (24 shorter events, 3.2 us)
Async XLA Ops:
  0.6 9.4 %copy-start.3 = (f32[16384]{0:T(1024)S(1)}, f32[16384]{0:T(1024)}, u32[]{:S(2)}) copy-start(f32[16384]{0:T(1024)} %param.9) | copy-start | bytes 196612
  0.6 13.6 %copy-start = (f32[64,4096]{1,0:T(8,128)S(1)}, f32[64,4096]{1,0:T(8,128)}, u32[]{:S(2)}) copy-start(f32[64,4096]{1,0:T(8,128)} %basis_ref.5) | copy-start | bytes 3145732
  4.3 8.2 %collective-permute-start = (f32[40,128]{1,0:T(8,128)}, f32[40,128]{1,0:T(8,128)S(1)}, u32[]{:S(2)}, u32[]{:S(2)}) collective-permute-start(f32[40,128]{1,0:T(8,128)} %get-tuple-element.37), channel_id=1, source_target_pairs={{0,2},{1,3},{2,0},{3,1},{4,6},{5,7},{6,4},{7,5},{8,10},{9,11},{10,... | collective-permute-start | bytes 61448 | tf_op jit(solution)/shard_map/ppermute | solution.py:51
  8.4 5.8 %collective-permute-start.1 = (f32[40,128]{1,0:T(8,128)}, f32[40,128]{1,0:T(8,128)S(1)}, u32[]{:S(2)}, u32[]{:S(2)}) collective-permute-start(f32[40,128]{1,0:T(8,128)} %get-tuple-element.38), channel_id=1, source_target_pairs={{0,3},{1,2},{2,1},{3,0},{4,7},{5,6},{6,5},{7,4},{8,11},{9,10},{10,... | collective-permute-start | bytes 61448 | tf_op jit(solution)/shard_map/ppermute | solution.py:51
  9.7 4.4 %collective-permute-start.2 = (f32[40,128]{1,0:T(8,128)}, f32[40,128]{1,0:T(8,128)S(1)}, u32[]{:S(2)}, u32[]{:S(2)}) collective-permute-start(f32[40,128]{1,0:T(8,128)} %get-tuple-element.39), channel_id=1, source_target_pairs={{0,1},{1,0},{2,3},{3,2},{4,5},{5,4},{6,7},{7,6},{8,9},{9,8},{10,11... | collective-permute-start | bytes 61448 | tf_op jit(solution)/shard_map/ppermute | solution.py:51
  10.0 1.0 %copy-start.2 = (f32[64,1,2048]{2,1,0:T(1,128)S(1)}, f32[64,1,2048]{2,1,0:T(1,128)}, u32[]{:S(2)}) copy-start(f32[64,1,2048]{2,1,0:T(1,128)} %basis_ref.3) | copy-start | bytes 1572868
  11.0 0.7 copy-start.4
  27.1 6.4 %copy-start.1 = (bf16[1,16,128,128]{3,2,1,0:T(8,128)(2,1)S(1)}, bf16[1,16,128,128]{3,2,1,0:T(8,128)(2,1)}, u32[]{:S(2)}) copy-start(bf16[1,16,128,128]{3,2,1,0:T(8,128)(2,1)} %param.5) | copy-start | bytes 1572868
  27.5 5.0 %collective-permute-start.3 = (f32[40,128]{1,0:T(8,128)S(1)}, f32[40,128]{1,0:T(8,128)S(1)}, u32[]{:S(2)}, u32[]{:S(2)}) collective-permute-start(f32[40,128]{1,0:T(8,128)S(1)} %get-tuple-element.44), channel_id=1, source_target_pairs={{0,2},{1,3},{2,0},{3,1},{4,6},{5,7},{6,4},{7,5},{8,10},{9,11},{10,... | collective-permute-start | bytes 61448 | tf_op jit(solution)/shard_map/ppermute | solution.py:51
  27.8 5.6 %collective-permute-start.4 = (f32[40,128]{1,0:T(8,128)S(1)}, f32[40,128]{1,0:T(8,128)S(1)}, u32[]{:S(2)}, u32[]{:S(2)}) collective-permute-start(f32[40,128]{1,0:T(8,128)S(1)} %get-tuple-element.45), channel_id=1, source_target_pairs={{0,3},{1,2},{2,1},{3,0},{4,7},{5,6},{6,5},{7,4},{8,11},{9,10},{10,... | collective-permute-start | bytes 61448 | tf_op jit(solution)/shard_map/ppermute | solution.py:51
  29.2 4.2 %copy-start.5 = (s32[1,16]{1,0:T(1,128)S(1)}, s32[1,16]{1,0:T(1,128)}, u32[]{:S(2)}) copy-start(s32[1,16]{1,0:T(1,128)} %slots_ref.5) | copy-start | bytes 196
  29.3 4.2 %collective-permute-start.5 = (f32[40,128]{1,0:T(8,128)S(1)}, f32[40,128]{1,0:T(8,128)S(1)}, u32[]{:S(2)}, u32[]{:S(2)}) collective-permute-start(f32[40,128]{1,0:T(8,128)S(1)} %get-tuple-element.46), channel_id=1, source_target_pairs={{0,1},{1,0},{2,3},{3,2},{4,5},{5,4},{6,7},{7,6},{8,9},{9,8},{10,11... | collective-permute-start | bytes 61448 | tf_op jit(solution)/shard_map/ppermute | solution.py:51
  59.9 4.9 %collective-permute-start.6 = (f32[32,128]{1,0:T(8,128)S(1)}, f32[32,128]{1,0:T(8,128)S(1)}, u32[]{:S(2)}, u32[]{:S(2)}) collective-permute-start(f32[32,128]{1,0:T(8,128)S(1)} %get-tuple-element.54), channel_id=1, source_target_pairs={{0,2},{1,3},{2,0},{3,1},{4,6},{5,7},{6,4},{7,5},{8,10},{9,11},{10,... | collective-permute-start | bytes 49160 | tf_op jit(solution)/shard_map/ppermute | solution.py:51
  60.4 5.5 %collective-permute-start.7 = (f32[32,128]{1,0:T(8,128)S(1)}, f32[32,128]{1,0:T(8,128)S(1)}, u32[]{:S(2)}, u32[]{:S(2)}) collective-permute-start(f32[32,128]{1,0:T(8,128)S(1)} %get-tuple-element.55), channel_id=1, source_target_pairs={{0,3},{1,2},{2,1},{3,0},{4,7},{5,6},{6,5},{7,4},{8,11},{9,10},{10,... | collective-permute-start | bytes 49160 | tf_op jit(solution)/shard_map/ppermute | solution.py:51
  62.6 3.7 %collective-permute-start.8 = (f32[32,128]{1,0:T(8,128)S(1)}, f32[32,128]{1,0:T(8,128)S(1)}, u32[]{:S(2)}, u32[]{:S(2)}) collective-permute-start(f32[32,128]{1,0:T(8,128)S(1)} %get-tuple-element.56), channel_id=1, source_target_pairs={{0,1},{1,0},{2,3},{3,2},{4,5},{5,4},{6,7},{7,6},{8,9},{9,8},{10,11... | collective-permute-start | bytes 49160 | tf_op jit(solution)/shard_map/ppermute | solution.py:51
  76.0 5.0 %collective-permute-start.11 = (f32[32,128]{1,0:T(8,128)S(1)}, f32[32,128]{1,0:T(8,128)S(1)}, u32[]{:S(2)}, u32[]{:S(2)}) collective-permute-start(f32[32,128]{1,0:T(8,128)S(1)} %get-tuple-element.61.refs_0_.refs_3_), channel_id=1, source_target_pairs={{0,2},{1,3},{2,0},{3,1},{4,6},{5,7},{6,4},{7,5},{8,10},{9,11},{10,... | collective-permute-start | bytes 49160 | tf_op jit(solution)/shard_map/ppermute | solution.py:51
  76.6 5.5 %collective-permute-start.10 = (f32[32,128]{1,0:T(8,128)S(1)}, f32[32,128]{1,0:T(8,128)S(1)}, u32[]{:S(2)}, u32[]{:S(2)}) collective-permute-start(f32[32,128]{1,0:T(8,128)S(1)} %get-tuple-element.61.refs_0_.refs_3_), channel_id=1, source_target_pairs={{0,3},{1,2},{2,1},{3,0},{4,7},{5,6},{6,5},{7,4},{8,11},{9,10},{10,... | collective-permute-start | bytes 49160 | tf_op jit(solution)/shard_map/ppermute | solution.py:51
  78.9 3.7 %collective-permute-start.9 = (f32[32,128]{1,0:T(8,128)S(1)}, f32[32,128]{1,0:T(8,128)S(1)}, u32[]{:S(2)}, u32[]{:S(2)}) collective-permute-start(f32[32,128]{1,0:T(8,128)S(1)} %get-tuple-element.61.refs_0_.refs_3_), channel_id=1, source_target_pairs={{0,1},{1,0},{2,3},{3,2},{4,5},{5,4},{6,7},{7,6},{8,9},{9,8},{10,11... | collective-permute-start | bytes 49160 | tf_op jit(solution)/shard_map/ppermute | solution.py:51
